TPU v7x, 128 devices: a whole 4x4x4 slice. The times are simulated.
128 devices in a mesh: tm: 16 (over z_lo, x, core), space: 8 (over y, z_hi).
Axes of the slice: x: 4, y: 4, z: 4 (z_hi: 2, z_lo: 2; z = z_hi * 2 + z_lo), core: 2. Of those that a mesh axis runs over, the one named last changes fastest.
Arguments:
- coarse_guess: float32 [16, 64, 12, 512], P('tm', 'space'), may hold values from -6 to 6
- initial_state: float32 [64, 12, 512], P('space'), may hold values from -6 to 6
- fine_volume: bfloat16 [512, 512], replicated
- coarse_volume: bfloat16 [512, 512], replicated
- lift_matrix: bfloat16 [384, 512], replicated, may hold values from -0.0390625 to 0.0390625
- wave_speed: float32 [12], replicated, may hold values from 0.1 to 0.6
- reaction_rate: float32 [24], replicated, may hold values from 0.05 to 0.5
- species_map: int32 [24, 3], replicated, may hold values from 0 to 11
- neighbour_element: int32 [64, 6], P('space'), may hold values from 0 to 7
- neighbour_rank: int32 [64, 6], P('space'), may hold values from -1 to 1
Outputs:
- iterate: float32 [64, 64, 12, 512], P('tm', 'space')
All inputs are finite; a program needn't handle non-finite values.
Results may differ from a plain program's by a relative error of at most 0.025.
Values may be sent and summed in bfloat16 or wider, within the bound.
No kernel may reach another device: no remote copies, remote signals or barrier semaphores. Data moves between devices by JAX's collectives and lax.ppermute only.
A program may use at most 64 MiB of HBM per device.

v0:
```python
import jax
import jax.numpy as jnp
import numpy as np
from jax import lax
from jax.sharding import PartitionSpec as P

SIDE = 8
NODES = 512
FACE_NODES = 384
VARS = 12
STRIDE = 4


coarse_gain = 4.0


def extended(block, sides, width):
    for axis, dim in sides:
        count = lax.axis_size(axis)
        forward = [(i, i + 1) for i in range(count - 1)]
        forward.append((count - 1, 0))
        backward = [(target, source) for source, target in forward]
        low = lax.ppermute(
            lax.slice_in_dim(block, block.shape[dim] - width, None, axis=dim), axis, forward
        )
        high = lax.ppermute(lax.slice_in_dim(block, 0, width, axis=dim), axis, backward)
        block = jnp.concatenate([low, block, high], axis=dim)
    return block


def passed_along(shard, axis, by):
    size = lax.axis_size(axis)
    pairs = [(i, i + by) for i in range(size) if 0 <= i + by < size]
    return lax.ppermute(shard, axis, pairs)


def face_tables(side):
    plane = side * side
    nodes = side**3
    inner = np.arange(plane)
    first = inner // side
    second = inner % side
    last = side - 1
    node_lists = [
        0 * plane + first * side + second,
        last * plane + first * side + second,
        first * plane + 0 * side + second,
        first * plane + last * side + second,
        first * plane + second * side + 0,
        first * plane + second * side + last,
    ]
    table = np.zeros((nodes, 12 * plane), np.float32)
    for which_face in range(6):
        table[node_lists[which_face], which_face * plane + inner] = 1.0
        table[node_lists[which_face ^ 1], (6 + which_face) * plane + inner] = 1.0
    masks = np.zeros((6, 1, 1, 6 * plane), np.float32)
    for which_face in range(6):
        masks[which_face, 0, 0, which_face * plane : (which_face + 1) * plane] = 1.0
    return (table, masks)


def selections(species_map):
    labels = jnp.arange(VARS, dtype=jnp.int32)[None, :]
    first_table = (species_map[:, 0:1] == labels).astype(jnp.float32)
    second_table = (species_map[:, 1:2] == labels).astype(jnp.float32)
    made_table = (species_map[:, 2:3] == labels).astype(jnp.float32)
    return (first_table, second_table, made_table - first_table)


def react(state, tables, scaled_rates):
    first_table, second_table, change_table = tables
    first_amount = jnp.einsum(
        "rv,...vn->...rn", first_table, state, precision=lax.Precision.HIGHEST
    )
    second_amount = jnp.einsum(
        "rv,...vn->...rn", second_table, state, precision=lax.Precision.HIGHEST
    )
    speed_term = (
        scaled_rates[:, None]
        * first_amount
        * second_amount
        / (1.0 + first_amount * first_amount + second_amount * second_amount)
    )
    return state + jnp.einsum(
        "rv,...rn->...vn", change_table, speed_term, precision=lax.Precision.HIGHEST
    )


def body(
    coarse_guess,
    initial_state,
    fine_volume,
    coarse_volume,
    lift_matrix,
    wave_speed,
    reaction_rate,
    species_map,
    neighbour_element,
    neighbour_rank,
):
    elements = initial_state.shape[0]
    columns = initial_state.shape[1]
    lookup = (neighbour_rank + 1) * elements + neighbour_element
    tables = selections(species_map)
    table_np, masks_np = face_tables(SIDE)
    face_table = jnp.asarray(table_np).astype(jnp.bfloat16)
    face_masks = jnp.asarray(masks_np)
    sources = jnp.arange(3 * elements, dtype=jnp.int32)[None, :]
    picker = (jnp.transpose(lookup).reshape(6 * elements, 1) == sources).astype(jnp.bfloat16)
    speeds = wave_speed[None, :, None]

    def substep(state, volume, gain):
        rounded = state.astype(jnp.bfloat16)
        flat_rounded = rounded.reshape(elements * columns, NODES)
        both_faces = jnp.dot(flat_rounded, face_table, preferred_element_type=jnp.float32)
        own_faces = both_faces[:, :FACE_NODES].reshape(elements, columns, FACE_NODES)
        swapped = (
            both_faces[:, FACE_NODES:].astype(jnp.bfloat16).reshape(elements, columns * FACE_NODES)
        )
        padded = extended(swapped, (("space", 0),), elements)
        picked = jnp.dot(picker, padded, preferred_element_type=jnp.float32)
        picked = picked.reshape(6, elements, columns, FACE_NODES)
        across = jnp.sum(picked * face_masks, axis=0)
        jumps = speeds * (across - own_faces)
        jumps = jumps.astype(jnp.bfloat16).reshape(elements * columns, FACE_NODES)
        moved = jnp.dot(flat_rounded, volume, preferred_element_type=jnp.float32)
        moved = moved + jnp.dot(jumps, lift_matrix, preferred_element_type=jnp.float32)
        return react(moved.reshape(state.shape), tables, reaction_rate * gain)

    def fine_step(state):
        return substep(substep(state, fine_volume, 1.0), fine_volume, 1.0)

    def coarse_step(state):
        return substep(state, coarse_volume, coarse_gain)

    def relax(start_state):
        points = []
        current = start_state
        for number in range(STRIDE - 1):
            current = fine_step(current)
            points.append(current)
        return points

    at_start = lax.axis_index("tm") == 0

    def entry(received):
        return jnp.where(at_start, initial_state, received)

    starting = entry(coarse_guess[0])
    relaxed = fine_step(relax(starting)[-1])
    second = entry(passed_along(relaxed.astype(jnp.bfloat16), "tm", 1).astype(relaxed.dtype))
    correction = fine_step(relax(second)[-1]) - coarse_step(second)
    gathered = lax.all_gather(correction[None], "tm", axis=0, tiled=True)
    position = lax.axis_index("tm")

    def advance(index, carry):
        value, kept_begin, kept_end = carry
        kept_begin = jnp.where(index == position, value, kept_begin)
        value = coarse_step(value) + lax.dynamic_index_in_dim(gathered, index, 0, keepdims=False)
        kept_end = jnp.where(index == position, value, kept_end)
        return (value, kept_begin, kept_end)

    final_value, beginning, ending = lax.fori_loop(
        0, lax.axis_size("tm"), advance, (initial_state, initial_state, initial_state)
    )
    points = relax(beginning) + [ending]
    return jnp.stack(points, axis=0)


def solution(mesh):
    placed = (
        P("tm", "space", None, None),
        P("space", None, None),
        P(),
        P(),
        P(),
        P(),
        P(),
        P(),
        P("space", None),
        P("space", None),
    )
    return jax.shard_map(
        body, mesh=mesh, in_specs=placed, out_specs=P("tm", "space", None, None), check_vma=False
    )
```

profile of v0, /device:TPU:24, one launch (start us, length us, event | category | flops | bytes accessed | tf_op | source)
XLA Modules:
  0.0 533.6 jit_solution(8992050762641135845)
XLA Ops:
  9.5 3.9 collective-permute-start.2
  32.4 3.6 collective-permute-start.6
  55.1 3.0 collective-permute-start.10
  77.2 3.1 collective-permute-start.14
  84.0 2.8 collective-permute-done.15
  102.3 4.0 collective-permute-start.19
  109.1 4.3 collective-permute-done.20
  117.6 3.0 collective-permute-start.22
  140.8 2.7 collective-permute-start.25
  152.4 3.2 collective-permute-start.27
  188.0 2.8 collective-permute-start.33
  203.4 39.6 %all-gather.3.cloned.1.call-done = f32[128,12,512]{2,0,1:T(8,128)} async-done(((f32[8,12,512]{2,0,1:T(8,128)}), f32[128,12,512]{2,0,1:T(8,128)}) %all-gather.3.cloned.1.call-update) | async-done | bytes 3145744 | tf_op jit(solution)/shard_map/all_gather | solution.py:153
  243.0 212.4 %while.20 = (s32[]{:T(128)}, bf16[8,12,512]{2,1,0:T(8,128)(2,1)S(1)}, bf16[8,12,512]{2,1,0:T(8,128)(2,1)S(1)}, f32[8,12,512]{2,1,0:T(8,128)}, bf16[512,512]{1,0:...) while((s32[]{:T(128)}, ...), condition=%wide.region_18.0_spmd.clone.clone.clone, body=%wide.region_16.0_spmd.sunk.clone.clone.clone.sunk | while | flops 218829632 | bytes 10833684 | solution.py:163
  243.4 3.4 collective-permute-start
  249.4 4.2 collective-permute-done.1
  313.5 3.4 collective-permute-done.1
  321.4 3.6 collective-permute-start
  327.3 4.5 collective-permute-done.1
  348.8 3.3 collective-permute-start
  354.8 4.4 collective-permute-done.1
  369.6 2.7 collective-permute-done.1
  390.4 2.7 collective-permute-start.1
  427.2 3.5 collective-permute-start
  433.1 4.3 collective-permute-done.1
  447.8 3.5 collective-permute-done.1
  455.9 4.4 collective-permute-start.36
  460.5 2.8 collective-permute-done.35
  467.3 3.5 collective-permute-start.37
  479.2 3.0 collective-permute-start.39
  490.7 3.0 collective-permute-start.41
  502.0 2.7 collective-permute-start.43
  513.0 3.0 collective-permute-start.45
  (781 shorter events, 373.9 us)
Async XLA Ops:
  6.5 236.5 %all-gather.3.cloned.1.call-start = ((), (), s32[]{:S(2)}) async-start(), calls=%async_computation | async-start | bytes 3342336 | tf_op jit(solution)/shard_map/all_gather | solution.py:153
  9.5 7.1 %collective-permute-start.2 = (bf16[8,4608]{1,0:T(8,128)(2,1)S(1)}, bf16[8,4608]{1,0:T(8,128)(2,1)S(1)}, u32[]{:S(2)}, u32[]{:S(2)}) collective-permute-start(bf16[8,4608]{1,0:T(8,128)(2,1)S(1)} %reshape.411), channel_id=1, source_target_pairs={{0,1},{1,2},{2,3},{3,4},{4,5},{5,6},{6,7},{7,0},{8,9},{9,10},{10,1... | collective-permute-start | bytes 221192 | tf_op jit(solution)/shard_map/ppermute | solution.py:23
  21.8 6.8 %collective-permute-start.4 = (bf16[8,4608]{1,0:T(8,128)(2,1)S(1)}, bf16[8,4608]{1,0:T(8,128)(2,1)S(1)}, u32[]{:S(2)}, u32[]{:S(2)}) collective-permute-start(bf16[8,4608]{1,0:T(8,128)(2,1)S(1)} %reshape.415), channel_id=1, source_target_pairs={{0,1},{1,2},{2,3},{3,4},{4,5},{5,6},{6,7},{7,0},{8,9},{9,10},{10,1... | collective-permute-start | bytes 221192 | tf_op jit(solution)/shard_map/ppermute | solution.py:23
  32.4 6.9 %collective-permute-start.6 = (bf16[8,4608]{1,0:T(8,128)(2,1)S(1)}, bf16[8,4608]{1,0:T(8,128)(2,1)S(1)}, u32[]{:S(2)}, u32[]{:S(2)}) collective-permute-start(bf16[8,4608]{1,0:T(8,128)(2,1)S(1)} %reshape.419), channel_id=1, source_target_pairs={{0,1},{1,2},{2,3},{3,4},{4,5},{5,6},{6,7},{7,0},{8,9},{9,10},{10,1... | collective-permute-start | bytes 221192 | tf_op jit(solution)/shard_map/ppermute | solution.py:23
  44.3 6.8 %collective-permute-start.8 = (bf16[8,4608]{1,0:T(8,128)(2,1)S(1)}, bf16[8,4608]{1,0:T(8,128)(2,1)S(1)}, u32[]{:S(2)}, u32[]{:S(2)}) collective-permute-start(bf16[8,4608]{1,0:T(8,128)(2,1)S(1)} %reshape.423), channel_id=1, source_target_pairs={{0,1},{1,2},{2,3},{3,4},{4,5},{5,6},{6,7},{7,0},{8,9},{9,10},{10,1... | collective-permute-start | bytes 221192 | tf_op jit(solution)/shard_map/ppermute | solution.py:23
  55.1 6.8 %collective-permute-start.10 = (bf16[8,4608]{1,0:T(8,128)(2,1)S(1)}, bf16[8,4608]{1,0:T(8,128)(2,1)S(1)}, u32[]{:S(2)}, u32[]{:S(2)}) collective-permute-start(bf16[8,4608]{1,0:T(8,128)(2,1)S(1)} %reshape.427), channel_id=1, source_target_pairs={{0,1},{1,2},{2,3},{3,4},{4,5},{5,6},{6,7},{7,0},{8,9},{9,10},{10,1... | collective-permute-start | bytes 221192 | tf_op jit(solution)/shard_map/ppermute | solution.py:23
  66.6 6.8 %collective-permute-start.12 = (bf16[8,4608]{1,0:T(8,128)(2,1)S(1)}, bf16[8,4608]{1,0:T(8,128)(2,1)S(1)}, u32[]{:S(2)}, u32[]{:S(2)}) collective-permute-start(bf16[8,4608]{1,0:T(8,128)(2,1)S(1)} %reshape.431), channel_id=1, source_target_pairs={{0,1},{1,2},{2,3},{3,4},{4,5},{5,6},{6,7},{7,0},{8,9},{9,10},{10,1... | collective-permute-start | bytes 221192 | tf_op jit(solution)/shard_map/ppermute | solution.py:23
  77.2 6.8 %collective-permute-start.14 = (bf16[8,4608]{1,0:T(8,128)(2,1)S(1)}, bf16[8,4608]{1,0:T(8,128)(2,1)S(1)}, u32[]{:S(2)}, u32[]{:S(2)}) collective-permute-start(bf16[8,4608]{1,0:T(8,128)(2,1)S(1)} %reshape.435), channel_id=1, source_target_pairs={{0,1},{1,2},{2,3},{3,4},{4,5},{5,6},{6,7},{7,0},{8,9},{9,10},{10,1... | collective-permute-start | bytes 221192 | tf_op jit(solution)/shard_map/ppermute | solution.py:23
  89.3 6.8 %collective-permute-start.16 = (bf16[8,4608]{1,0:T(8,128)(2,1)S(1)}, bf16[8,4608]{1,0:T(8,128)(2,1)S(1)}, u32[]{:S(2)}, u32[]{:S(2)}) collective-permute-start(bf16[8,4608]{1,0:T(8,128)(2,1)S(1)} %reshape.439), channel_id=1, source_target_pairs={{0,1},{1,2},{2,3},{3,4},{4,5},{5,6},{6,7},{7,0},{8,9},{9,10},{10,1... | collective-permute-start | bytes 221192 | tf_op jit(solution)/shard_map/ppermute | solution.py:23
  102.3 6.8 %collective-permute-start.19 = (bf16[8,4608]{1,0:T(8,128)(2,1)S(1)}, bf16[8,4608]{1,0:T(8,128)(2,1)S(1)}, u32[]{:S(2)}, u32[]{:S(2)}) collective-permute-start(bf16[8,4608]{1,0:T(8,128)(2,1)S(1)} %reshape.443), channel_id=1, source_target_pairs={{0,1},{1,2},{2,3},{3,4},{4,5},{5,6},{6,7},{7,0},{8,9},{9,10},{10,1... | collective-permute-start | bytes 221192 | tf_op jit(solution)/shard_map/ppermute | solution.py:23
  106.3 7.2 %collective-permute-start.20 = (bf16[8,4608]{1,0:T(8,128)(2,1)S(1)}, bf16[8,4608]{1,0:T(8,128)(2,1)S(1)}, u32[]{:S(2)}, u32[]{:S(2)}) collective-permute-start(bf16[8,4608]{1,0:T(8,128)(2,1)S(1)} %reshape.443), channel_id=1, source_target_pairs={{1,0},{2,1},{3,2},{4,3},{5,4},{6,5},{7,6},{0,7},{9,8},{10,9},{11,1... | collective-permute-start | bytes 221192 | tf_op jit(solution)/shard_map/ppermute | solution.py:26
  116.2 7.9 %collective-permute-start.21 = (bf16[8,4608]{1,0:T(8,128)(2,1)S(1)}, bf16[8,4608]{1,0:T(8,128)(2,1)S(1)}, u32[]{:S(2)}, u32[]{:S(2)}) collective-permute-start(bf16[8,4608]{1,0:T(8,128)(2,1)S(1)} %reshape.447), channel_id=1, source_target_pairs={{0,1},{1,2},{2,3},{3,4},{4,5},{5,6},{6,7},{7,0},{8,9},{9,10},{10,1... | collective-permute-start | bytes 221192 | tf_op jit(solution)/shard_map/ppermute | solution.py:23
  117.6 7.6 %collective-permute-start.22 = (bf16[8,4608]{1,0:T(8,128)(2,1)S(1)}, bf16[8,4608]{1,0:T(8,128)(2,1)}, u32[]{:S(2)}, u32[]{:S(2)}) collective-permute-start(bf16[8,4608]{1,0:T(8,128)(2,1)S(1)} %reshape.447), channel_id=1, source_target_pairs={{1,0},{2,1},{3,2},{4,3},{5,4},{6,5},{7,6},{0,7},{9,8},{10,9},{11,1... | collective-permute-start | bytes 221192 | tf_op jit(solution)/shard_map/ppermute | solution.py:26
  129.2 6.9 %collective-permute-start.23 = (bf16[8,4608]{1,0:T(8,128)(2,1)S(1)}, bf16[8,4608]{1,0:T(8,128)(2,1)S(1)}, u32[]{:S(2)}, u32[]{:S(2)}) collective-permute-start(bf16[8,4608]{1,0:T(8,128)(2,1)S(1)} %reshape.451), channel_id=1, source_target_pairs={{0,1},{1,2},{2,3},{3,4},{4,5},{5,6},{6,7},{7,0},{8,9},{9,10},{10,1... | collective-permute-start | bytes 221192 | tf_op jit(solution)/shard_map/ppermute | solution.py:23
  140.8 6.9 %collective-permute-start.25 = (bf16[8,4608]{1,0:T(8,128)(2,1)S(1)}, bf16[8,4608]{1,0:T(8,128)(2,1)S(1)}, u32[]{:S(2)}, u32[]{:S(2)}) collective-permute-start(bf16[8,4608]{1,0:T(8,128)(2,1)S(1)} %reshape.455), channel_id=1, source_target_pairs={{0,1},{1,2},{2,3},{3,4},{4,5},{5,6},{6,7},{7,0},{8,9},{9,10},{10,1... | collective-permute-start | bytes 221192 | tf_op jit(solution)/shard_map/ppermute | solution.py:23
  152.4 6.8 %collective-permute-start.27 = (bf16[8,4608]{1,0:T(8,128)(2,1)S(1)}, bf16[8,4608]{1,0:T(8,128)(2,1)S(1)}, u32[]{:S(2)}, u32[]{:S(2)}) collective-permute-start(bf16[8,4608]{1,0:T(8,128)(2,1)S(1)} %reshape.459), channel_id=1, source_target_pairs={{0,1},{1,2},{2,3},{3,4},{4,5},{5,6},{6,7},{7,0},{8,9},{9,10},{10,1... | collective-permute-start | bytes 221192 | tf_op jit(solution)/shard_map/ppermute | solution.py:23
  164.8 6.8 %collective-permute-start.29 = (bf16[8,4608]{1,0:T(8,128)(2,1)S(1)}, bf16[8,4608]{1,0:T(8,128)(2,1)S(1)}, u32[]{:S(2)}, u32[]{:S(2)}) collective-permute-start(bf16[8,4608]{1,0:T(8,128)(2,1)S(1)} %reshape.463), channel_id=1, source_target_pairs={{0,1},{1,2},{2,3},{3,4},{4,5},{5,6},{6,7},{7,0},{8,9},{9,10},{10,1... | collective-permute-start | bytes 221192 | tf_op jit(solution)/shard_map/ppermute | solution.py:23
  176.3 6.8 %collective-permute-start.31 = (bf16[8,4608]{1,0:T(8,128)(2,1)S(1)}, bf16[8,4608]{1,0:T(8,128)(2,1)S(1)}, u32[]{:S(2)}, u32[]{:S(2)}) collective-permute-start(bf16[8,4608]{1,0:T(8,128)(2,1)S(1)} %reshape.467), channel_id=1, source_target_pairs={{0,1},{1,2},{2,3},{3,4},{4,5},{5,6},{6,7},{7,0},{8,9},{9,10},{10,1... | collective-permute-start | bytes 221192 | tf_op jit(solution)/shard_map/ppermute | solution.py:23
  188.0 6.8 %collective-permute-start.33 = (bf16[8,4608]{1,0:T(8,128)(2,1)S(1)}, bf16[8,4608]{1,0:T(8,128)(2,1)S(1)}, u32[]{:S(2)}, u32[]{:S(2)}) collective-permute-start(bf16[8,4608]{1,0:T(8,128)(2,1)S(1)} %reshape.471), channel_id=1, source_target_pairs={{0,1},{1,2},{2,3},{3,4},{4,5},{5,6},{6,7},{7,0},{8,9},{9,10},{10,1... | collective-permute-start | bytes 221192 | tf_op jit(solution)/shard_map/ppermute | solution.py:23
  246.8 6.8 %collective-permute-start.1 = (bf16[8,4608]{1,0:T(8,128)(2,1)S(1)}, bf16[8,4608]{1,0:T(8,128)(2,1)S(1)}, u32[]{:S(2)}, u32[]{:S(2)}) collective-permute-start(bf16[8,4608]{1,0:T(8,128)(2,1)S(1)} %reshape.526), channel_id=1, source_target_pairs={{0,1},{1,2},{2,3},{3,4},{4,5},{5,6},{6,7},{7,0},{8,9},{9,10},{10,1... | collective-permute-start | bytes 221192 | tf_op jit(solution)/shard_map/while/body/eval_jaxpr/ppermute | solution.py:23
  258.1 6.8 %collective-permute-start.1 = (bf16[8,4608]{1,0:T(8,128)(2,1)S(1)}, bf16[8,4608]{1,0:T(8,128)(2,1)S(1)}, u32[]{:S(2)}, u32[]{:S(2)}) collective-permute-start(bf16[8,4608]{1,0:T(8,128)(2,1)S(1)} %reshape.526), channel_id=1, source_target_pairs={{0,1},{1,2},{2,3},{3,4},{4,5},{5,6},{6,7},{7,0},{8,9},{9,10},{10,1... | collective-permute-start | bytes 221192 | tf_op jit(solution)/shard_map/while/body/eval_jaxpr/ppermute | solution.py:23
  271.1 6.8 %collective-permute-start.1 = (bf16[8,4608]{1,0:T(8,128)(2,1)S(1)}, bf16[8,4608]{1,0:T(8,128)(2,1)S(1)}, u32[]{:S(2)}, u32[]{:S(2)}) collective-permute-start(bf16[8,4608]{1,0:T(8,128)(2,1)S(1)} %reshape.526), channel_id=1, source_target_pairs={{0,1},{1,2},{2,3},{3,4},{4,5},{5,6},{6,7},{7,0},{8,9},{9,10},{10,1... | collective-permute-start | bytes 221192 | tf_op jit(solution)/shard_map/while/body/eval_jaxpr/ppermute | solution.py:23
  325.0 6.9 %collective-permute-start.1 = (bf16[8,4608]{1,0:T(8,128)(2,1)S(1)}, bf16[8,4608]{1,0:T(8,128)(2,1)S(1)}, u32[]{:S(2)}, u32[]{:S(2)}) collective-permute-start(bf16[8,4608]{1,0:T(8,128)(2,1)S(1)} %reshape.526), channel_id=1, source_target_pairs={{0,1},{1,2},{2,3},{3,4},{4,5},{5,6},{6,7},{7,0},{8,9},{9,10},{10,1... | collective-permute-start | bytes 221192 | tf_op jit(solution)/shard_map/while/body/eval_jaxpr/ppermute | solution.py:23
  352.2 7.0 %collective-permute-start.1 = (bf16[8,4608]{1,0:T(8,128)(2,1)S(1)}, bf16[8,4608]{1,0:T(8,128)(2,1)S(1)}, u32[]{:S(2)}, u32[]{:S(2)}) collective-permute-start(bf16[8,4608]{1,0:T(8,128)(2,1)S(1)} %reshape.526), channel_id=1, source_target_pairs={{0,1},{1,2},{2,3},{3,4},{4,5},{5,6},{6,7},{7,0},{8,9},{9,10},{10,1... | collective-permute-start | bytes 221192 | tf_op jit(solution)/shard_map/while/body/eval_jaxpr/ppermute | solution.py:23
  444.2 7.1 %collective-permute-start.1 = (bf16[8,4608]{1,0:T(8,128)(2,1)S(1)}, bf16[8,4608]{1,0:T(8,128)(2,1)S(1)}, u32[]{:S(2)}, u32[]{:S(2)}) collective-permute-start(bf16[8,4608]{1,0:T(8,128)(2,1)S(1)} %reshape.526), channel_id=1, source_target_pairs={{0,1},{1,2},{2,3},{3,4},{4,5},{5,6},{6,7},{7,0},{8,9},{9,10},{10,1... | collective-permute-start | bytes 221192 | tf_op jit(solution)/shard_map/while/body/eval_jaxpr/ppermute | solution.py:23
  455.8 7.5 %collective-permute-start.35 = (bf16[8,4608]{1,0:T(8,128)(2,1)S(1)}, bf16[8,4608]{1,0:T(8,128)(2,1)S(1)}, u32[]{:S(2)}, u32[]{:S(2)}) collective-permute-start(bf16[8,4608]{1,0:T(8,128)(2,1)S(1)} %reshape.476), channel_id=1, source_target_pairs={{0,1},{1,2},{2,3},{3,4},{4,5},{5,6},{6,7},{7,0},{8,9},{9,10},{10,1... | collective-permute-start | bytes 221192 | tf_op jit(solution)/shard_map/ppermute | solution.py:23
  455.9 8.9 %collective-permute-start.36 = (bf16[8,4608]{1,0:T(8,128)(2,1)S(1)}, bf16[8,4608]{1,0:T(8,128)(2,1)S(1)}, u32[]{:S(2)}, u32[]{:S(2)}) collective-permute-start(bf16[8,4608]{1,0:T(8,128)(2,1)S(1)} %reshape.476), channel_id=1, source_target_pairs={{1,0},{2,1},{3,2},{4,3},{5,4},{6,5},{7,6},{0,7},{9,8},{10,9},{11,1... | collective-permute-start | bytes 221192 | tf_op jit(solution)/shard_map/ppermute | solution.py:26
  467.3 6.9 %collective-permute-start.37 = (bf16[8,4608]{1,0:T(8,128)(2,1)S(1)}, bf16[8,4608]{1,0:T(8,128)(2,1)S(1)}, u32[]{:S(2)}, u32[]{:S(2)}) collective-permute-start(bf16[8,4608]{1,0:T(8,128)(2,1)S(1)} %reshape.480), channel_id=1, source_target_pairs={{0,1},{1,2},{2,3},{3,4},{4,5},{5,6},{6,7},{7,0},{8,9},{9,10},{10,1... | collective-permute-start | bytes 221192 | tf_op jit(solution)/shard_map/ppermute | solution.py:23
  479.2 6.8 %collective-permute-start.39 = (bf16[8,4608]{1,0:T(8,128)(2,1)S(1)}, bf16[8,4608]{1,0:T(8,128)(2,1)S(1)}, u32[]{:S(2)}, u32[]{:S(2)}) collective-permute-start(bf16[8,4608]{1,0:T(8,128)(2,1)S(1)} %reshape.484), channel_id=1, source_target_pairs={{0,1},{1,2},{2,3},{3,4},{4,5},{5,6},{6,7},{7,0},{8,9},{9,10},{10,1... | collective-permute-start | bytes 221192 | tf_op jit(solution)/shard_map/ppermute | solution.py:23
  490.7 6.8 %collective-permute-start.41 = (bf16[8,4608]{1,0:T(8,128)(2,1)S(1)}, bf16[8,4608]{1,0:T(8,128)(2,1)S(1)}, u32[]{:S(2)}, u32[]{:S(2)}) collective-permute-start(bf16[8,4608]{1,0:T(8,128)(2,1)S(1)} %reshape.488), channel_id=1, source_target_pairs={{0,1},{1,2},{2,3},{3,4},{4,5},{5,6},{6,7},{7,0},{8,9},{9,10},{10,1... | collective-permute-start | bytes 221192 | tf_op jit(solution)/shard_map/ppermute | solution.py:23
  502.0 6.8 %collective-permute-start.43 = (bf16[8,4608]{1,0:T(8,128)(2,1)S(1)}, bf16[8,4608]{1,0:T(8,128)(2,1)S(1)}, u32[]{:S(2)}, u32[]{:S(2)}) collective-permute-start(bf16[8,4608]{1,0:T(8,128)(2,1)S(1)} %reshape.492), channel_id=1, source_target_pairs={{0,1},{1,2},{2,3},{3,4},{4,5},{5,6},{6,7},{7,0},{8,9},{9,10},{10,1... | collective-permute-start | bytes 221192 | tf_op jit(solution)/shard_map/ppermute | solution.py:23
  513.0 6.8 %collective-permute-start.45 = (bf16[8,4608]{1,0:T(8,128)(2,1)S(1)}, bf16[8,4608]{1,0:T(8,128)(2,1)S(1)}, u32[]{:S(2)}, u32[]{:S(2)}) collective-permute-start(bf16[8,4608]{1,0:T(8,128)(2,1)S(1)} %reshape.496), channel_id=1, source_target_pairs={{0,1},{1,2},{2,3},{3,4},{4,5},{5,6},{6,7},{7,0},{8,9},{9,10},{10,1... | collective-permute-start | bytes 221192 | tf_op jit(solution)/shard_map/ppermute | solution.py:23
  (58 other events, 435.3 us)
Sparse Core Ops, SparseCore 0:
  201.7 41.2 all-gather.2
where the time goes:
time: 543 us; the launch traced here: 534 us
  waiting for transfers between devices  189 us (35%)
  starting transfers between devices  159 us (29%)
  matrix products  130 us (24%)
  local copies, waits for them, and re-layouts  28.8 us (5%)
  between operations  16.1 us (3%)
  other arithmetic  8.49 us (2%)
    ppermute x38, waiting for transfers between devices, extended(): lax.ppermute(lax.slice_in_dim(block, block.shape[dim] - width, None, axis...  87.5 us
    ppermute x38, starting transfers between devices, extended(): lax.ppermute(lax.slice_in_dim(block, block.shape[dim] - width, None, axis...  84.8 us
    ppermute x38, starting transfers between devices, extended(): lax.ppermute(lax.slice_in_dim(block, 0, width, axis=dim), axis, backward)  72.9 us
    ppermute x38, waiting for transfers between devices, extended(): lax.ppermute(lax.slice_in_dim(block, 0, width, axis=dim), axis, backward)  61.4 us
    dot_general x39, matrix products, react(): jnp.einsum('rv,...rn->...vn', change_table, speed_term, precision=lax.Pre...  52.7 us
    all_gather x1, waiting for transfers between devices, body(): gathered = lax.all_gather(correction[None], 'tm', axis=0, tiled=True)  39.6 us
    dot_general x39, matrix products, react(): jnp.einsum('rv,...vn->...rn', second_table, state, precision=lax.Precisio...  17.5 us
    dot_general x39, matrix products, react(): jnp.einsum('rv,...vn->...rn', first_table, state, precision=lax.Precision...  17.5 us
  transfers between devices with their start and end apart: 78, of which 76 were waited for; matrix products, arithmetic and copies ran while one was open for 6% of the time, Pallas kernels for 0%

commit v1 on v0

v1 whole, which is shorter than its diff:
```python
import jax
import jax.numpy as jnp
import numpy as np
from jax import lax
from jax.experimental import pallas as pl
from jax.experimental.pallas import tpu as pltpu
from jax.sharding import PartitionSpec as P

SIDE = 8
NODES = 512
FACES = 384
VARS = 12
REACTIONS = 24
BLOCK = 8
BLOCKS = 8
ELEMS = 64
ROWS = VARS * ELEMS
OWN = 4
STRIDE = 4
GAIN = 4.0
BF = jnp.bfloat16
F32 = jnp.float32


def swapped_face_table():
    inner = np.arange(64)
    first, second = inner // 8, inner % 8
    nodes = [
        first * 64 + second,
        first * 64 + 56 + second,
        first * 64 + second * 8,
        first * 64 + second * 8 + 7,
    ]
    table = np.zeros((NODES, 256), np.float32)
    for place, face in enumerate((1, 0, 3, 2)):
        table[nodes[face], place * 64 + inner] = 1.0
    return table


def gather_tables(code, table_ref):
    row = lax.broadcasted_iota(jnp.int32, (ELEMS, ELEMS), 0)
    column = lax.broadcasted_iota(jnp.int32, (ELEMS, ELEMS), 1)
    minus = jnp.where(row == column, -1.0, 0.0)
    home = row - jnp.bitwise_and(row, 7)
    for pair in range(3):
        parts = []
        for face in (2 * pair, 2 * pair + 1):
            source = jnp.bitwise_and(home + code[:, face : face + 1] + 56, 63)
            parts.append(jnp.where(source == column, 1.0, 0.0))
        table_ref[pair, :, 0:128] = jnp.concatenate(parts, axis=1).astype(BF)
        table_ref[pair, :, 128:192] = minus.astype(BF)


def transport(xj_ref, t_ref, s_ref, table_ref, face_ref, w_ref, speed_ref):
    lane = lax.broadcasted_iota(jnp.int32, (ELEMS, 128), 1)
    left = lane < 64
    zero = jnp.zeros((ELEMS, 128), BF)
    s_ref[:, 128:384] = jnp.dot(xj_ref[:, 0:NODES], face_ref[...], preferred_element_type=F32).astype(BF)
    lo = xj_ref[:, 0:128]
    hi = xj_ref[:, NODES - 128 : NODES]
    s_ref[:, 0:128] = jnp.concatenate([hi[:, 64:128], lo[:, 0:64]], axis=1)

    for v in range(0, VARS, 2):
        for pair in range(3):
            stacks = []
            for half in range(2):
                swapped = s_ref[pl.ds((v + half) * ELEMS, ELEMS), pair * 128 : (pair + 1) * 128]
                own = jnp.concatenate([swapped[:, 64:128], swapped[:, 0:64]], axis=1)
                stacks.append(
                    jnp.concatenate(
                        [jnp.where(left, swapped, zero), jnp.where(left, zero, swapped), own], axis=0
                    )
                )
            jump = jnp.dot(
                table_ref[pair], jnp.concatenate(stacks, axis=1), preferred_element_type=F32
            )
            for half in range(2):
                xj_ref[pl.ds((v + half) * ELEMS, ELEMS), NODES + pair * 128 : NODES + (pair + 1) * 128] = (
                    jump[:, half * 128 : (half + 1) * 128] * speed_ref[v + half]
                ).astype(BF)

    for cut in range(2):
        lanes = pl.ds(cut * 256, 256)
        moved = jnp.dot(xj_ref[...], w_ref[:, lanes], preferred_element_type=F32)
        t_ref[:, :, lanes] = moved.reshape(VARS, ELEMS, 256).astype(t_ref.dtype)


def react(t_ref, plus_ref, minus_ref, species_ref, rate_ref, gain):
    plus_ref[...] = t_ref[...]
    minus_ref[...] = jnp.zeros_like(minus_ref)

    def one(r, carry):
        first = species_ref[r, 0]
        second = species_ref[r, 1]
        made = species_ref[r, 2]
        a = t_ref[first]
        b = t_ref[second]
        rate = (gain * rate_ref[r]) * (a * b) / (1.0 + a * a + b * b)
        plus_ref[made] += rate
        minus_ref[first] += rate
        return carry

    lax.fori_loop(0, REACTIONS, one, 0)


def substep(xj_ref, t_ref, s_ref, table_ref, face_ref, w_ref, speed_ref,
            plus_ref, minus_ref, species_ref, rate_ref, gain):
    transport(xj_ref, t_ref, s_ref, table_ref, face_ref, w_ref, speed_ref)
    react(t_ref, plus_ref, minus_ref, species_ref, rate_ref, gain)


def state_of(plus_ref, minus_ref):
    return (plus_ref[...] - minus_ref[...]).reshape(ROWS, NODES)


def own_rows(value, v):
    return value[v * ELEMS + OWN * BLOCK : v * ELEMS + (OWN + 1) * BLOCK]


def relax_kernel(group_ref, species_ref, rate_ref, speed_ref, *refs):
    parts = refs[:BLOCKS]
    face_ref, fine_ref, coarse_ref, lift_ref = refs[BLOCKS : BLOCKS + 4]
    send_ref, base_ref, second_ref, table_ref = refs[BLOCKS + 4 : BLOCKS + 8]
    xj, t, s, plus, minus, w, g = refs[BLOCKS + 8 :]
    group = group_ref[0]
    values = [part[...].astype(F32) for part in parts]
    for v in range(VARS):
        rows = jnp.concatenate([p[v * BLOCK : (v + 1) * BLOCK] for p in values], axis=0)
        xj[v * ELEMS : (v + 1) * ELEMS, 0:NODES] = rows.astype(BF)
    codes = jnp.concatenate([p[VARS * BLOCK : (VARS + 1) * BLOCK, 0:128] for p in values], axis=0)
    gather_tables(codes.astype(jnp.int32), table_ref)
    w[0:NODES, :] = fine_ref[...]
    w[NODES:, :] = lift_ref[...]
    second_ref[...] = xj[:, 0:NODES]

    def fine(index, carry):
        substep(xj, t, s, table_ref, face_ref, w, speed_ref, plus, minus, species_ref, rate_ref, 1.0)
        xj[:, 0:NODES] = state_of(plus, minus).astype(BF)
        return carry

    lax.fori_loop(0, 8, fine, 0)

    @pl.when(group == 0)
    def _():
        xj[:, 0:NODES] = second_ref[...]

    second_ref[...] = xj[:, 0:NODES]
    w[0:NODES, :] = coarse_ref[...]
    substep(xj, t, s, table_ref, face_ref, w, speed_ref, plus, minus, species_ref, rate_ref, GAIN)
    g[...] = state_of(plus, minus)
    w[0:NODES, :] = fine_ref[...]
    lax.fori_loop(0, 8, fine, 0)
    last = state_of(plus, minus)
    correction = last - g[...]
    send = jnp.where(group == 1, last, correction)
    send_ref[...] = send.astype(BF)
    base = jnp.where(group <= 1, last, correction)
    for v in range(VARS):
        base_ref[v] = own_rows(base, v)


def chain_kernel(group_ref, species_ref, rate_ref, speed_ref,
                 first_ref, term_ref, second_ref, base_ref, table_ref,
                 face_ref, fine_ref, coarse_ref, lift_ref, out_ref,
                 xj, t, s, plus, minus, w, begin):
    group = group_ref[0]
    step = pl.program_id(0)
    index = step + 2

    @pl.when(step == 0)
    def _():
        w[0:NODES, :] = coarse_ref[...]
        w[NODES:, :] = lift_ref[...]
        xj[:, 0:NODES] = first_ref[0]
        begin[...] = second_ref[...]
        out_ref[STRIDE - 1] = base_ref[...]

    @pl.when(index == group)
    def _():
        begin[...] = xj[:, 0:NODES]

    substep(xj, t, s, table_ref, face_ref, w, speed_ref, plus, minus, species_ref, rate_ref, GAIN)
    stepped = state_of(plus, minus)

    @pl.when(index == group)
    def _():
        for v in range(VARS):
            out_ref[STRIDE - 1, v] = own_rows(stepped, v) + base_ref[v]

    xj[:, 0:NODES] = (stepped + term_ref[0].astype(F32)).astype(BF)

    @pl.when(step == pl.num_programs(0) - 1)
    def _():
        w[0:NODES, :] = fine_ref[...]
        xj[:, 0:NODES] = begin[...]

        def fine(index, carry):
            substep(
                xj, t, s, table_ref, face_ref, w, speed_ref, plus, minus, species_ref, rate_ref, 1.0
            )
            state = state_of(plus, minus)
            xj[:, 0:NODES] = state.astype(BF)
            for v in range(VARS):
                out_ref[index // 2, v] = own_rows(state, v)
            return carry

        lax.fori_loop(0, 2 * (STRIDE - 1), fine, 0)


VMEM_SPEC = pl.BlockSpec(memory_space=pltpu.VMEM)
SMEM_SPEC = pl.BlockSpec(memory_space=pltpu.SMEM)


def work_buffers():
    return [
        pltpu.VMEM((ROWS, NODES + FACES), BF),
        pltpu.VMEM((VARS, ELEMS, NODES), F32),
        pltpu.VMEM((ROWS, FACES), BF),
        pltpu.VMEM((VARS, ELEMS, NODES), F32),
        pltpu.VMEM((VARS, ELEMS, NODES), F32),
        pltpu.VMEM((NODES + FACES, NODES), BF),
    ]


def body(
    coarse_guess,
    initial_state,
    fine_volume,
    coarse_volume,
    lift_matrix,
    wave_speed,
    reaction_rate,
    species_map,
    neighbour_element,
    neighbour_rank,
):
    group = lax.axis_index("tm")
    groups = lax.axis_size("tm")
    start = jnp.where((group == 0) | (group == groups - 1), initial_state, coarse_guess[0])
    start = jnp.transpose(start, (1, 0, 2)).reshape(VARS * BLOCK, NODES).astype(BF)
    code = ((neighbour_rank + 1) * BLOCK + neighbour_element).astype(BF)
    code = jnp.pad(code, ((0, 8), (0, NODES - 6)))
    payload = jnp.concatenate([start, code], axis=0)
    parts = []
    for place in range(BLOCKS):
        pairs = []
        for source in range(groups):
            for block in range(BLOCKS):
                target = (source + 1) % groups
                pairs.append((source * BLOCKS + block, target * BLOCKS + (block + OWN - place) % BLOCKS))
        parts.append(lax.ppermute(payload, ("tm", "space"), pairs))
    face_table = jnp.asarray(swapped_face_table()).astype(BF)
    group_array = group.astype(jnp.int32).reshape(1)
    params = pltpu.CompilerParams(vmem_limit_bytes=56 * 1024 * 1024)
    send, base, second, table = pl.pallas_call(
        relax_kernel,
        out_shape=(
            jax.ShapeDtypeStruct((ROWS, NODES), BF),
            jax.ShapeDtypeStruct((VARS, BLOCK, NODES), F32),
            jax.ShapeDtypeStruct((ROWS, NODES), BF),
            jax.ShapeDtypeStruct((3, ELEMS, 192), BF),
        ),
        in_specs=[SMEM_SPEC] * 4 + [VMEM_SPEC] * (BLOCKS + 4),
        out_specs=(VMEM_SPEC,) * 4,
        scratch_shapes=work_buffers() + [pltpu.VMEM((ROWS, NODES), F32)],
        compiler_params=params,
    )(
        group_array, species_map, reaction_rate, wave_speed,
        *parts, face_table, fine_volume, coarse_volume, lift_matrix,
    )
    terms = lax.all_gather(send, "tm", axis=0, tiled=False)
    full = lambda *shape: pl.BlockSpec(shape, lambda k: (0,) * len(shape))
    out = pl.pallas_call(
        chain_kernel,
        grid=(14,),
        out_shape=jax.ShapeDtypeStruct((STRIDE, VARS, BLOCK, NODES), F32),
        in_specs=[SMEM_SPEC] * 4
        + [
            pl.BlockSpec((1, ROWS, NODES), lambda k: (1, 0, 0)),
            pl.BlockSpec((1, ROWS, NODES), lambda k: (k + 2, 0, 0)),
            full(ROWS, NODES),
            full(VARS, BLOCK, NODES),
            full(3, ELEMS, 192),
            full(NODES, 256),
            full(NODES, NODES),
            full(NODES, NODES),
            full(FACES, NODES),
        ],
        out_specs=full(STRIDE, VARS, BLOCK, NODES),
        scratch_shapes=work_buffers() + [pltpu.VMEM((ROWS, NODES), BF)],
        compiler_params=params,
    )(
        group_array, species_map, reaction_rate, wave_speed,
        terms, terms, second, base, table, face_table, fine_volume, coarse_volume, lift_matrix,
    )
    return jnp.transpose(out, (0, 2, 1, 3))


def solution(mesh):
    placed = (
        P("tm", "space", None, None),
        P("space", None, None),
        P(),
        P(),
        P(),
        P(),
        P(),
        P(),
        P("space", None),
        P("space", None),
    )
    return jax.shard_map(
        body, mesh=mesh, in_specs=placed, out_specs=P("tm", "space", None, None), check_vma=False
    )
```

time: 543 us -> 255 us (0.47)
  the two profiles are of different devices: /device:TPU:24 before, /device:TPU:1 now
where the time goes in v1:
time: 255 us
  Pallas kernels  141 us (55%)
  waiting for transfers between devices  75.2 us (29%)
  starting transfers between devices  20.9 us (8%)
  between operations  13.5 us (5%)
    pallas_call x1, Pallas kernels, body(): pl.pallas_call(chain_kernel, grid=(14,), out_shape=jax.ShapeDtypeStruct((...  77.3 us
    all_gather x1, waiting for transfers between devices, body(): terms = lax.all_gather(send, 'tm', axis=0, tiled=False)  70.1 us
    pallas_call x1, Pallas kernels, body(): pl.pallas_call(relax_kernel, out_shape=(jax.ShapeDtypeStruct((ROWS, NODES...  64.1 us
    ppermute x8, starting transfers between devices, body(): parts.append(lax.ppermute(payload, ('tm', 'space'), pairs))  20.9 us
    ppermute x8, waiting for transfers between devices, body(): parts.append(lax.ppermute(payload, ('tm', 'space'), pairs))  5.14 us
  transfers between devices with their start and end apart: 9, of which 3 were waited for; matrix products, arithmetic and copies ran while one was open for 1% of the time, Pallas kernels for 0%

profile of v1, /device:TPU:1, one launch (start us, length us, event | category | flops | bytes accessed | tf_op | source)
XLA Modules:
  0.0 254.7 jit_solution(8152375226158786422)
XLA Ops:
  6.5 0.0 all-gather.3.cloned.1.call-start
  6.5 0.7 add_convert_fusion
  7.2 1.0 fusion.3
  8.2 8.6 %collective-permute-start.7 = (bf16[112,512]{1,0:T(8,128)(2,1)S(1)}, bf16[112,512]{1,0:T(8,128)(2,1)S(1)}, u32[]{:S(2)}, u32[]{:S(2)}) collective-permute-start(bf16[112,512]{1,0:T(8,128)(2,1)S(1)} %fusion.2), channel_id=1, source_target_pairs={{0,13},{1,14},{2,15},{3,8},{4,9},{5,10},{6,11},{7,12},{8,21},{9,22... | collective-permute-start | bytes 344072 | tf_op jit(solution)/shard_map/ppermute | solution.py:251
  16.8 0.5 collective-permute-start.6
  17.3 0.3 collective-permute-start.5
  17.6 1.5 collective-permute-start.4
  19.1 3.7 %collective-permute-start.3 = (bf16[112,512]{1,0:T(8,128)(2,1)S(1)}, bf16[112,512]{1,0:T(8,128)(2,1)S(1)}, u32[]{:S(2)}, u32[]{:S(2)}) collective-permute-start(bf16[112,512]{1,0:T(8,128)(2,1)S(1)} %fusion.2), channel_id=1, source_target_pairs={{0,9},{1,10},{2,11},{3,12},{4,13},{5,14},{6,15},{7,8},{8,17},{9,18... | collective-permute-start | bytes 344072 | tf_op jit(solution)/shard_map/ppermute | solution.py:251
  22.8 0.0 collective-permute-done.7.refs_7_
  22.8 0.6 collective-permute-start.2
  23.4 1.3 collective-permute-done.6.refs_6_
  24.7 1.2 collective-permute-start.1
  25.9 0.0 collective-permute-done.5.refs_5_
  25.9 4.6 %collective-permute-start = (bf16[112,512]{1,0:T(8,128)(2,1)S(1)}, bf16[112,512]{1,0:T(8,128)(2,1)S(1)}, u32[]{:S(2)}, u32[]{:S(2)}) collective-permute-start(bf16[112,512]{1,0:T(8,128)(2,1)S(1)} %fusion.2), channel_id=1, source_target_pairs={{0,12},{1,13},{2,14},{3,15},{4,8},{5,9},{6,10},{7,11},{8,20},{9,21... | collective-permute-start | bytes 344072 | tf_op jit(solution)/shard_map/ppermute | solution.py:251
  30.5 1.4 copy.13.species_ref
  31.8 0.0 collective-permute-done.4.refs_4_
  31.8 0.0 collective-permute-done.3.refs_3_
  31.8 0.0 copy-start.4
  31.9 0.0 collective-permute-done.2.refs_2_
  31.9 0.0 copy-start.5
  31.9 3.8 %collective-permute-done.1.refs_1_ = bf16[112,512]{1,0:T(8,128)(2,1)S(1)} collective-permute-done((bf16[112,512]{1,0:T(8,128)(2,1)S(1)}, bf16[112,512]{1,0:T(8,128)(2,1)S(1)}, u32[]{:S(2)}, u32[]{:S(2)}) %collective-permute-start.1) | collective-permute-done | bytes 114720 | tf_op jit(solution)/shard_map/ppermute | solution.py:251
  35.7 0.0 collective-permute-done.refs_0_
  35.7 0.0 copy-done
  35.7 0.0 copy-done.1
  35.7 0.0 copy-done.2
  35.7 0.0 copy-done.3
  35.7 0.6 copy-done.6
  36.3 0.1 copy-done.7
  36.4 64.1 %shard_map.109 = (bf16[768,512]{1,0:T(8,128)(2,1)}, f32[12,8,512]{2,1,0:T(8,128)}, bf16[768,512]{1,0:T(8,128)(2,1)}, bf16[3,64,192]{2,1,0:T(8,128)(2,1)}) custom-call(s32[1]{0:T(128)} %bitcast.group_ref, s32[24,3]{1,0:T(8,128)} %copy.13.species_ref, f32[24]{0:T(128)} %rate_ref.3, f32[12]{0:T(128)} %speed_ref.3, bf16[112,512]{1,0:T(8,128)(2,1)} %copy-done.7, ...), custom_call_target="tpu_custom_call" | custom-call | tf_op jit(solution)/shard_map/pallas_call | solution.py:255
  100.5 0.0 all-gather.3.cloned.1.call-update
  100.5 70.1 %all-gather.3.cloned.1.call-done = bf16[12288,512]{1,0:T(8,128)(2,1)} async-done(((bf16[768,512]{1,0:T(8,128)(2,1)}), bf16[12288,512]{1,0:T(8,128)(2,1)}) %all-gather.3.cloned.1.call-update) | async-done | bytes 12582928 | tf_op jit(solution)/shard_map/all_gather | solution.py:271
  170.6 77.3 %shard_map.110 = f32[4,12,8,512]{3,2,1,0:T(8,128)} custom-call(s32[1]{0:T(128)} %bitcast.group_ref, s32[24,3]{1,0:T(8,128)} %copy.13.species_ref, f32[24]{0:T(128)} %rate_ref.3, f32[12]{0:T(128)} %speed_ref.3, bf16[16,768,512]{2,1,0:T(8,128)(2,1)} %bitcast.13, bf16[16,768,512]{2,1,0:T(8,128)(2,1)} %bitcast.14, ...), custom_call_target="tpu_custom_call" | custom-call | tf_op jit(solution)/shard_map/pallas_call | solution.py:273
  (9 shorter events, 0.0 us)
Async XLA Ops:
  6.5 164.0 %all-gather.3.cloned.1.call-start = ((), (), s32[]{:S(2)}) async-start(), calls=%async_computation | async-start | bytes 13369344 | tf_op jit(solution)/shard_map/all_gather | solution.py:271
  8.2 14.6 %collective-permute-start.7 = (bf16[112,512]{1,0:T(8,128)(2,1)S(1)}, bf16[112,512]{1,0:T(8,128)(2,1)S(1)}, u32[]{:S(2)}, u32[]{:S(2)}) collective-permute-start(bf16[112,512]{1,0:T(8,128)(2,1)S(1)} %fusion.2), channel_id=1, source_target_pairs={{0,13},{1,14},{2,15},{3,8},{4,9},{5,10},{6,11},{7,12},{8,21},{9,22... | collective-permute-start | bytes 344072 | tf_op jit(solution)/shard_map/ppermute | solution.py:251
  16.8 7.9 %collective-permute-start.6 = (bf16[112,512]{1,0:T(8,128)(2,1)S(1)}, bf16[112,512]{1,0:T(8,128)(2,1)S(1)}, u32[]{:S(2)}, u32[]{:S(2)}) collective-permute-start(bf16[112,512]{1,0:T(8,128)(2,1)S(1)} %fusion.2), channel_id=1, source_target_pairs={{0,14},{1,15},{2,8},{3,9},{4,10},{5,11},{6,12},{7,13},{8,22},{9,23... | collective-permute-start | bytes 344072 | tf_op jit(solution)/shard_map/ppermute | solution.py:251
  17.3 8.6 %collective-permute-start.5 = (bf16[112,512]{1,0:T(8,128)(2,1)S(1)}, bf16[112,512]{1,0:T(8,128)(2,1)S(1)}, u32[]{:S(2)}, u32[]{:S(2)}) collective-permute-start(bf16[112,512]{1,0:T(8,128)(2,1)S(1)} %fusion.2), channel_id=1, source_target_pairs={{0,15},{1,8},{2,9},{3,10},{4,11},{5,12},{6,13},{7,14},{8,23},{9,16... | collective-permute-start | bytes 344072 | tf_op jit(solution)/shard_map/ppermute | solution.py:251
  17.6 14.2 %collective-permute-start.4 = (bf16[112,512]{1,0:T(8,128)(2,1)S(1)}, bf16[112,512]{1,0:T(8,128)(2,1)S(1)}, u32[]{:S(2)}, u32[]{:S(2)}) collective-permute-start(bf16[112,512]{1,0:T(8,128)(2,1)S(1)} %fusion.2), channel_id=1, source_target_pairs={{0,8},{1,9},{2,10},{3,11},{4,12},{5,13},{6,14},{7,15},{8,16},{9,17... | collective-permute-start | bytes 344072 | tf_op jit(solution)/shard_map/ppermute | solution.py:251
  19.1 12.7 %collective-permute-start.3 = (bf16[112,512]{1,0:T(8,128)(2,1)S(1)}, bf16[112,512]{1,0:T(8,128)(2,1)S(1)}, u32[]{:S(2)}, u32[]{:S(2)}) collective-permute-start(bf16[112,512]{1,0:T(8,128)(2,1)S(1)} %fusion.2), channel_id=1, source_target_pairs={{0,9},{1,10},{2,11},{3,12},{4,13},{5,14},{6,15},{7,8},{8,17},{9,18... | collective-permute-start | bytes 344072 | tf_op jit(solution)/shard_map/ppermute | solution.py:251
  22.8 12.9 %copy-start = (bf16[112,512]{1,0:T(8,128)(2,1)}, bf16[112,512]{1,0:T(8,128)(2,1)S(1)}, u32[]{:S(2)}) copy-start(bf16[112,512]{1,0:T(8,128)(2,1)S(1)} %collective-permute-done.7.refs_7_) | copy-start | bytes 344068
  22.8 9.0 %collective-permute-start.2 = (bf16[112,512]{1,0:T(8,128)(2,1)S(1)}, bf16[112,512]{1,0:T(8,128)(2,1)S(1)}, u32[]{:S(2)}, u32[]{:S(2)}) collective-permute-start(bf16[112,512]{1,0:T(8,128)(2,1)S(1)} %fusion.2), channel_id=1, source_target_pairs={{0,10},{1,11},{2,12},{3,13},{4,14},{5,15},{6,8},{7,9},{8,18},{9,19... | collective-permute-start | bytes 344072 | tf_op jit(solution)/shard_map/ppermute | solution.py:251
  24.7 11.0 %copy-start.1 = (bf16[112,512]{1,0:T(8,128)(2,1)}, bf16[112,512]{1,0:T(8,128)(2,1)S(1)}, u32[]{:S(2)}) copy-start(bf16[112,512]{1,0:T(8,128)(2,1)S(1)} %collective-permute-done.6.refs_6_) | copy-start | bytes 344068
  24.7 10.9 %collective-permute-start.1 = (bf16[112,512]{1,0:T(8,128)(2,1)S(1)}, bf16[112,512]{1,0:T(8,128)(2,1)S(1)}, u32[]{:S(2)}, u32[]{:S(2)}) collective-permute-start(bf16[112,512]{1,0:T(8,128)(2,1)S(1)} %fusion.2), channel_id=1, source_target_pairs={{0,11},{1,12},{2,13},{3,14},{4,15},{5,8},{6,9},{7,10},{8,19},{9,20... | collective-permute-start | bytes 344072 | tf_op jit(solution)/shard_map/ppermute | solution.py:251
  25.9 9.8 %copy-start.2 = (bf16[112,512]{1,0:T(8,128)(2,1)}, bf16[112,512]{1,0:T(8,128)(2,1)S(1)}, u32[]{:S(2)}) copy-start(bf16[112,512]{1,0:T(8,128)(2,1)S(1)} %collective-permute-done.5.refs_5_) | copy-start | bytes 344068
  25.9 9.8 %collective-permute-start = (bf16[112,512]{1,0:T(8,128)(2,1)S(1)}, bf16[112,512]{1,0:T(8,128)(2,1)S(1)}, u32[]{:S(2)}, u32[]{:S(2)}) collective-permute-start(bf16[112,512]{1,0:T(8,128)(2,1)S(1)} %fusion.2), channel_id=1, source_target_pairs={{0,12},{1,13},{2,14},{3,15},{4,8},{5,9},{6,10},{7,11},{8,20},{9,21... | collective-permute-start | bytes 344072 | tf_op jit(solution)/shard_map/ppermute | solution.py:251
  31.8 3.9 %copy-start.3 = (bf16[112,512]{1,0:T(8,128)(2,1)}, bf16[112,512]{1,0:T(8,128)(2,1)S(1)}, u32[]{:S(2)}) copy-start(bf16[112,512]{1,0:T(8,128)(2,1)S(1)} %collective-permute-done.4.refs_4_) | copy-start | bytes 344068
  31.8 3.9 %copy-start.4 = (bf16[112,512]{1,0:T(8,128)(2,1)}, bf16[112,512]{1,0:T(8,128)(2,1)S(1)}, u32[]{:S(2)}) copy-start(bf16[112,512]{1,0:T(8,128)(2,1)S(1)} %collective-permute-done.3.refs_3_) | copy-start | bytes 344068
  31.9 3.9 %copy-start.5 = (bf16[112,512]{1,0:T(8,128)(2,1)}, bf16[112,512]{1,0:T(8,128)(2,1)S(1)}, u32[]{:S(2)}) copy-start(bf16[112,512]{1,0:T(8,128)(2,1)S(1)} %collective-permute-done.2.refs_2_) | copy-start | bytes 344068
  35.7 0.6 copy-start.6
  35.7 0.7 copy-start.7
Sparse Core Ops, SparseCore 0:
  100.6 69.9 all-gather.2

commit v2 on v1

v2 whole, which is shorter than its diff:
```python
import jax
import jax.numpy as jnp
import numpy as np
from jax import lax
from jax.experimental import pallas as pl
from jax.experimental.pallas import tpu as pltpu
from jax.sharding import PartitionSpec as P

SIDE = 8
NODES = 512
FACES = 384
VARS = 12
REACTIONS = 24
BLOCK = 8
BLOCKS = 8
ELEMS = 64
ROWS = VARS * ELEMS
HALF = NODES // 2
OWN = 4
STRIDE = 4
GAIN = 4.0
BF = jnp.bfloat16
F32 = jnp.float32


def swapped_face_table():
    inner = np.arange(64)
    first, second = inner // 8, inner % 8
    nodes = [
        first * 64 + second,
        first * 64 + 56 + second,
        first * 64 + second * 8,
        first * 64 + second * 8 + 7,
    ]
    table = np.zeros((NODES, 256), np.float32)
    for place, face in enumerate((1, 0, 3, 2)):
        table[nodes[face], place * 64 + inner] = 1.0
    return table


def gather_tables(code, table_ref):
    row = lax.broadcasted_iota(jnp.int32, (ELEMS, ELEMS), 0)
    column = lax.broadcasted_iota(jnp.int32, (ELEMS, ELEMS), 1)
    home = row - jnp.bitwise_and(row, 7)
    for pair in range(3):
        parts = []
        for face in (2 * pair, 2 * pair + 1):
            source = jnp.bitwise_and(home + code[:, face : face + 1] + 56, 63)
            parts.append(jnp.where(source == column, 1.0, 0.0))
        table_ref[pair] = jnp.concatenate(parts, axis=1).astype(BF)


def exchange(xj_ref, s_ref, table_ref, face_ref, speed_ref):
    lane = lax.broadcasted_iota(jnp.int32, (ELEMS, 128), 1)
    left = lane < 64
    zero = jnp.zeros((ELEMS, 128), BF)
    s_ref[:, 128:384] = jnp.dot(
        xj_ref[:, 0:NODES], face_ref[...], preferred_element_type=F32
    ).astype(BF)
    lo = xj_ref[:, 0:128]
    hi = xj_ref[:, NODES - 128 : NODES]
    s_ref[:, 0:128] = jnp.concatenate([hi[:, 64:128], lo[:, 0:64]], axis=1)
    for v in range(0, VARS, 2):
        for pair in range(3):
            lanes = slice(pair * 128, (pair + 1) * 128)
            stacks = []
            for half in range(2):
                swapped = s_ref[(v + half) * ELEMS : (v + half + 1) * ELEMS, lanes]
                stacks.append(
                    jnp.concatenate(
                        [jnp.where(left, swapped, zero), jnp.where(left, zero, swapped)], axis=0
                    )
                )
            across = jnp.dot(
                table_ref[pair], jnp.concatenate(stacks, axis=1), preferred_element_type=F32
            )
            for half in range(2):
                rows = slice((v + half) * ELEMS, (v + half + 1) * ELEMS)
                swapped = s_ref[rows, lanes]
                own = jnp.concatenate([swapped[:, 64:128], swapped[:, 0:64]], axis=1).astype(F32)
                xj_ref[rows, NODES + pair * 128 : NODES + (pair + 1) * 128] = (
                    (across[:, half * 128 : (half + 1) * 128] - own) * speed_ref[v + half]
                ).astype(BF)


def move(xj_ref, w_ref, t_ref, cut, row, rows):
    moved = jnp.dot(
        xj_ref[row : row + rows, :],
        w_ref[:, cut * HALF : (cut + 1) * HALF],
        preferred_element_type=F32,
    )
    t_ref[row // ELEMS : (row + rows) // ELEMS] = moved.reshape(rows // ELEMS, ELEMS, HALF)


def prepare(work, cut):
    t = work.t[cut][...]
    work.plus[cut][...] = t
    work.square[cut][...] = 0.5 + t * t
    work.minus[cut][...] = jnp.zeros_like(t)


def react(work, cut, reaction):
    first, second, made, scale = reaction
    t, square = work.t[cut], work.square[cut]
    rate = scale * (t[first] * t[second]) / (square[first] + square[second])
    work.plus[cut][made] += rate
    work.minus[cut][first] += rate


def result(work, cut):
    return work.plus[cut][...] - work.minus[cut][...]


def own_result(work, cut):
    rows = slice(OWN * BLOCK, (OWN + 1) * BLOCK)
    return work.plus[cut][:, rows, :] - work.minus[cut][:, rows, :]


def substep(work, reactions, finish):
    exchange(work.xj, work.s, work.table, work.face, work.speed)
    move(work.xj, work.w, work.t[0], 0, 0, ROWS)
    prepare(work, 0)
    for number, reaction in enumerate(reactions):
        react(work, 0, reaction)
        if number % 4 == 1:
            move(work.xj, work.w, work.t[1], 1, number // 4 * 128, 128)
    finish(0)
    prepare(work, 1)
    for reaction in reactions:
        react(work, 1, reaction)
    finish(1)


def reactions_of(species_ref, rate_ref, gain):
    return [
        (species_ref[r, 0], species_ref[r, 1], species_ref[r, 2], gain * rate_ref[r])
        for r in range(REACTIONS)
    ]


def half(cut):
    return slice(cut * HALF, (cut + 1) * HALF)


def keep(work):
    def finish(cut):
        work.xj[:, half(cut)] = result(work, cut).astype(BF).reshape(ROWS, HALF)

    return finish


def relax_kernel(group_ref, species_ref, rate_ref, speed_ref, *refs):
    parts = refs[:BLOCKS]
    face_ref, fine_ref, coarse_ref, lift_ref = refs[BLOCKS : BLOCKS + 4]
    send_ref, base_ref, second_ref, table_ref = refs[BLOCKS + 4 : BLOCKS + 8]
    work = Work(refs[BLOCKS + 8 : -2], table_ref, face_ref, speed_ref)
    stepped = refs[-2:]
    xj, w = work.xj, work.w
    group = group_ref[0]
    values = [part[...].astype(F32) for part in parts]
    for v in range(VARS):
        rows = jnp.concatenate([p[v * BLOCK : (v + 1) * BLOCK] for p in values], axis=0)
        xj[v * ELEMS : (v + 1) * ELEMS, 0:NODES] = rows.astype(BF)
    codes = jnp.concatenate([p[VARS * BLOCK : (VARS + 1) * BLOCK, 0:128] for p in values], axis=0)
    gather_tables(codes.astype(jnp.int32), table_ref)
    w[0:NODES, :] = fine_ref[...]
    w[NODES:, :] = lift_ref[...]
    second_ref[...] = xj[:, 0:NODES]
    reactions = reactions_of(species_ref, rate_ref, 1.0)

    def fine(index, carry):
        substep(work, reactions, keep(work))
        return carry

    lax.fori_loop(0, 8, fine, 0)

    @pl.when(group == 0)
    def _():
        xj[:, 0:NODES] = second_ref[...]

    second_ref[...] = xj[:, 0:NODES]
    w[0:NODES, :] = coarse_ref[...]

    def hold(cut):
        stepped[cut][...] = result(work, cut)

    substep(work, reactions_of(species_ref, rate_ref, GAIN), hold)
    w[0:NODES, :] = fine_ref[...]
    lax.fori_loop(0, 8, fine, 0)
    own = slice(OWN * BLOCK, (OWN + 1) * BLOCK)
    for cut in range(2):
        last = result(work, cut)
        term = last - stepped[cut][...]
        send_ref[:, half(cut)] = jnp.where(group == 1, last, term).astype(BF).reshape(ROWS, HALF)
        base_ref[:, :, half(cut)] = jnp.where(group <= 1, last[:, own], term[:, own])


def chain_kernel(group_ref, species_ref, rate_ref, speed_ref,
                 first_ref, term_ref, second_ref, base_ref, table_ref,
                 face_ref, fine_ref, coarse_ref, lift_ref, out_ref, *refs):
    work = Work(refs[:-1], table_ref, face_ref, speed_ref)
    begin = refs[-1]
    xj, w = work.xj, work.w
    group = group_ref[0]
    step = pl.program_id(0)
    index = step + 2

    @pl.when(step == 0)
    def _():
        w[0:NODES, :] = coarse_ref[...]
        w[NODES:, :] = lift_ref[...]
        xj[:, 0:NODES] = first_ref[0]
        begin[...] = second_ref[...]
        out_ref[STRIDE - 1] = base_ref[...]

    @pl.when(index == group)
    def _():
        begin[...] = xj[:, 0:NODES]

    def chained(cut):
        value = result(work, cut).reshape(ROWS, HALF) + term_ref[0, :, half(cut)].astype(F32)
        xj[:, half(cut)] = value.astype(BF)

    substep(work, reactions_of(species_ref, rate_ref, GAIN), chained)

    @pl.when(index == group)
    def _():
        for cut in range(2):
            out_ref[STRIDE - 1, :, :, half(cut)] = own_result(work, cut) + base_ref[:, :, half(cut)]

    @pl.when(step == pl.num_programs(0) - 1)
    def _():
        w[0:NODES, :] = fine_ref[...]
        xj[:, 0:NODES] = begin[...]
        reactions = reactions_of(species_ref, rate_ref, 1.0)

        def fine(index, carry):
            substep(work, reactions, keep(work))
            for cut in range(2):
                out_ref[index // 2, :, :, half(cut)] = own_result(work, cut)
            return carry

        lax.fori_loop(0, 2 * (STRIDE - 1), fine, 0)


class Work:
    def __init__(self, refs, table, face, speed):
        self.xj, self.s, self.w = refs[:3]
        self.t, self.plus, self.minus, self.square = (refs[i : i + 2] for i in (3, 5, 7, 9))
        self.table, self.face, self.speed = table, face, speed


VMEM_SPEC = pl.BlockSpec(memory_space=pltpu.VMEM)
SMEM_SPEC = pl.BlockSpec(memory_space=pltpu.SMEM)


def work_buffers():
    return [
        pltpu.VMEM((ROWS, NODES + FACES), BF),
        pltpu.VMEM((ROWS, FACES), BF),
        pltpu.VMEM((NODES + FACES, NODES), BF),
    ] + [pltpu.VMEM((VARS, ELEMS, HALF), F32)] * 8


def body(
    coarse_guess,
    initial_state,
    fine_volume,
    coarse_volume,
    lift_matrix,
    wave_speed,
    reaction_rate,
    species_map,
    neighbour_element,
    neighbour_rank,
):
    group = lax.axis_index("tm")
    groups = lax.axis_size("tm")
    start = jnp.where((group == 0) | (group == groups - 1), initial_state, coarse_guess[0])
    start = jnp.transpose(start, (1, 0, 2)).reshape(VARS * BLOCK, NODES).astype(BF)
    code = ((neighbour_rank + 1) * BLOCK + neighbour_element).astype(BF)
    code = jnp.pad(code, ((0, 8), (0, NODES - 6)))
    payload = jnp.concatenate([start, code], axis=0)
    parts = []
    for place in range(BLOCKS):
        pairs = []
        for source in range(groups):
            for block in range(BLOCKS):
                target = (source + 1) % groups
                pairs.append((source * BLOCKS + block, target * BLOCKS + (block + OWN - place) % BLOCKS))
        parts.append(lax.ppermute(payload, ("tm", "space"), pairs))
    face_table = jnp.asarray(swapped_face_table()).astype(BF)
    group_array = group.astype(jnp.int32).reshape(1)
    params = pltpu.CompilerParams(vmem_limit_bytes=56 * 1024 * 1024)
    send, base, second, table = pl.pallas_call(
        relax_kernel,
        out_shape=(
            jax.ShapeDtypeStruct((ROWS, NODES), BF),
            jax.ShapeDtypeStruct((VARS, BLOCK, NODES), F32),
            jax.ShapeDtypeStruct((ROWS, NODES), BF),
            jax.ShapeDtypeStruct((3, ELEMS, 128), BF),
        ),
        in_specs=[SMEM_SPEC] * 4 + [VMEM_SPEC] * (BLOCKS + 4),
        out_specs=(VMEM_SPEC,) * 4,
        scratch_shapes=work_buffers() + [pltpu.VMEM((VARS, ELEMS, HALF), F32)] * 2,
        compiler_params=params,
    )(
        group_array, species_map, reaction_rate, wave_speed,
        *parts, face_table, fine_volume, coarse_volume, lift_matrix,
    )
    terms = lax.all_gather(send, "tm", axis=0, tiled=False)
    full = lambda *shape: pl.BlockSpec(shape, lambda k: (0,) * len(shape))
    out = pl.pallas_call(
        chain_kernel,
        grid=(14,),
        out_shape=jax.ShapeDtypeStruct((STRIDE, VARS, BLOCK, NODES), F32),
        in_specs=[SMEM_SPEC] * 4
        + [
            pl.BlockSpec((1, ROWS, NODES), lambda k: (1, 0, 0)),
            pl.BlockSpec((1, ROWS, NODES), lambda k: (k + 2, 0, 0)),
            full(ROWS, NODES),
            full(VARS, BLOCK, NODES),
            full(3, ELEMS, 128),
            full(NODES, 256),
            full(NODES, NODES),
            full(NODES, NODES),
            full(FACES, NODES),
        ],
        out_specs=full(STRIDE, VARS, BLOCK, NODES),
        scratch_shapes=work_buffers() + [pltpu.VMEM((ROWS, NODES), BF)],
        compiler_params=params,
    )(
        group_array, species_map, reaction_rate, wave_speed,
        terms, terms, second, base, table, face_table, fine_volume, coarse_volume, lift_matrix,
    )
    return jnp.transpose(out, (0, 2, 1, 3))


def solution(mesh):
    placed = (
        P("tm", "space", None, None),
        P("space", None, None),
        P(),
        P(),
        P(),
        P(),
        P(),
        P(),
        P("space", None),
        P("space", None),
    )
    return jax.shard_map(
        body, mesh=mesh, in_specs=placed, out_specs=P("tm", "space", None, None), check_vma=False
    )
```

time: 255 us -> 223 us (0.87)
  Pallas kernels: 141 us -> 110 us
    pallas_call x1, Pallas kernels: 77.3 us -> 61 us  [body(): pl.pallas_call(chain_kernel, grid=(14,), out_shape=jax.ShapeDtypeStruct((...]
    pallas_call x1, Pallas kernels: 64.1 us -> 48.9 us  [body(): pl.pallas_call(relax_kernel, out_shape=(jax.ShapeDtypeStruct((ROWS, NODES...]
where the time goes in v2:
time: 223 us
  Pallas kernels  110 us (49%)
  waiting for transfers between devices  75.2 us (34%)
  starting transfers between devices  20.9 us (9%)
  between operations  13.5 us (6%)
    all_gather x1, waiting for transfers between devices, body(): terms = lax.all_gather(send, 'tm', axis=0, tiled=False)  70.1 us
    pallas_call x1, Pallas kernels, body(): pl.pallas_call(chain_kernel, grid=(14,), out_shape=jax.ShapeDtypeStruct((...  61 us
    pallas_call x1, Pallas kernels, body(): pl.pallas_call(relax_kernel, out_shape=(jax.ShapeDtypeStruct((ROWS, NODES...  48.9 us
    ppermute x8, starting transfers between devices, body(): parts.append(lax.ppermute(payload, ('tm', 'space'), pairs))  20.9 us
    ppermute x8, waiting for transfers between devices, body(): parts.append(lax.ppermute(payload, ('tm', 'space'), pairs))  5.14 us
  transfers between devices with their start and end apart: 9, of which 3 were waited for; matrix products, arithmetic and copies ran while one was open for 1% of the time, Pallas kernels for 0%

profile of v2, /device:TPU:1, one launch (start us, length us, event | category | flops | bytes accessed | tf_op | source)
XLA Modules:
  0.0 223.2 jit_solution(13245777625018984305)
XLA Ops:
  6.5 0.0 all-gather.3.cloned.1.call-start
  6.5 0.7 add_convert_fusion
  7.2 1.0 fusion.3
  8.2 8.6 %collective-permute-start.7 = (bf16[112,512]{1,0:T(8,128)(2,1)S(1)}, bf16[112,512]{1,0:T(8,128)(2,1)S(1)}, u32[]{:S(2)}, u32[]{:S(2)}) collective-permute-start(bf16[112,512]{1,0:T(8,128)(2,1)S(1)} %fusion.2), channel_id=1, source_target_pairs={{0,13},{1,14},{2,15},{3,8},{4,9},{5,10},{6,11},{7,12},{8,21},{9,22... | collective-permute-start | bytes 344072 | tf_op jit(solution)/shard_map/ppermute | solution.py:291
  16.8 0.5 collective-permute-start.6
  17.3 0.3 collective-permute-start.5
  17.6 1.5 collective-permute-start.4
  19.1 3.7 %collective-permute-start.3 = (bf16[112,512]{1,0:T(8,128)(2,1)S(1)}, bf16[112,512]{1,0:T(8,128)(2,1)S(1)}, u32[]{:S(2)}, u32[]{:S(2)}) collective-permute-start(bf16[112,512]{1,0:T(8,128)(2,1)S(1)} %fusion.2), channel_id=1, source_target_pairs={{0,9},{1,10},{2,11},{3,12},{4,13},{5,14},{6,15},{7,8},{8,17},{9,18... | collective-permute-start | bytes 344072 | tf_op jit(solution)/shard_map/ppermute | solution.py:291
  22.8 0.0 collective-permute-done.7.refs_7_
  22.8 0.6 collective-permute-start.2
  23.4 1.3 collective-permute-done.6.refs_6_
  24.7 1.2 collective-permute-start.1
  25.9 0.0 collective-permute-done.5.refs_5_
  25.9 4.6 %collective-permute-start = (bf16[112,512]{1,0:T(8,128)(2,1)S(1)}, bf16[112,512]{1,0:T(8,128)(2,1)S(1)}, u32[]{:S(2)}, u32[]{:S(2)}) collective-permute-start(bf16[112,512]{1,0:T(8,128)(2,1)S(1)} %fusion.2), channel_id=1, source_target_pairs={{0,12},{1,13},{2,14},{3,15},{4,8},{5,9},{6,10},{7,11},{8,20},{9,21... | collective-permute-start | bytes 344072 | tf_op jit(solution)/shard_map/ppermute | solution.py:291
  30.5 1.4 copy.13.species_ref
  31.8 0.0 collective-permute-done.4.refs_4_
  31.8 0.0 collective-permute-done.3.refs_3_
  31.8 0.0 copy-start.4
  31.9 0.0 collective-permute-done.2.refs_2_
  31.9 0.0 copy-start.5
  31.9 3.8 %collective-permute-done.1.refs_1_ = bf16[112,512]{1,0:T(8,128)(2,1)S(1)} collective-permute-done((bf16[112,512]{1,0:T(8,128)(2,1)S(1)}, bf16[112,512]{1,0:T(8,128)(2,1)S(1)}, u32[]{:S(2)}, u32[]{:S(2)}) %collective-permute-start.1) | collective-permute-done | bytes 114720 | tf_op jit(solution)/shard_map/ppermute | solution.py:291
  35.7 0.0 collective-permute-done.refs_0_
  35.7 0.0 copy-done
  35.7 0.0 copy-done.1
  35.7 0.0 copy-done.2
  35.7 0.0 copy-done.3
  35.7 0.6 copy-done.6
  36.3 0.1 copy-done.7
  36.4 48.9 %shard_map.109 = (bf16[768,512]{1,0:T(8,128)(2,1)}, f32[12,8,512]{2,1,0:T(8,128)}, bf16[768,512]{1,0:T(8,128)(2,1)}, bf16[3,64,128]{2,1,0:T(8,128)(2,1)}) custom-call(s32[1]{0:T(128)} %bitcast.group_ref, s32[24,3]{1,0:T(8,128)} %copy.13.species_ref, f32[24]{0:T(128)} %rate_ref.3, f32[12]{0:T(128)} %speed_ref.3, bf16[112,512]{1,0:T(8,128)(2,1)} %copy-done.7, ...), custom_call_target="tpu_custom_call" | custom-call | tf_op jit(solution)/shard_map/pallas_call | solution.py:295
  85.3 0.0 all-gather.3.cloned.1.call-update
  85.3 70.1 %all-gather.3.cloned.1.call-done = bf16[12288,512]{1,0:T(8,128)(2,1)} async-done(((bf16[768,512]{1,0:T(8,128)(2,1)}), bf16[12288,512]{1,0:T(8,128)(2,1)}) %all-gather.3.cloned.1.call-update) | async-done | bytes 12582928 | tf_op jit(solution)/shard_map/all_gather | solution.py:311
  155.4 61.0 %shard_map.110 = f32[4,12,8,512]{3,2,1,0:T(8,128)} custom-call(s32[1]{0:T(128)} %bitcast.group_ref, s32[24,3]{1,0:T(8,128)} %copy.13.species_ref, f32[24]{0:T(128)} %rate_ref.3, f32[12]{0:T(128)} %speed_ref.3, bf16[16,768,512]{2,1,0:T(8,128)(2,1)} %bitcast.13, bf16[16,768,512]{2,1,0:T(8,128)(2,1)} %bitcast.14, ...), custom_call_target="tpu_custom_call" | custom-call | tf_op jit(solution)/shard_map/pallas_call | solution.py:313
  (9 shorter events, 0.0 us)
Async XLA Ops:
  6.5 148.9 %all-gather.3.cloned.1.call-start = ((), (), s32[]{:S(2)}) async-start(), calls=%async_computation | async-start | bytes 13369344 | tf_op jit(solution)/shard_map/all_gather | solution.py:311
  8.2 14.6 %collective-permute-start.7 = (bf16[112,512]{1,0:T(8,128)(2,1)S(1)}, bf16[112,512]{1,0:T(8,128)(2,1)S(1)}, u32[]{:S(2)}, u32[]{:S(2)}) collective-permute-start(bf16[112,512]{1,0:T(8,128)(2,1)S(1)} %fusion.2), channel_id=1, source_target_pairs={{0,13},{1,14},{2,15},{3,8},{4,9},{5,10},{6,11},{7,12},{8,21},{9,22... | collective-permute-start | bytes 344072 | tf_op jit(solution)/shard_map/ppermute | solution.py:291
  16.8 7.9 %collective-permute-start.6 = (bf16[112,512]{1,0:T(8,128)(2,1)S(1)}, bf16[112,512]{1,0:T(8,128)(2,1)S(1)}, u32[]{:S(2)}, u32[]{:S(2)}) collective-permute-start(bf16[112,512]{1,0:T(8,128)(2,1)S(1)} %fusion.2), channel_id=1, source_target_pairs={{0,14},{1,15},{2,8},{3,9},{4,10},{5,11},{6,12},{7,13},{8,22},{9,23... | collective-permute-start | bytes 344072 | tf_op jit(solution)/shard_map/ppermute | solution.py:291
  17.3 8.6 %collective-permute-start.5 = (bf16[112,512]{1,0:T(8,128)(2,1)S(1)}, bf16[112,512]{1,0:T(8,128)(2,1)S(1)}, u32[]{:S(2)}, u32[]{:S(2)}) collective-permute-start(bf16[112,512]{1,0:T(8,128)(2,1)S(1)} %fusion.2), channel_id=1, source_target_pairs={{0,15},{1,8},{2,9},{3,10},{4,11},{5,12},{6,13},{7,14},{8,23},{9,16... | collective-permute-start | bytes 344072 | tf_op jit(solution)/shard_map/ppermute | solution.py:291
  17.6 14.2 %collective-permute-start.4 = (bf16[112,512]{1,0:T(8,128)(2,1)S(1)}, bf16[112,512]{1,0:T(8,128)(2,1)S(1)}, u32[]{:S(2)}, u32[]{:S(2)}) collective-permute-start(bf16[112,512]{1,0:T(8,128)(2,1)S(1)} %fusion.2), channel_id=1, source_target_pairs={{0,8},{1,9},{2,10},{3,11},{4,12},{5,13},{6,14},{7,15},{8,16},{9,17... | collective-permute-start | bytes 344072 | tf_op jit(solution)/shard_map/ppermute | solution.py:291
  19.1 12.7 %collective-permute-start.3 = (bf16[112,512]{1,0:T(8,128)(2,1)S(1)}, bf16[112,512]{1,0:T(8,128)(2,1)S(1)}, u32[]{:S(2)}, u32[]{:S(2)}) collective-permute-start(bf16[112,512]{1,0:T(8,128)(2,1)S(1)} %fusion.2), channel_id=1, source_target_pairs={{0,9},{1,10},{2,11},{3,12},{4,13},{5,14},{6,15},{7,8},{8,17},{9,18... | collective-permute-start | bytes 344072 | tf_op jit(solution)/shard_map/ppermute | solution.py:291
  22.8 12.9 %copy-start = (bf16[112,512]{1,0:T(8,128)(2,1)}, bf16[112,512]{1,0:T(8,128)(2,1)S(1)}, u32[]{:S(2)}) copy-start(bf16[112,512]{1,0:T(8,128)(2,1)S(1)} %collective-permute-done.7.refs_7_) | copy-start | bytes 344068
  22.8 9.0 %collective-permute-start.2 = (bf16[112,512]{1,0:T(8,128)(2,1)S(1)}, bf16[112,512]{1,0:T(8,128)(2,1)S(1)}, u32[]{:S(2)}, u32[]{:S(2)}) collective-permute-start(bf16[112,512]{1,0:T(8,128)(2,1)S(1)} %fusion.2), channel_id=1, source_target_pairs={{0,10},{1,11},{2,12},{3,13},{4,14},{5,15},{6,8},{7,9},{8,18},{9,19... | collective-permute-start | bytes 344072 | tf_op jit(solution)/shard_map/ppermute | solution.py:291
  24.7 11.0 %copy-start.1 = (bf16[112,512]{1,0:T(8,128)(2,1)}, bf16[112,512]{1,0:T(8,128)(2,1)S(1)}, u32[]{:S(2)}) copy-start(bf16[112,512]{1,0:T(8,128)(2,1)S(1)} %collective-permute-done.6.refs_6_) | copy-start | bytes 344068
  24.7 10.9 %collective-permute-start.1 = (bf16[112,512]{1,0:T(8,128)(2,1)S(1)}, bf16[112,512]{1,0:T(8,128)(2,1)S(1)}, u32[]{:S(2)}, u32[]{:S(2)}) collective-permute-start(bf16[112,512]{1,0:T(8,128)(2,1)S(1)} %fusion.2), channel_id=1, source_target_pairs={{0,11},{1,12},{2,13},{3,14},{4,15},{5,8},{6,9},{7,10},{8,19},{9,20... | collective-permute-start | bytes 344072 | tf_op jit(solution)/shard_map/ppermute | solution.py:291
  25.9 9.8 %copy-start.2 = (bf16[112,512]{1,0:T(8,128)(2,1)}, bf16[112,512]{1,0:T(8,128)(2,1)S(1)}, u32[]{:S(2)}) copy-start(bf16[112,512]{1,0:T(8,128)(2,1)S(1)} %collective-permute-done.5.refs_5_) | copy-start | bytes 344068
  25.9 9.8 %collective-permute-start = (bf16[112,512]{1,0:T(8,128)(2,1)S(1)}, bf16[112,512]{1,0:T(8,128)(2,1)S(1)}, u32[]{:S(2)}, u32[]{:S(2)}) collective-permute-start(bf16[112,512]{1,0:T(8,128)(2,1)S(1)} %fusion.2), channel_id=1, source_target_pairs={{0,12},{1,13},{2,14},{3,15},{4,8},{5,9},{6,10},{7,11},{8,20},{9,21... | collective-permute-start | bytes 344072 | tf_op jit(solution)/shard_map/ppermute | solution.py:291
  31.8 3.9 %copy-start.3 = (bf16[112,512]{1,0:T(8,128)(2,1)}, bf16[112,512]{1,0:T(8,128)(2,1)S(1)}, u32[]{:S(2)}) copy-start(bf16[112,512]{1,0:T(8,128)(2,1)S(1)} %collective-permute-done.4.refs_4_) | copy-start | bytes 344068
  31.8 3.9 %copy-start.4 = (bf16[112,512]{1,0:T(8,128)(2,1)}, bf16[112,512]{1,0:T(8,128)(2,1)S(1)}, u32[]{:S(2)}) copy-start(bf16[112,512]{1,0:T(8,128)(2,1)S(1)} %collective-permute-done.3.refs_3_) | copy-start | bytes 344068
  31.9 3.9 %copy-start.5 = (bf16[112,512]{1,0:T(8,128)(2,1)}, bf16[112,512]{1,0:T(8,128)(2,1)S(1)}, u32[]{:S(2)}) copy-start(bf16[112,512]{1,0:T(8,128)(2,1)S(1)} %collective-permute-done.2.refs_2_) | copy-start | bytes 344068
  35.7 0.6 copy-start.6
  35.7 0.7 copy-start.7
Sparse Core Ops, SparseCore 0:
  85.4 69.9 all-gather.2

commit v3 on v2

--- a/solution.py
+++ b/solution.py
@@ -16,6 +16,7 @@
 ELEMS = 64
 ROWS = VARS * ELEMS
 HALF = NODES // 2
+PAYLOAD = 112
 OWN = 4
 STRIDE = 4
 GAIN = 4.0
@@ -50,7 +51,7 @@
         table_ref[pair] = jnp.concatenate(parts, axis=1).astype(BF)
 
 
-def exchange(xj_ref, s_ref, table_ref, face_ref, speed_ref):
+def exchange(xj_ref, s_ref, table_ref, face_ref, speed_ref, low, high):
     lane = lax.broadcasted_iota(jnp.int32, (ELEMS, 128), 1)
     left = lane < 64
     zero = jnp.zeros((ELEMS, 128), BF)
@@ -72,10 +73,10 @@
                     )
                 )
             across = jnp.dot(
-                table_ref[pair], jnp.concatenate(stacks, axis=1), preferred_element_type=F32
+                table_ref[pair, low:high], jnp.concatenate(stacks, axis=1), preferred_element_type=F32
             )
             for half in range(2):
-                rows = slice((v + half) * ELEMS, (v + half + 1) * ELEMS)
+                rows = slice((v + half) * ELEMS + low, (v + half) * ELEMS + high)
                 swapped = s_ref[rows, lanes]
                 own = jnp.concatenate([swapped[:, 64:128], swapped[:, 0:64]], axis=1).astype(F32)
                 xj_ref[rows, NODES + pair * 128 : NODES + (pair + 1) * 128] = (
@@ -92,43 +93,66 @@
     t_ref[row // ELEMS : (row + rows) // ELEMS] = moved.reshape(rows // ELEMS, ELEMS, HALF)
 
 
-def prepare(work, cut):
-    t = work.t[cut][...]
-    work.plus[cut][...] = t
-    work.square[cut][...] = 0.5 + t * t
-    work.minus[cut][...] = jnp.zeros_like(t)
-
-
-def react(work, cut, reaction):
+def move_some(xj_ref, w_ref, t_ref, cut, low, high):
+    rows = jnp.concatenate([xj_ref[v * ELEMS + low : v * ELEMS + high, :] for v in range(VARS)], axis=0)
+    moved = jnp.dot(
+        rows, w_ref[:, cut * HALF : (cut + 1) * HALF], preferred_element_type=F32
+    )
+    t_ref[:, low:high, :] = moved.reshape(VARS, high - low, HALF)
+
+
+def prepare(work, cut, low, high):
+    rows = slice(low, high)
+    t = work.t[cut][:, rows, :]
+    work.plus[cut][:, rows, :] = t
+    work.square[cut][:, rows, :] = 0.5 + t * t
+    work.minus[cut][:, rows, :] = jnp.zeros_like(t)
+
+
+def react(work, cut, reaction, low, high):
     first, second, made, scale = reaction
+    rows = slice(low, high)
     t, square = work.t[cut], work.square[cut]
-    rate = scale * (t[first] * t[second]) / (square[first] + square[second])
-    work.plus[cut][made] += rate
-    work.minus[cut][first] += rate
-
-
-def result(work, cut):
-    return work.plus[cut][...] - work.minus[cut][...]
+    rate = scale * (t[first, rows] * t[second, rows]) / (square[first, rows] + square[second, rows])
+    work.plus[cut][made, rows] += rate
+    work.minus[cut][first, rows] += rate
+
+
+def result(work, cut, low=0, high=ELEMS):
+    return work.plus[cut][:, low:high, :] - work.minus[cut][:, low:high, :]
 
 
 def own_result(work, cut):
-    rows = slice(OWN * BLOCK, (OWN + 1) * BLOCK)
-    return work.plus[cut][:, rows, :] - work.minus[cut][:, rows, :]
+    return result(work, cut, OWN * BLOCK, (OWN + 1) * BLOCK)
 
 
 def substep(work, reactions, finish):
-    exchange(work.xj, work.s, work.table, work.face, work.speed)
+    exchange(work.xj, work.s, work.table, work.face, work.speed, 0, ELEMS)
     move(work.xj, work.w, work.t[0], 0, 0, ROWS)
-    prepare(work, 0)
+    prepare(work, 0, 0, ELEMS)
     for number, reaction in enumerate(reactions):
-        react(work, 0, reaction)
+        react(work, 0, reaction, 0, ELEMS)
         if number % 4 == 1:
             move(work.xj, work.w, work.t[1], 1, number // 4 * 128, 128)
     finish(0)
-    prepare(work, 1)
+    prepare(work, 1, 0, ELEMS)
     for reaction in reactions:
-        react(work, 1, reaction)
+        react(work, 1, reaction, 0, ELEMS)
     finish(1)
+
+
+def substep_some(work, reactions, low, high, store):
+    exchange(work.xj, work.s, work.table, work.face, work.speed, low, high)
+    for cut in range(2):
+        move_some(work.xj, work.w, work.t[cut], cut, low, high)
+    for cut in range(2):
+        prepare(work, cut, low, high)
+        for reaction in reactions:
+            react(work, cut, reaction, low, high)
+        if store:
+            value = result(work, cut, low, high).astype(BF)
+            for v in range(VARS):
+                work.xj[v * ELEMS + low : v * ELEMS + high, half(cut)] = value[v]
 
 
 def reactions_of(species_ref, rate_ref, gain):
@@ -150,14 +174,19 @@
 
 
 def relax_kernel(group_ref, species_ref, rate_ref, speed_ref, *refs):
-    parts = refs[:BLOCKS]
-    face_ref, fine_ref, coarse_ref, lift_ref = refs[BLOCKS : BLOCKS + 4]
-    send_ref, base_ref, second_ref, table_ref = refs[BLOCKS + 4 : BLOCKS + 8]
-    work = Work(refs[BLOCKS + 8 : -2], table_ref, face_ref, speed_ref)
+    pairs = refs[:4]
+    face_ref, fine_ref, coarse_ref, lift_ref = refs[4:8]
+    send_ref, base_ref, second_ref, table_ref = refs[8:12]
+    work = Work(refs[12:-2], table_ref, face_ref, speed_ref)
     stepped = refs[-2:]
     xj, w = work.xj, work.w
     group = group_ref[0]
-    values = [part[...].astype(F32) for part in parts]
+    even = group_ref[1] == 0
+    near = [pair[0:PAYLOAD].astype(F32) for pair in pairs]
+    far = [pair[PAYLOAD:].astype(F32) for pair in pairs]
+    values = []
+    for k in range(4):
+        values += [near[k], jnp.where(even, far[k], far[(k + 1) % 4])]
     for v in range(VARS):
         rows = jnp.concatenate([p[v * BLOCK : (v + 1) * BLOCK] for p in values], axis=0)
         xj[v * ELEMS : (v + 1) * ELEMS, 0:NODES] = rows.astype(BF)
@@ -230,17 +259,37 @@
 
     @pl.when(step == pl.num_programs(0) - 1)
     def _():
+        @pl.when(group == index + 1)
+        def _():
+            begin[...] = xj[:, 0:NODES]
+            substep_some(work, reactions_of(species_ref, rate_ref, GAIN), 32, 48, False)
+            for cut in range(2):
+                out_ref[STRIDE - 1, :, :, half(cut)] = (
+                    own_result(work, cut) + base_ref[:, :, half(cut)]
+                )
+
         w[0:NODES, :] = fine_ref[...]
         xj[:, 0:NODES] = begin[...]
         reactions = reactions_of(species_ref, rate_ref, 1.0)
 
-        def fine(index, carry):
+        def fine(number, carry):
             substep(work, reactions, keep(work))
-            for cut in range(2):
-                out_ref[index // 2, :, :, half(cut)] = own_result(work, cut)
+
+            @pl.when(number == 1)
+            def _():
+                for cut in range(2):
+                    out_ref[0, :, :, half(cut)] = own_result(work, cut)
+
             return carry
 
-        lax.fori_loop(0, 2 * (STRIDE - 1), fine, 0)
+        lax.fori_loop(0, 3, fine, 0)
+        substep_some(work, reactions, 16, 64, True)
+        for cut in range(2):
+            out_ref[1, :, :, half(cut)] = own_result(work, cut)
+        substep_some(work, reactions, 16, 48, True)
+        substep_some(work, reactions, 32, 48, False)
+        for cut in range(2):
+            out_ref[2, :, :, half(cut)] = own_result(work, cut)
 
 
 class Work:
@@ -281,16 +330,25 @@
     code = ((neighbour_rank + 1) * BLOCK + neighbour_element).astype(BF)
     code = jnp.pad(code, ((0, 8), (0, NODES - 6)))
     payload = jnp.concatenate([start, code], axis=0)
-    parts = []
-    for place in range(BLOCKS):
+    def sent(array, place):
         pairs = []
         for source in range(groups):
             for block in range(BLOCKS):
-                target = (source + 1) % groups
-                pairs.append((source * BLOCKS + block, target * BLOCKS + (block + OWN - place) % BLOCKS))
-        parts.append(lax.ppermute(payload, ("tm", "space"), pairs))
+                target, there = place(source, block)
+                pairs.append((source * BLOCKS + block, target % groups * BLOCKS + there % BLOCKS))
+        return lax.ppermute(array, ("tm", "space"), pairs)
+
+    near = sent(payload, lambda i, s: (i + 1, s))
+    far = sent(payload, lambda i, s: (i + 1, s ^ 1))
+    here = jnp.concatenate([near, far], axis=0)
+    parts = [
+        sent(here, lambda i, s: (i, s + 4)),
+        sent(here, lambda i, s: (i, s + 2)),
+        here,
+        sent(here, lambda i, s: (i, s - 2)),
+    ]
     face_table = jnp.asarray(swapped_face_table()).astype(BF)
-    group_array = group.astype(jnp.int32).reshape(1)
+    group_array = jnp.stack([group, lax.axis_index("space") % 2]).astype(jnp.int32)
     params = pltpu.CompilerParams(vmem_limit_bytes=56 * 1024 * 1024)
     send, base, second, table = pl.pallas_call(
         relax_kernel,
@@ -300,7 +358,7 @@
             jax.ShapeDtypeStruct((ROWS, NODES), BF),
             jax.ShapeDtypeStruct((3, ELEMS, 128), BF),
         ),
-        in_specs=[SMEM_SPEC] * 4 + [VMEM_SPEC] * (BLOCKS + 4),
+        in_specs=[SMEM_SPEC] * 4 + [VMEM_SPEC] * 8,
         out_specs=(VMEM_SPEC,) * 4,
         scratch_shapes=work_buffers() + [pltpu.VMEM((VARS, ELEMS, HALF), F32)] * 2,
         compiler_params=params,
@@ -312,7 +370,7 @@
     full = lambda *shape: pl.BlockSpec(shape, lambda k: (0,) * len(shape))
     out = pl.pallas_call(
         chain_kernel,
-        grid=(14,),
+        grid=(13,),
         out_shape=jax.ShapeDtypeStruct((STRIDE, VARS, BLOCK, NODES), F32),
         in_specs=[SMEM_SPEC] * 4
         + [

time: 223 us -> 218 us (0.978)
  starting transfers between devices: 20.9 us -> 10.5 us
  waiting for transfers between devices: 75.2 us -> 84.8 us
  Pallas kernels: 110 us -> 104 us
    ppermute x8 -> x5, starting transfers between devices: 20.9 us -> 10.5 us  [sent(): return lax.ppermute(array, ('tm', 'space'), pairs)]
    all_gather x1, waiting for transfers between devices: 70.1 us -> 76.9 us  [body(): terms = lax.all_gather(send, 'tm', axis=0, tiled=False)]
    pallas_call x1, Pallas kernels: 61 us -> 55.4 us  [body(): pl.pallas_call(chain_kernel, grid=(13,), out_shape=jax.ShapeDtypeStruct((...]
    ppermute x8 -> x5, waiting for transfers between devices: 5.14 us -> 7.91 us  [sent(): return lax.ppermute(array, ('tm', 'space'), pairs)]
  transfers between devices with their start and end apart: 9 -> 6, of which waited for: 3 -> 3; matrix products, arithmetic and copies ran while one was open for 1% -> 1% of each run, Pallas kernels for 0% -> 0%
where the time goes in v3:
time: 218 us
  Pallas kernels  104 us (48%)
  waiting for transfers between devices  84.8 us (39%)
  between operations  13.4 us (6%)
  starting transfers between devices  10.5 us (5%)
  local copies, waits for them, and re-layouts  2.75 us (1%)
  other arithmetic  2.34 us (1%)
    all_gather x1, waiting for transfers between devices, body(): terms = lax.all_gather(send, 'tm', axis=0, tiled=False)  76.9 us
    pallas_call x1, Pallas kernels, body(): pl.pallas_call(chain_kernel, grid=(13,), out_shape=jax.ShapeDtypeStruct((...  55.4 us
    pallas_call x1, Pallas kernels, body(): pl.pallas_call(relax_kernel, out_shape=(jax.ShapeDtypeStruct((ROWS, NODES...  48.9 us
    ppermute x5, starting transfers between devices, sent(): return lax.ppermute(array, ('tm', 'space'), pairs)  10.5 us
    ppermute x5, waiting for transfers between devices, sent(): return lax.ppermute(array, ('tm', 'space'), pairs)  7.91 us
  transfers between devices with their start and end apart: 6, of which 3 were waited for; matrix products, arithmetic and copies ran while one was open for 1% of the time, Pallas kernels for 0%

profile of v3, /device:TPU:1, one launch (start us, length us, event | category | flops | bytes accessed | tf_op | source)
XLA Modules:
  0.0 218.1 jit_solution(8060920752183976105)
XLA Ops:
  6.5 0.0 all-gather.3.cloned.1.call-start
  6.5 0.7 add_convert_fusion
  7.2 1.0 fusion.3
  8.2 2.7 %collective-permute-start = (bf16[112,512]{1,0:T(8,128)(2,1)S(1)}, bf16[112,512]{1,0:T(8,128)(2,1)S(1)}, u32[]{:S(2)}, u32[]{:S(2)}) collective-permute-start(bf16[112,512]{1,0:T(8,128)(2,1)S(1)} %fusion.2), channel_id=1, source_target_pairs={{0,8},{1,9},{2,10},{3,11},{4,12},{5,13},{6,14},{7,15},{8,16},{9,17... | collective-permute-start | bytes 344072 | tf_op jit(solution)/shard_map/ppermute | solution.py:339
  10.9 3.4 %collective-permute-start.1 = (bf16[112,512]{1,0:T(8,128)(2,1)S(1)}, bf16[112,512]{1,0:T(8,128)(2,1)S(1)}, u32[]{:S(2)}, u32[]{:S(2)}) collective-permute-start(bf16[112,512]{1,0:T(8,128)(2,1)S(1)} %fusion.2), channel_id=1, source_target_pairs={{0,9},{1,8},{2,11},{3,10},{4,13},{5,12},{6,15},{7,14},{8,17},{9,16... | collective-permute-start | bytes 344072 | tf_op jit(solution)/shard_map/ppermute | solution.py:339
  14.3 0.0 collective-permute-done
  14.3 2.3 %collective-permute-done.1 = bf16[112,512]{1,0:T(8,128)(2,1)S(1)} collective-permute-done((bf16[112,512]{1,0:T(8,128)(2,1)S(1)}, bf16[112,512]{1,0:T(8,128)(2,1)S(1)}, u32[]{:S(2)}, u32[]{:S(2)}) %collective-permute-start.1) | collective-permute-done | bytes 114720 | tf_op jit(solution)/shard_map/ppermute | solution.py:339
  16.6 0.0 copy-start
  16.6 2.8 %collective-permute-start.4 = (bf16[224,512]{1,0:T(8,128)(2,1)S(1)}, bf16[224,512]{1,0:T(8,128)(2,1)S(1)}, u32[]{:S(2)}, u32[]{:S(2)}) collective-permute-start(bf16[224,512]{1,0:T(8,128)(2,1)S(1)} %constant_dynamic-update-slice_fusion.refs_2_), channel_id=1, source_target_pairs={{0,6},{1,7},{2,0},{3,1},{4,2},{5,3},{6,4},{7,5},{8,14},{9,15},{10,... | collective-permute-start | bytes 688136 | tf_op jit(solution)/shard_map/ppermute | solution.py:339
  19.4 0.0 collective-permute-start.3
  19.4 1.6 collective-permute-start.2
  21.1 1.4 copy.13.species_ref
  22.4 0.7 pad_add_fusion.group_ref
  23.1 0.0 collective-permute-done.4.refs_3_
  23.1 0.0 copy-start.1
  23.1 5.6 %collective-permute-done.3.refs_1_ = bf16[224,512]{1,0:T(8,128)(2,1)S(1)} collective-permute-done((bf16[224,512]{1,0:T(8,128)(2,1)S(1)}, bf16[224,512]{1,0:T(8,128)(2,1)S(1)}, u32[]{:S(2)}, u32[]{:S(2)}) %collective-permute-start.3) | collective-permute-done | bytes 229408 | tf_op jit(solution)/shard_map/ppermute | solution.py:339
  28.7 0.0 copy-start.2
  28.7 0.0 collective-permute-done.2.refs_0_
  28.7 0.0 copy-done
  28.7 0.0 copy-done.1
  28.7 0.7 copy-done.2
  29.4 0.0 copy-start.3
  29.4 0.7 copy-done.3
  30.1 48.9 %shard_map.109 = (bf16[768,512]{1,0:T(8,128)(2,1)}, f32[12,8,512]{2,1,0:T(8,128)}, bf16[768,512]{1,0:T(8,128)(2,1)}, bf16[3,64,128]{2,1,0:T(8,128)(2,1)}) custom-call(s32[2]{0:T(128)} %pad_add_fusion.group_ref, s32[24,3]{1,0:T(8,128)} %copy.13.species_ref, f32[24]{0:T(128)} %rate_ref.3, f32[12]{0:T(128)} %speed_ref.3, bf16[224,512]{1,0:T(8,128)(2,1)} %copy-done.3, ...), custom_call_target="tpu_custom_call" | custom-call | tf_op jit(solution)/shard_map/pallas_call | solution.py:353
  79.0 0.0 all-gather.3.cloned.1.call-update
  79.0 76.9 %all-gather.3.cloned.1.call-done = bf16[12288,512]{1,0:T(8,128)(2,1)} async-done(((bf16[768,512]{1,0:T(8,128)(2,1)}), bf16[12288,512]{1,0:T(8,128)(2,1)}) %all-gather.3.cloned.1.call-update) | async-done | bytes 12582928 | tf_op jit(solution)/shard_map/all_gather | solution.py:369
  155.9 55.4 %shard_map.110 = f32[4,12,8,512]{3,2,1,0:T(8,128)} custom-call(s32[2]{0:T(128)} %pad_add_fusion.group_ref, s32[24,3]{1,0:T(8,128)} %copy.13.species_ref, f32[24]{0:T(128)} %rate_ref.3, f32[12]{0:T(128)} %speed_ref.3, bf16[16,768,512]{2,1,0:T(8,128)(2,1)} %bitcast.14, bf16[16,768,512]{2,1,0:T(8,128)(2,1)} %bitcast.15, ...), custom_call_target="tpu_custom_call" | custom-call | tf_op jit(solution)/shard_map/pallas_call | solution.py:371
  (3 shorter events, 0.0 us)
Async XLA Ops:
  6.5 149.4 %all-gather.3.cloned.1.call-start = ((), (), s32[]{:S(2)}) async-start(), calls=%async_computation | async-start | bytes 13369344 | tf_op jit(solution)/shard_map/all_gather | solution.py:369
  8.2 6.1 %collective-permute-start = (bf16[112,512]{1,0:T(8,128)(2,1)S(1)}, bf16[112,512]{1,0:T(8,128)(2,1)S(1)}, u32[]{:S(2)}, u32[]{:S(2)}) collective-permute-start(bf16[112,512]{1,0:T(8,128)(2,1)S(1)} %fusion.2), channel_id=1, source_target_pairs={{0,8},{1,9},{2,10},{3,11},{4,12},{5,13},{6,14},{7,15},{8,16},{9,17... | collective-permute-start | bytes 344072 | tf_op jit(solution)/shard_map/ppermute | solution.py:339
  10.9 5.7 %collective-permute-start.1 = (bf16[112,512]{1,0:T(8,128)(2,1)S(1)}, bf16[112,512]{1,0:T(8,128)(2,1)S(1)}, u32[]{:S(2)}, u32[]{:S(2)}) collective-permute-start(bf16[112,512]{1,0:T(8,128)(2,1)S(1)} %fusion.2), channel_id=1, source_target_pairs={{0,9},{1,8},{2,11},{3,10},{4,13},{5,12},{6,15},{7,14},{8,17},{9,16... | collective-permute-start | bytes 344072 | tf_op jit(solution)/shard_map/ppermute | solution.py:339
  16.6 12.1 %copy-start = (bf16[224,512]{1,0:T(8,128)(2,1)}, bf16[224,512]{1,0:T(8,128)(2,1)S(1)}, u32[]{:S(2)}) copy-start(bf16[224,512]{1,0:T(8,128)(2,1)S(1)} %constant_dynamic-update-slice_fusion.refs_2_) | copy-start | bytes 688132
  16.6 6.5 %collective-permute-start.4 = (bf16[224,512]{1,0:T(8,128)(2,1)S(1)}, bf16[224,512]{1,0:T(8,128)(2,1)S(1)}, u32[]{:S(2)}, u32[]{:S(2)}) collective-permute-start(bf16[224,512]{1,0:T(8,128)(2,1)S(1)} %constant_dynamic-update-slice_fusion.refs_2_), channel_id=1, source_target_pairs={{0,6},{1,7},{2,0},{3,1},{4,2},{5,3},{6,4},{7,5},{8,14},{9,15},{10,... | collective-permute-start | bytes 688136 | tf_op jit(solution)/shard_map/ppermute | solution.py:339
  19.4 9.3 %collective-permute-start.3 = (bf16[224,512]{1,0:T(8,128)(2,1)S(1)}, bf16[224,512]{1,0:T(8,128)(2,1)S(1)}, u32[]{:S(2)}, u32[]{:S(2)}) collective-permute-start(bf16[224,512]{1,0:T(8,128)(2,1)S(1)} %constant_dynamic-update-slice_fusion.refs_2_), channel_id=1, source_target_pairs={{0,2},{1,3},{2,4},{3,5},{4,6},{5,7},{6,0},{7,1},{8,10},{9,11},{10,... | collective-permute-start | bytes 688136 | tf_op jit(solution)/shard_map/ppermute | solution.py:339
  19.4 9.3 %collective-permute-start.2 = (bf16[224,512]{1,0:T(8,128)(2,1)S(1)}, bf16[224,512]{1,0:T(8,128)(2,1)S(1)}, u32[]{:S(2)}, u32[]{:S(2)}) collective-permute-start(bf16[224,512]{1,0:T(8,128)(2,1)S(1)} %constant_dynamic-update-slice_fusion.refs_2_), channel_id=1, source_target_pairs={{0,4},{1,5},{2,6},{3,7},{4,0},{5,1},{6,2},{7,3},{8,12},{9,13},{10,... | collective-permute-start | bytes 688136 | tf_op jit(solution)/shard_map/ppermute | solution.py:339
  23.1 5.6 %copy-start.1 = (bf16[224,512]{1,0:T(8,128)(2,1)}, bf16[224,512]{1,0:T(8,128)(2,1)S(1)}, u32[]{:S(2)}) copy-start(bf16[224,512]{1,0:T(8,128)(2,1)S(1)} %collective-permute-done.4.refs_3_) | copy-start | bytes 688132
  28.7 0.7 copy-start.2
  29.4 0.7 copy-start.3
Sparse Core Ops, SparseCore 0:
  79.2 76.6 all-gather.2

commit v4 on v3

--- a/solution.py
+++ b/solution.py
@@ -17,6 +17,7 @@
 ROWS = VARS * ELEMS
 HALF = NODES // 2
 PAYLOAD = 112
+THIRD = ROWS // 3
 OWN = 4
 STRIDE = 4
 GAIN = 4.0
@@ -224,72 +225,109 @@
         base_ref[:, :, half(cut)] = jnp.where(group <= 1, last[:, own], term[:, own])
 
 
-def chain_kernel(group_ref, species_ref, rate_ref, speed_ref,
-                 first_ref, term_ref, second_ref, base_ref, table_ref,
-                 face_ref, fine_ref, coarse_ref, lift_ref, out_ref, *refs):
-    work = Work(refs[:-1], table_ref, face_ref, speed_ref)
-    begin = refs[-1]
+def chain_kernel(group_ref, species_ref, rate_ref, speed_ref, *refs):
+    terms = refs[:20]
+    second_ref, base_ref, table_ref, face_ref, fine_ref, coarse_ref, lift_ref, out_ref = refs[20:28]
+    work = Work(refs[28:-3], table_ref, face_ref, speed_ref)
+    begin, term_buffer, arrived = refs[-3:]
     xj, w = work.xj, work.w
     group = group_ref[0]
-    step = pl.program_id(0)
-    index = step + 2
-
-    @pl.when(step == 0)
-    def _():
-        w[0:NODES, :] = coarse_ref[...]
-        w[NODES:, :] = lift_ref[...]
-        xj[:, 0:NODES] = first_ref[0]
-        begin[...] = second_ref[...]
-        out_ref[STRIDE - 1] = base_ref[...]
-
-    @pl.when(index == group)
-    def _():
-        begin[...] = xj[:, 0:NODES]
-
-    def chained(cut):
-        value = result(work, cut).reshape(ROWS, HALF) + term_ref[0, :, half(cut)].astype(F32)
-        xj[:, half(cut)] = value.astype(BF)
-
-    substep(work, reactions_of(species_ref, rate_ref, GAIN), chained)
-
-    @pl.when(index == group)
-    def _():
-        for cut in range(2):
-            out_ref[STRIDE - 1, :, :, half(cut)] = own_result(work, cut) + base_ref[:, :, half(cut)]
-
-    @pl.when(step == pl.num_programs(0) - 1)
-    def _():
-        @pl.when(group == index + 1)
+
+    def fetch(item, slot):
+        other_z = jnp.bitwise_xor(item, group) & 8
+        distance = ((item >> 1) - (group >> 1)) & 3
+        place = other_z + 2 * distance + (jnp.bitwise_xor(item, group) & 1)
+
+        def copy(source, rows):
+            pltpu.make_async_copy(source, term_buffer.at[slot, rows], arrived.at[slot]).start()
+
+        whole = [n for n in range(16) if n not in (12, 13)]
+        for number, n in enumerate(whole):
+
+            @pl.when(place == n)
+            def _(number=number):
+                copy(terms[number], pl.ds(0, ROWS))
+
+        for n in (12, 13):
+
+            @pl.when(place == n)
+            def _(n=n):
+                for third in range(3):
+                    copy(terms[14 + third + 3 * (n - 12)], pl.ds(third * THIRD, THIRD))
+
+    def await_term(slot):
+        pltpu.make_async_copy(terms[0], term_buffer.at[slot], arrived.at[slot]).wait()
+
+    fetch(1, 1)
+    w[0:NODES, :] = coarse_ref[...]
+    w[NODES:, :] = lift_ref[...]
+    begin[...] = second_ref[...]
+    out_ref[STRIDE - 1] = base_ref[...]
+    await_term(1)
+    xj[:, 0:NODES] = term_buffer[1]
+    fetch(2, 0)
+    coarse_reactions = reactions_of(species_ref, rate_ref, GAIN)
+
+    def chain(index, carry):
+        slot = index & 1
+        await_term(slot)
+
+        @pl.when(index < 14)
+        def _():
+            fetch(index + 1, 1 - slot)
+
+        @pl.when(index == group)
         def _():
             begin[...] = xj[:, 0:NODES]
-            substep_some(work, reactions_of(species_ref, rate_ref, GAIN), 32, 48, False)
+
+        def chained(cut):
+            term = term_buffer[slot, :, half(cut)].astype(F32)
+            xj[:, half(cut)] = (result(work, cut).reshape(ROWS, HALF) + term).astype(BF)
+
+        substep(work, coarse_reactions, chained)
+
+        @pl.when(index == group)
+        def _():
             for cut in range(2):
                 out_ref[STRIDE - 1, :, :, half(cut)] = (
                     own_result(work, cut) + base_ref[:, :, half(cut)]
                 )
 
-        w[0:NODES, :] = fine_ref[...]
-        xj[:, 0:NODES] = begin[...]
-        reactions = reactions_of(species_ref, rate_ref, 1.0)
-
-        def fine(number, carry):
-            substep(work, reactions, keep(work))
-
-            @pl.when(number == 1)
-            def _():
-                for cut in range(2):
-                    out_ref[0, :, :, half(cut)] = own_result(work, cut)
-
-            return carry
-
-        lax.fori_loop(0, 3, fine, 0)
-        substep_some(work, reactions, 16, 64, True)
+        return carry
+
+    lax.fori_loop(2, 15, chain, 0)
+
+    @pl.when(group == 15)
+    def _():
+        begin[...] = xj[:, 0:NODES]
+        substep_some(work, coarse_reactions, 32, 48, False)
         for cut in range(2):
-            out_ref[1, :, :, half(cut)] = own_result(work, cut)
-        substep_some(work, reactions, 16, 48, True)
-        substep_some(work, reactions, 32, 48, False)
-        for cut in range(2):
-            out_ref[2, :, :, half(cut)] = own_result(work, cut)
+            out_ref[STRIDE - 1, :, :, half(cut)] = (
+                own_result(work, cut) + base_ref[:, :, half(cut)]
+            )
+
+    w[0:NODES, :] = fine_ref[...]
+    xj[:, 0:NODES] = begin[...]
+    reactions = reactions_of(species_ref, rate_ref, 1.0)
+
+    def fine(number, carry):
+        substep(work, reactions, keep(work))
+
+        @pl.when(number == 1)
+        def _():
+            for cut in range(2):
+                out_ref[0, :, :, half(cut)] = own_result(work, cut)
+
+        return carry
+
+    lax.fori_loop(0, 3, fine, 0)
+    substep_some(work, reactions, 16, 64, True)
+    for cut in range(2):
+        out_ref[1, :, :, half(cut)] = own_result(work, cut)
+    substep_some(work, reactions, 16, 48, True)
+    substep_some(work, reactions, 32, 48, False)
+    for cut in range(2):
+        out_ref[2, :, :, half(cut)] = own_result(work, cut)
 
 
 class Work:
@@ -366,30 +404,48 @@
         group_array, species_map, reaction_rate, wave_speed,
         *parts, face_table, fine_volume, coarse_volume, lift_matrix,
     )
-    terms = lax.all_gather(send, "tm", axis=0, tiled=False)
-    full = lambda *shape: pl.BlockSpec(shape, lambda k: (0,) * len(shape))
+
+    def over(array, other_z, along_x, other_core):
+        def place(i, s):
+            z, x, core = i // 8, i // 2 % 4, i % 2
+            return (z ^ other_z) * 8 + (x + along_x) % 4 * 2 + (core ^ other_core), s
+
+        return sent(array, place)
+
+    low, middle, high = (slice(k * THIRD, (k + 1) * THIRD) for k in range(3))
+    below, above, across = over(send, 0, 1, 0), over(send, 0, -1, 0), over(send, 1, 0, 0)
+    send_pair = over(send, 0, 0, 1)
+    far_x, across_above, across_below = over(below, 0, 1, 0), over(across, 0, -1, 0), over(below, 1, 0, 0)
+    below_pair, above_pair, across_pair = (over(item, 0, 0, 1) for item in (below, above, across))
+    last = [
+        over(across_above[low], 0, -1, 0),
+        over(across_below[middle], 0, 1, 0),
+        over(far_x[high], 1, 0, 0),
+    ]
+    far_pair, across_above_pair, across_below_pair = (
+        over(item, 0, 0, 1) for item in (far_x, across_above, across_below)
+    )
+    last_pair = [over(item, 0, 0, 1) for item in last]
+    terms = [
+        send, send_pair, above, above_pair, far_x, far_pair, below, below_pair,
+        across, across_pair, across_above, across_above_pair, across_below, across_below_pair,
+        *last, *last_pair,
+    ]
     out = pl.pallas_call(
         chain_kernel,
-        grid=(13,),
         out_shape=jax.ShapeDtypeStruct((STRIDE, VARS, BLOCK, NODES), F32),
-        in_specs=[SMEM_SPEC] * 4
+        in_specs=[SMEM_SPEC] * 4 + [pl.BlockSpec(memory_space=pl.ANY)] * 20 + [VMEM_SPEC] * 7,
+        out_specs=VMEM_SPEC,
+        scratch_shapes=work_buffers()
         + [
-            pl.BlockSpec((1, ROWS, NODES), lambda k: (1, 0, 0)),
-            pl.BlockSpec((1, ROWS, NODES), lambda k: (k + 2, 0, 0)),
-            full(ROWS, NODES),
-            full(VARS, BLOCK, NODES),
-            full(3, ELEMS, 128),
-            full(NODES, 256),
-            full(NODES, NODES),
-            full(NODES, NODES),
-            full(FACES, NODES),
+            pltpu.VMEM((ROWS, NODES), BF),
+            pltpu.VMEM((2, ROWS, NODES), BF),
+            pltpu.SemaphoreType.DMA((2,)),
         ],
-        out_specs=full(STRIDE, VARS, BLOCK, NODES),
-        scratch_shapes=work_buffers() + [pltpu.VMEM((ROWS, NODES), BF)],
         compiler_params=params,
     )(
         group_array, species_map, reaction_rate, wave_speed,
-        terms, terms, second, base, table, face_table, fine_volume, coarse_volume, lift_matrix,
+        *terms, second, base, table, face_table, fine_volume, coarse_volume, lift_matrix,
     )
     return jnp.transpose(out, (0, 2, 1, 3))
 

time: 218 us -> 209 us (0.959)
  starting transfers between devices: 10.5 us -> 41.2 us
  waiting for transfers between devices: 84.8 us -> 54.2 us
  between operations: 13.4 us -> 0.42 us
  local copies, waits for them, and re-layouts: 2.75 us -> 5.38 us
    all_gather x1 -> x0, waiting for transfers between devices: 76.9 us -> none  [body(): terms = lax.all_gather(send, 'tm', axis=0, tiled=False)]
    ppermute x5 -> x24, waiting for transfers between devices: 7.91 us -> 54.2 us  [sent(): return lax.ppermute(array, ('tm', 'space'), pairs)]
    ppermute x5 -> x24, starting transfers between devices: 10.5 us -> 41.2 us  [sent(): return lax.ppermute(array, ('tm', 'space'), pairs)]
    unnamed x10 -> x54, local copies, waits for them, and re-layouts: 2.74 us -> 5.32 us
  transfers between devices with their start and end apart: 6 -> 24, of which waited for: 3 -> 10; matrix products, arithmetic and copies ran while one was open for 1% -> 1% of each run, Pallas kernels for 0% -> 0%
where the time goes in v4:
time: 209 us
  Pallas kernels  106 us (51%)
  waiting for transfers between devices  54.2 us (26%)
  starting transfers between devices  41.2 us (20%)
  local copies, waits for them, and re-layouts  5.38 us (3%)
    pallas_call x1, Pallas kernels, body(): pl.pallas_call(chain_kernel, out_shape=jax.ShapeDtypeStruct((STRIDE, VARS...  56.9 us
    ppermute x24, waiting for transfers between devices, sent(): return lax.ppermute(array, ('tm', 'space'), pairs)  54.2 us
    pallas_call x1, Pallas kernels, body(): pl.pallas_call(relax_kernel, out_shape=(jax.ShapeDtypeStruct((ROWS, NODES...  48.9 us
    ppermute x24, starting transfers between devices, sent(): return lax.ppermute(array, ('tm', 'space'), pairs)  41.2 us
    unnamed x54, local copies, waits for them, and re-layouts  5.32 us
  transfers between devices with their start and end apart: 24, of which 10 were waited for; matrix products, arithmetic and copies ran while one was open for 1% of the time, Pallas kernels for 0%

profile of v4, /device:TPU:1, one launch (start us, length us, event | category | flops | bytes accessed | tf_op | source)
XLA Modules:
  0.0 208.7 jit_solution(17970772109925286822)
XLA Ops:
  0.0 0.7 copy-done.24
  0.7 1.0 fusion.3
  1.7 2.7 %collective-permute-start = (bf16[112,512]{1,0:T(8,128)(2,1)S(1)}, bf16[112,512]{1,0:T(8,128)(2,1)S(1)}, u32[]{:S(2)}, u32[]{:S(2)}) collective-permute-start(bf16[112,512]{1,0:T(8,128)(2,1)S(1)} %fusion.2), channel_id=1, source_target_pairs={{0,8},{1,9},{2,10},{3,11},{4,12},{5,13},{6,14},{7,15},{8,16},{9,17... | collective-permute-start | bytes 344072 | tf_op jit(solution)/shard_map/ppermute | solution.py:377
  4.4 3.4 %collective-permute-start.1 = (bf16[112,512]{1,0:T(8,128)(2,1)S(1)}, bf16[112,512]{1,0:T(8,128)(2,1)S(1)}, u32[]{:S(2)}, u32[]{:S(2)}) collective-permute-start(bf16[112,512]{1,0:T(8,128)(2,1)S(1)} %fusion.2), channel_id=1, source_target_pairs={{0,9},{1,8},{2,11},{3,10},{4,13},{5,12},{6,15},{7,14},{8,17},{9,16... | collective-permute-start | bytes 344072 | tf_op jit(solution)/shard_map/ppermute | solution.py:377
  7.8 2.3 %collective-permute-done.1 = bf16[112,512]{1,0:T(8,128)(2,1)S(1)} collective-permute-done((bf16[112,512]{1,0:T(8,128)(2,1)S(1)}, bf16[112,512]{1,0:T(8,128)(2,1)S(1)}, u32[]{:S(2)}, u32[]{:S(2)}) %collective-permute-start.1) | collective-permute-done | bytes 114720 | tf_op jit(solution)/shard_map/ppermute | solution.py:377
  10.1 2.8 %collective-permute-start.4 = (bf16[224,512]{1,0:T(8,128)(2,1)S(1)}, bf16[224,512]{1,0:T(8,128)(2,1)S(1)}, u32[]{:S(2)}, u32[]{:S(2)}) collective-permute-start(bf16[224,512]{1,0:T(8,128)(2,1)S(1)} %constant_dynamic-update-slice_fusion.refs_2_), channel_id=1, source_target_pairs={{0,6},{1,7},{2,0},{3,1},{4,2},{5,3},{6,4},{7,5},{8,14},{9,15},{10,... | collective-permute-start | bytes 688136 | tf_op jit(solution)/shard_map/ppermute | solution.py:377
  12.9 1.6 collective-permute-start.2
  14.6 0.7 copy-done.25
  15.2 0.7 copy.13.species_ref
  15.9 0.7 pad_add_fusion.group_ref
  16.6 5.6 %collective-permute-done.3.refs_1_ = bf16[224,512]{1,0:T(8,128)(2,1)S(1)} collective-permute-done((bf16[224,512]{1,0:T(8,128)(2,1)S(1)}, bf16[224,512]{1,0:T(8,128)(2,1)S(1)}, u32[]{:S(2)}, u32[]{:S(2)}) %collective-permute-start.3) | collective-permute-done | bytes 229408 | tf_op jit(solution)/shard_map/ppermute | solution.py:377
  22.2 0.7 copy-done.21
  22.9 0.7 copy-done.22
  23.6 48.9 %shard_map.109 = (bf16[768,512]{1,0:T(8,128)(2,1)}, f32[12,8,512]{2,1,0:T(8,128)}, bf16[768,512]{1,0:T(8,128)(2,1)}, bf16[3,64,128]{2,1,0:T(8,128)(2,1)}) custom-call(s32[2]{0:T(128)} %pad_add_fusion.group_ref, s32[24,3]{1,0:T(8,128)} %copy.13.species_ref, f32[24]{0:T(128)} %rate_ref.3, f32[12]{0:T(128)} %speed_ref.3, bf16[224,512]{1,0:T(8,128)(2,1)} %copy-done.22, ...), custom_call_target="tpu_custom_call" | custom-call | tf_op jit(solution)/shard_map/pallas_call | solution.py:391
  72.5 4.7 %collective-permute-start.12 = (bf16[768,512]{1,0:T(8,128)(2,1)}, bf16[768,512]{1,0:T(8,128)(2,1)S(1)}, u32[]{:S(2)}, u32[]{:S(2)}) collective-permute-start(bf16[768,512]{1,0:T(8,128)(2,1)} %get-tuple-element.9.refs_0_), channel_id=1, source_target_pairs={{0,64},{1,65},{2,66},{3,67},{4,68},{5,69},{6,70},{7,71},{8,72},{9,... | collective-permute-start | bytes 2359304 | tf_op jit(solution)/shard_map/ppermute | solution.py:377
  77.2 3.2 %collective-permute-start.8 = (bf16[768,512]{1,0:T(8,128)(2,1)}, bf16[768,512]{1,0:T(8,128)(2,1)S(1)}, u32[]{:S(2)}, u32[]{:S(2)}) collective-permute-start(bf16[768,512]{1,0:T(8,128)(2,1)} %get-tuple-element.9.refs_0_), channel_id=1, source_target_pairs={{0,16},{1,17},{2,18},{3,19},{4,20},{5,21},{6,22},{7,23},{8,24},{9,... | collective-permute-start | bytes 2359304 | tf_op jit(solution)/shard_map/ppermute | solution.py:377
  80.5 10.9 %collective-permute-done.12.refs_8_ = bf16[768,512]{1,0:T(8,128)(2,1)S(1)} collective-permute-done((bf16[768,512]{1,0:T(8,128)(2,1)}, bf16[768,512]{1,0:T(8,128)(2,1)S(1)}, u32[]{:S(2)}, u32[]{:S(2)}) %collective-permute-start.12) | collective-permute-done | bytes 786464 | tf_op jit(solution)/shard_map/ppermute | solution.py:377
  91.4 2.8 %collective-permute-start.14 = (bf16[768,512]{1,0:T(8,128)(2,1)S(1)}, bf16[768,512]{1,0:T(8,128)(2,1)S(1)}, u32[]{:S(2)}, u32[]{:S(2)}) collective-permute-start(bf16[768,512]{1,0:T(8,128)(2,1)S(1)} %collective-permute-done.12.refs_8_), channel_id=1, source_target_pairs={{0,48},{1,49},{2,50},{3,51},{4,52},{5,53},{6,54},{7,55},{8,56},{9,... | collective-permute-start | bytes 2359304 | tf_op jit(solution)/shard_map/ppermute | solution.py:377
  94.1 2.2 %collective-permute-done.8.refs_6_ = bf16[768,512]{1,0:T(8,128)(2,1)S(1)} collective-permute-done((bf16[768,512]{1,0:T(8,128)(2,1)}, bf16[768,512]{1,0:T(8,128)(2,1)S(1)}, u32[]{:S(2)}, u32[]{:S(2)}) %collective-permute-start.8) | collective-permute-done | bytes 786464 | tf_op jit(solution)/shard_map/ppermute | solution.py:377
  96.7 2.3 %collective-permute-start.5 = (bf16[768,512]{1,0:T(8,128)(2,1)}, bf16[768,512]{1,0:T(8,128)(2,1)S(1)}, u32[]{:S(2)}, u32[]{:S(2)}) collective-permute-start(bf16[768,512]{1,0:T(8,128)(2,1)} %get-tuple-element.9.refs_0_), channel_id=1, source_target_pairs={{0,8},{1,9},{2,10},{3,11},{4,12},{5,13},{6,14},{7,15},{8,0},{9,1},... | collective-permute-start | bytes 2359304 | tf_op jit(solution)/shard_map/ppermute | solution.py:377
  99.0 3.0 %collective-permute-start.11 = (bf16[768,512]{1,0:T(8,128)(2,1)S(1)}, bf16[768,512]{1,0:T(8,128)(2,1)S(1)}, u32[]{:S(2)}, u32[]{:S(2)}) collective-permute-start(bf16[768,512]{1,0:T(8,128)(2,1)S(1)} %collective-permute-done.8.refs_6_), channel_id=1, source_target_pairs={{0,8},{1,9},{2,10},{3,11},{4,12},{5,13},{6,14},{7,15},{8,0},{9,1},... | collective-permute-start | bytes 2359304 | tf_op jit(solution)/shard_map/ppermute | solution.py:377
  102.0 13.7 %collective-permute-done.14.refs_10_ = bf16[768,512]{1,0:T(8,128)(2,1)S(1)} collective-permute-done((bf16[768,512]{1,0:T(8,128)(2,1)S(1)}, bf16[768,512]{1,0:T(8,128)(2,1)S(1)}, u32[]{:S(2)}, u32[]{:S(2)}) %collective-permute-start.14) | collective-permute-done | bytes 786464 | tf_op jit(solution)/shard_map/ppermute | solution.py:377
  115.7 2.1 collective-permute-start.7
  117.9 2.7 %collective-permute-start.18 = (bf16[256,512]{1,0:T(8,128)(2,1)S(1)}, bf16[256,512]{1,0:T(8,128)(2,1)S(1)}, u32[]{:S(2)}, u32[]{:S(2)}) collective-permute-start(bf16[256,512]{1,0:T(8,128)(2,1)S(1)} %slice.12), channel_id=1, source_target_pairs={{0,48},{1,49},{2,50},{3,51},{4,52},{5,53},{6,54},{7,55},{8,56},{9,... | collective-permute-start | bytes 786440 | tf_op jit(solution)/shard_map/ppermute | solution.py:377
  121.0 13.2 %collective-permute-done.9.refs_4_ = bf16[768,512]{1,0:T(8,128)(2,1)S(1)} collective-permute-done((bf16[768,512]{1,0:T(8,128)(2,1)S(1)}, bf16[768,512]{1,0:T(8,128)(2,1)S(1)}, u32[]{:S(2)}, u32[]{:S(2)}) %collective-permute-start.9) | collective-permute-done | bytes 786464 | tf_op jit(solution)/shard_map/ppermute | solution.py:377
  134.2 5.0 %collective-permute-start.17 = (bf16[768,512]{1,0:T(8,128)(2,1)S(1)}, bf16[768,512]{1,0:T(8,128)(2,1)S(1)}, u32[]{:S(2)}, u32[]{:S(2)}) collective-permute-start(bf16[768,512]{1,0:T(8,128)(2,1)S(1)} %collective-permute-done.16.refs_12_), channel_id=1, source_target_pairs={{0,8},{1,9},{2,10},{3,11},{4,12},{5,13},{6,14},{7,15},{8,0},{9,1},... | collective-permute-start | bytes 2359304 | tf_op jit(solution)/shard_map/ppermute | solution.py:377
  139.8 2.7 %collective-permute-start.21 = (bf16[256,512]{1,0:T(8,128)(2,1)S(1)}, bf16[256,512]{1,0:T(8,128)(2,1)S(1)}, u32[]{:S(2)}, u32[]{:S(2)}) collective-permute-start(bf16[256,512]{1,0:T(8,128)(2,1)S(1)} %collective-permute-done.18.refs_14_), channel_id=1, source_target_pairs={{0,8},{1,9},{2,10},{3,11},{4,12},{5,13},{6,14},{7,15},{8,0},{9,1},... | collective-permute-start | bytes 786440 | tf_op jit(solution)/shard_map/ppermute | solution.py:377
  142.5 4.4 %collective-permute-done.20.refs_16_ = bf16[256,512]{1,0:T(8,128)(2,1)S(1)} collective-permute-done((bf16[256,512]{1,0:T(8,128)(2,1)S(1)}, bf16[256,512]{1,0:T(8,128)(2,1)S(1)}, u32[]{:S(2)}, u32[]{:S(2)}) %collective-permute-start.20) | collective-permute-done | bytes 262176 | tf_op jit(solution)/shard_map/ppermute | solution.py:377
  146.9 1.3 collective-permute-start.22
  148.2 1.1 collective-permute-done.22.refs_18_
  149.7 0.9 copy-done.10
  151.6 56.9 %shard_map.110 = f32[4,12,8,512]{3,2,1,0:T(8,128)} custom-call(s32[2]{0:T(128)} %pad_add_fusion.group_ref, s32[24,3]{1,0:T(8,128)} %copy.13.species_ref, f32[24]{0:T(128)} %rate_ref.3, f32[12]{0:T(128)} %speed_ref.3, bf16[768,512]{1,0:T(8,128)(2,1)} %get-tuple-element.9.refs_0_, bf16[768,512]{1,0:T(8,128)(2,1)} %copy-done.6, bf16[768,512]{1,0:T(8,128)(2,1)} %copy-done.5, ...), custom_call_target="tpu_custom_call" | custom-call | tf_op jit(solution)/shard_map/pallas_call | solution.py:434
  (80 shorter events, 2.9 us)
Async XLA Ops:
  1.7 6.1 %collective-permute-start = (bf16[112,512]{1,0:T(8,128)(2,1)S(1)}, bf16[112,512]{1,0:T(8,128)(2,1)S(1)}, u32[]{:S(2)}, u32[]{:S(2)}) collective-permute-start(bf16[112,512]{1,0:T(8,128)(2,1)S(1)} %fusion.2), channel_id=1, source_target_pairs={{0,8},{1,9},{2,10},{3,11},{4,12},{5,13},{6,14},{7,15},{8,16},{9,17... | collective-permute-start | bytes 344072 | tf_op jit(solution)/shard_map/ppermute | solution.py:377
  4.4 5.7 %collective-permute-start.1 = (bf16[112,512]{1,0:T(8,128)(2,1)S(1)}, bf16[112,512]{1,0:T(8,128)(2,1)S(1)}, u32[]{:S(2)}, u32[]{:S(2)}) collective-permute-start(bf16[112,512]{1,0:T(8,128)(2,1)S(1)} %fusion.2), channel_id=1, source_target_pairs={{0,9},{1,8},{2,11},{3,10},{4,13},{5,12},{6,15},{7,14},{8,17},{9,16... | collective-permute-start | bytes 344072 | tf_op jit(solution)/shard_map/ppermute | solution.py:377
  10.1 6.5 %collective-permute-start.4 = (bf16[224,512]{1,0:T(8,128)(2,1)S(1)}, bf16[224,512]{1,0:T(8,128)(2,1)S(1)}, u32[]{:S(2)}, u32[]{:S(2)}) collective-permute-start(bf16[224,512]{1,0:T(8,128)(2,1)S(1)} %constant_dynamic-update-slice_fusion.refs_2_), channel_id=1, source_target_pairs={{0,6},{1,7},{2,0},{3,1},{4,2},{5,3},{6,4},{7,5},{8,14},{9,15},{10,... | collective-permute-start | bytes 688136 | tf_op jit(solution)/shard_map/ppermute | solution.py:377
  12.9 9.3 %collective-permute-start.3 = (bf16[224,512]{1,0:T(8,128)(2,1)S(1)}, bf16[224,512]{1,0:T(8,128)(2,1)S(1)}, u32[]{:S(2)}, u32[]{:S(2)}) collective-permute-start(bf16[224,512]{1,0:T(8,128)(2,1)S(1)} %constant_dynamic-update-slice_fusion.refs_2_), channel_id=1, source_target_pairs={{0,2},{1,3},{2,4},{3,5},{4,6},{5,7},{6,0},{7,1},{8,10},{9,11},{10,... | collective-permute-start | bytes 688136 | tf_op jit(solution)/shard_map/ppermute | solution.py:377
  12.9 9.3 %collective-permute-start.2 = (bf16[224,512]{1,0:T(8,128)(2,1)S(1)}, bf16[224,512]{1,0:T(8,128)(2,1)S(1)}, u32[]{:S(2)}, u32[]{:S(2)}) collective-permute-start(bf16[224,512]{1,0:T(8,128)(2,1)S(1)} %constant_dynamic-update-slice_fusion.refs_2_), channel_id=1, source_target_pairs={{0,4},{1,5},{2,6},{3,7},{4,0},{5,1},{6,2},{7,3},{8,12},{9,13},{10,... | collective-permute-start | bytes 688136 | tf_op jit(solution)/shard_map/ppermute | solution.py:377
  72.5 18.9 %collective-permute-start.12 = (bf16[768,512]{1,0:T(8,128)(2,1)}, bf16[768,512]{1,0:T(8,128)(2,1)S(1)}, u32[]{:S(2)}, u32[]{:S(2)}) collective-permute-start(bf16[768,512]{1,0:T(8,128)(2,1)} %get-tuple-element.9.refs_0_), channel_id=1, source_target_pairs={{0,64},{1,65},{2,66},{3,67},{4,68},{5,69},{6,70},{7,71},{8,72},{9,... | collective-permute-start | bytes 2359304 | tf_op jit(solution)/shard_map/ppermute | solution.py:377
  77.2 19.1 %collective-permute-start.8 = (bf16[768,512]{1,0:T(8,128)(2,1)}, bf16[768,512]{1,0:T(8,128)(2,1)S(1)}, u32[]{:S(2)}, u32[]{:S(2)}) collective-permute-start(bf16[768,512]{1,0:T(8,128)(2,1)} %get-tuple-element.9.refs_0_), channel_id=1, source_target_pairs={{0,16},{1,17},{2,18},{3,19},{4,20},{5,21},{6,22},{7,23},{8,24},{9,... | collective-permute-start | bytes 2359304 | tf_op jit(solution)/shard_map/ppermute | solution.py:377
  80.5 18.5 %collective-permute-start.6 = (bf16[768,512]{1,0:T(8,128)(2,1)}, bf16[768,512]{1,0:T(8,128)(2,1)S(1)}, u32[]{:S(2)}, u32[]{:S(2)}) collective-permute-start(bf16[768,512]{1,0:T(8,128)(2,1)} %get-tuple-element.9.refs_0_), channel_id=1, source_target_pairs={{0,48},{1,49},{2,50},{3,51},{4,52},{5,53},{6,54},{7,55},{8,56},{9,... | collective-permute-start | bytes 2359304 | tf_op jit(solution)/shard_map/ppermute | solution.py:377
  91.4 60.1 %copy-start.3 = (bf16[768,512]{1,0:T(8,128)(2,1)}, bf16[768,512]{1,0:T(8,128)(2,1)S(1)}, u32[]{:S(2)}) copy-start(bf16[768,512]{1,0:T(8,128)(2,1)S(1)} %collective-permute-done.12.refs_8_) | copy-start | bytes 2359300
  91.4 24.3 %collective-permute-start.14 = (bf16[768,512]{1,0:T(8,128)(2,1)S(1)}, bf16[768,512]{1,0:T(8,128)(2,1)S(1)}, u32[]{:S(2)}, u32[]{:S(2)}) collective-permute-start(bf16[768,512]{1,0:T(8,128)(2,1)S(1)} %collective-permute-done.12.refs_8_), channel_id=1, source_target_pairs={{0,48},{1,49},{2,50},{3,51},{4,52},{5,53},{6,54},{7,55},{8,56},{9,... | collective-permute-start | bytes 2359304 | tf_op jit(solution)/shard_map/ppermute | solution.py:377
  96.3 55.2 %copy-start.4 = (bf16[768,512]{1,0:T(8,128)(2,1)}, bf16[768,512]{1,0:T(8,128)(2,1)S(1)}, u32[]{:S(2)}) copy-start(bf16[768,512]{1,0:T(8,128)(2,1)S(1)} %collective-permute-done.8.refs_6_) | copy-start | bytes 2359300
  96.3 19.4 %collective-permute-start.16 = (bf16[768,512]{1,0:T(8,128)(2,1)S(1)}, bf16[768,512]{1,0:T(8,128)(2,1)S(1)}, u32[]{:S(2)}, u32[]{:S(2)}) collective-permute-start(bf16[768,512]{1,0:T(8,128)(2,1)S(1)} %collective-permute-done.8.refs_6_), channel_id=1, source_target_pairs={{0,64},{1,65},{2,66},{3,67},{4,68},{5,69},{6,70},{7,71},{8,72},{9,... | collective-permute-start | bytes 2359304 | tf_op jit(solution)/shard_map/ppermute | solution.py:377
  96.7 21.2 %collective-permute-start.5 = (bf16[768,512]{1,0:T(8,128)(2,1)}, bf16[768,512]{1,0:T(8,128)(2,1)S(1)}, u32[]{:S(2)}, u32[]{:S(2)}) collective-permute-start(bf16[768,512]{1,0:T(8,128)(2,1)} %get-tuple-element.9.refs_0_), channel_id=1, source_target_pairs={{0,8},{1,9},{2,10},{3,11},{4,12},{5,13},{6,14},{7,15},{8,0},{9,1},... | collective-permute-start | bytes 2359304 | tf_op jit(solution)/shard_map/ppermute | solution.py:377
  99.0 21.6 %collective-permute-start.13 = (bf16[768,512]{1,0:T(8,128)(2,1)S(1)}, bf16[768,512]{1,0:T(8,128)(2,1)S(1)}, u32[]{:S(2)}, u32[]{:S(2)}) collective-permute-start(bf16[768,512]{1,0:T(8,128)(2,1)S(1)} %collective-permute-done.12.refs_8_), channel_id=1, source_target_pairs={{0,8},{1,9},{2,10},{3,11},{4,12},{5,13},{6,14},{7,15},{8,0},{9,1},... | collective-permute-start | bytes 2359304 | tf_op jit(solution)/shard_map/ppermute | solution.py:377
  99.0 52.6 %copy-start.5 = (bf16[768,512]{1,0:T(8,128)(2,1)}, bf16[768,512]{1,0:T(8,128)(2,1)S(1)}, u32[]{:S(2)}) copy-start(bf16[768,512]{1,0:T(8,128)(2,1)S(1)} %collective-permute-done.6.refs_2_) | copy-start | bytes 2359300
  99.0 21.6 %collective-permute-start.11 = (bf16[768,512]{1,0:T(8,128)(2,1)S(1)}, bf16[768,512]{1,0:T(8,128)(2,1)S(1)}, u32[]{:S(2)}, u32[]{:S(2)}) collective-permute-start(bf16[768,512]{1,0:T(8,128)(2,1)S(1)} %collective-permute-done.8.refs_6_), channel_id=1, source_target_pairs={{0,8},{1,9},{2,10},{3,11},{4,12},{5,13},{6,14},{7,15},{8,0},{9,1},... | collective-permute-start | bytes 2359304 | tf_op jit(solution)/shard_map/ppermute | solution.py:377
  115.7 23.6 %copy-start = (bf16[768,512]{1,0:T(8,128)(2,1)}, bf16[768,512]{1,0:T(8,128)(2,1)S(1)}, u32[]{:S(2)}) copy-start(bf16[768,512]{1,0:T(8,128)(2,1)S(1)} %collective-permute-done.14.refs_10_) | copy-start | bytes 2359300
  115.7 18.5 %collective-permute-start.9 = (bf16[768,512]{1,0:T(8,128)(2,1)S(1)}, bf16[768,512]{1,0:T(8,128)(2,1)S(1)}, u32[]{:S(2)}, u32[]{:S(2)}) collective-permute-start(bf16[768,512]{1,0:T(8,128)(2,1)S(1)} %collective-permute-done.8.refs_6_), channel_id=1, source_target_pairs={{0,16},{1,17},{2,18},{3,19},{4,20},{5,21},{6,22},{7,23},{8,24},{9,... | collective-permute-start | bytes 2359304 | tf_op jit(solution)/shard_map/ppermute | solution.py:377
  115.7 35.8 %copy-start.1 = (bf16[768,512]{1,0:T(8,128)(2,1)}, bf16[768,512]{1,0:T(8,128)(2,1)S(1)}, u32[]{:S(2)}) copy-start(bf16[768,512]{1,0:T(8,128)(2,1)S(1)} %collective-permute-done.16.refs_12_) | copy-start | bytes 2359300
  115.7 23.4 %collective-permute-start.7 = (bf16[768,512]{1,0:T(8,128)(2,1)S(1)}, bf16[768,512]{1,0:T(8,128)(2,1)S(1)}, u32[]{:S(2)}, u32[]{:S(2)}) collective-permute-start(bf16[768,512]{1,0:T(8,128)(2,1)S(1)} %collective-permute-done.6.refs_2_), channel_id=1, source_target_pairs={{0,8},{1,9},{2,10},{3,11},{4,12},{5,13},{6,14},{7,15},{8,0},{9,1},... | collective-permute-start | bytes 2359304 | tf_op jit(solution)/shard_map/ppermute | solution.py:377
  117.9 33.7 %copy-start.6 = (bf16[768,512]{1,0:T(8,128)(2,1)}, bf16[768,512]{1,0:T(8,128)(2,1)S(1)}, u32[]{:S(2)}) copy-start(bf16[768,512]{1,0:T(8,128)(2,1)S(1)} %collective-permute-done.5.refs_1_) | copy-start | bytes 2359300
  117.9 21.4 %collective-permute-start.18 = (bf16[256,512]{1,0:T(8,128)(2,1)S(1)}, bf16[256,512]{1,0:T(8,128)(2,1)S(1)}, u32[]{:S(2)}, u32[]{:S(2)}) collective-permute-start(bf16[256,512]{1,0:T(8,128)(2,1)S(1)} %slice.12), channel_id=1, source_target_pairs={{0,48},{1,49},{2,50},{3,51},{4,52},{5,53},{6,54},{7,55},{8,56},{9,... | collective-permute-start | bytes 786440 | tf_op jit(solution)/shard_map/ppermute | solution.py:377
  120.6 31.0 %copy-start.7 = (bf16[768,512]{1,0:T(8,128)(2,1)}, bf16[768,512]{1,0:T(8,128)(2,1)S(1)}, u32[]{:S(2)}) copy-start(bf16[768,512]{1,0:T(8,128)(2,1)S(1)} %collective-permute-done.13.refs_9_) | copy-start | bytes 2359300
  120.6 19.2 %collective-permute-start.19 = (bf16[256,512]{1,0:T(8,128)(2,1)S(1)}, bf16[256,512]{1,0:T(8,128)(2,1)S(1)}, u32[]{:S(2)}, u32[]{:S(2)}) collective-permute-start(bf16[256,512]{1,0:T(8,128)(2,1)S(1)} %slice.13), channel_id=1, source_target_pairs={{0,16},{1,17},{2,18},{3,19},{4,20},{5,21},{6,22},{7,23},{8,24},{9,... | collective-permute-start | bytes 786440 | tf_op jit(solution)/shard_map/ppermute | solution.py:377
  120.6 31.0 %copy-start.8 = (bf16[768,512]{1,0:T(8,128)(2,1)}, bf16[768,512]{1,0:T(8,128)(2,1)S(1)}, u32[]{:S(2)}) copy-start(bf16[768,512]{1,0:T(8,128)(2,1)S(1)} %collective-permute-done.11.refs_7_) | copy-start | bytes 2359300
  120.6 29.1 %collective-permute-start.15 = (bf16[768,512]{1,0:T(8,128)(2,1)S(1)}, bf16[768,512]{1,0:T(8,128)(2,1)S(1)}, u32[]{:S(2)}, u32[]{:S(2)}) collective-permute-start(bf16[768,512]{1,0:T(8,128)(2,1)S(1)} %collective-permute-done.14.refs_10_), channel_id=1, source_target_pairs={{0,8},{1,9},{2,10},{3,11},{4,12},{5,13},{6,14},{7,15},{8,0},{9,1},... | collective-permute-start | bytes 2359304 | tf_op jit(solution)/shard_map/ppermute | solution.py:377
  134.2 15.5 %collective-permute-start.17 = (bf16[768,512]{1,0:T(8,128)(2,1)S(1)}, bf16[768,512]{1,0:T(8,128)(2,1)S(1)}, u32[]{:S(2)}, u32[]{:S(2)}) collective-permute-start(bf16[768,512]{1,0:T(8,128)(2,1)S(1)} %collective-permute-done.16.refs_12_), channel_id=1, source_target_pairs={{0,8},{1,9},{2,10},{3,11},{4,12},{5,13},{6,14},{7,15},{8,0},{9,1},... | collective-permute-start | bytes 2359304 | tf_op jit(solution)/shard_map/ppermute | solution.py:377
  139.2 10.5 %collective-permute-start.10 = (bf16[768,512]{1,0:T(8,128)(2,1)S(1)}, bf16[768,512]{1,0:T(8,128)(2,1)S(1)}, u32[]{:S(2)}, u32[]{:S(2)}) collective-permute-start(bf16[768,512]{1,0:T(8,128)(2,1)S(1)} %collective-permute-done.9.refs_4_), channel_id=1, source_target_pairs={{0,8},{1,9},{2,10},{3,11},{4,12},{5,13},{6,14},{7,15},{8,0},{9,1},... | collective-permute-start | bytes 2359304 | tf_op jit(solution)/shard_map/ppermute | solution.py:377
  139.3 7.5 %collective-permute-start.20 = (bf16[256,512]{1,0:T(8,128)(2,1)S(1)}, bf16[256,512]{1,0:T(8,128)(2,1)S(1)}, u32[]{:S(2)}, u32[]{:S(2)}) collective-permute-start(bf16[256,512]{1,0:T(8,128)(2,1)S(1)} %slice.14), channel_id=1, source_target_pairs={{0,64},{1,65},{2,66},{3,67},{4,68},{5,69},{6,70},{7,71},{8,72},{9,... | collective-permute-start | bytes 786440 | tf_op jit(solution)/shard_map/ppermute | solution.py:377
  139.8 8.3 %collective-permute-start.21 = (bf16[256,512]{1,0:T(8,128)(2,1)S(1)}, bf16[256,512]{1,0:T(8,128)(2,1)S(1)}, u32[]{:S(2)}, u32[]{:S(2)}) collective-permute-start(bf16[256,512]{1,0:T(8,128)(2,1)S(1)} %collective-permute-done.18.refs_14_), channel_id=1, source_target_pairs={{0,8},{1,9},{2,10},{3,11},{4,12},{5,13},{6,14},{7,15},{8,0},{9,1},... | collective-permute-start | bytes 786440 | tf_op jit(solution)/shard_map/ppermute | solution.py:377
  146.9 2.4 %collective-permute-start.22 = (bf16[256,512]{1,0:T(8,128)(2,1)S(1)}, bf16[256,512]{1,0:T(8,128)(2,1)S(1)}, u32[]{:S(2)}, u32[]{:S(2)}) collective-permute-start(bf16[256,512]{1,0:T(8,128)(2,1)S(1)} %collective-permute-done.19.refs_15_), channel_id=1, source_target_pairs={{0,8},{1,9},{2,10},{3,11},{4,12},{5,13},{6,14},{7,15},{8,0},{9,1},... | collective-permute-start | bytes 786440 | tf_op jit(solution)/shard_map/ppermute | solution.py:377
  148.1 1.5 collective-permute-start.23
  (18 other events, 86.9 us)

commit v5 on v4

--- a/solution.py
+++ b/solution.py
@@ -414,14 +414,17 @@
 
     low, middle, high = (slice(k * THIRD, (k + 1) * THIRD) for k in range(3))
     below, above, across = over(send, 0, 1, 0), over(send, 0, -1, 0), over(send, 1, 0, 0)
-    send_pair = over(send, 0, 0, 1)
     far_x, across_above, across_below = over(below, 0, 1, 0), over(across, 0, -1, 0), over(below, 1, 0, 0)
-    below_pair, above_pair, across_pair = (over(item, 0, 0, 1) for item in (below, above, across))
+    send, below, above, across, far_x, across_above, across_below = lax.optimization_barrier(
+        (send, below, above, across, far_x, across_above, across_below)
+    )
     last = [
         over(across_above[low], 0, -1, 0),
         over(across_below[middle], 0, 1, 0),
         over(far_x[high], 1, 0, 0),
     ]
+    send_pair = over(send, 0, 0, 1)
+    below_pair, above_pair, across_pair = (over(item, 0, 0, 1) for item in (below, above, across))
     far_pair, across_above_pair, across_below_pair = (
         over(item, 0, 0, 1) for item in (far_x, across_above, across_below)
     )

time: 209 us -> 196 us (0.938)
  starting transfers between devices: 41.2 us -> 34.2 us
  waiting for transfers between devices: 54.2 us -> 47.4 us
    ppermute x24, starting transfers between devices: 41.2 us -> 34.2 us  [sent(): return lax.ppermute(array, ('tm', 'space'), pairs)]
    ppermute x24, waiting for transfers between devices: 54.2 us -> 47.4 us  [sent(): return lax.ppermute(array, ('tm', 'space'), pairs)]
    unnamed x54 -> x50, local copies, waits for them, and re-layouts: 5.32 us -> 4.99 us
  transfers between devices with their start and end apart: 24 -> 24, of which waited for: 10 -> 11; matrix products, arithmetic and copies ran while one was open for 1% -> 1% of each run, Pallas kernels for 0% -> 0%
where the time goes in v5:
time: 196 us; the launch traced here: 194 us
  Pallas kernels  106 us (54%)
  waiting for transfers between devices  47.4 us (24%)
  starting transfers between devices  34.2 us (17%)
  local copies, waits for them, and re-layouts  5.05 us (3%)
    pallas_call x1, Pallas kernels, body(): pl.pallas_call(chain_kernel, out_shape=jax.ShapeDtypeStruct((STRIDE, VARS...  57 us
    pallas_call x1, Pallas kernels, body(): pl.pallas_call(relax_kernel, out_shape=(jax.ShapeDtypeStruct((ROWS, NODES...  49 us
    ppermute x24, waiting for transfers between devices, sent(): return lax.ppermute(array, ('tm', 'space'), pairs)  47.4 us
    ppermute x24, starting transfers between devices, sent(): return lax.ppermute(array, ('tm', 'space'), pairs)  34.2 us
    unnamed x50, local copies, waits for them, and re-layouts  4.99 us
  transfers between devices with their start and end apart: 24, of which 11 were waited for; matrix products, arithmetic and copies ran while one was open for 1% of the time, Pallas kernels for 0%

profile of v5, /device:TPU:1, one launch (start us, length us, event | category | flops | bytes accessed | tf_op | source)
XLA Modules:
  0.0 194.4 jit_solution(17252051060577957048)
XLA Ops:
  0.0 0.7 copy-done.22
  0.7 1.0 fusion.3
  1.7 2.7 %collective-permute-start = (bf16[112,512]{1,0:T(8,128)(2,1)S(1)}, bf16[112,512]{1,0:T(8,128)(2,1)S(1)}, u32[]{:S(2)}, u32[]{:S(2)}) collective-permute-start(bf16[112,512]{1,0:T(8,128)(2,1)S(1)} %fusion.2), channel_id=1, source_target_pairs={{0,8},{1,9},{2,10},{3,11},{4,12},{5,13},{6,14},{7,15},{8,16},{9,17... | collective-permute-start | bytes 344072 | tf_op jit(solution)/shard_map/ppermute | solution.py:377
  4.4 3.4 %collective-permute-start.1 = (bf16[112,512]{1,0:T(8,128)(2,1)S(1)}, bf16[112,512]{1,0:T(8,128)(2,1)S(1)}, u32[]{:S(2)}, u32[]{:S(2)}) collective-permute-start(bf16[112,512]{1,0:T(8,128)(2,1)S(1)} %fusion.2), channel_id=1, source_target_pairs={{0,9},{1,8},{2,11},{3,10},{4,13},{5,12},{6,15},{7,14},{8,17},{9,16... | collective-permute-start | bytes 344072 | tf_op jit(solution)/shard_map/ppermute | solution.py:377
  7.8 2.3 %collective-permute-done.1 = bf16[112,512]{1,0:T(8,128)(2,1)S(1)} collective-permute-done((bf16[112,512]{1,0:T(8,128)(2,1)S(1)}, bf16[112,512]{1,0:T(8,128)(2,1)S(1)}, u32[]{:S(2)}, u32[]{:S(2)}) %collective-permute-start.1) | collective-permute-done | bytes 114720 | tf_op jit(solution)/shard_map/ppermute | solution.py:377
  10.1 2.8 %collective-permute-start.4 = (bf16[224,512]{1,0:T(8,128)(2,1)S(1)}, bf16[224,512]{1,0:T(8,128)(2,1)S(1)}, u32[]{:S(2)}, u32[]{:S(2)}) collective-permute-start(bf16[224,512]{1,0:T(8,128)(2,1)S(1)} %constant_dynamic-update-slice_fusion.refs_2_), channel_id=1, source_target_pairs={{0,6},{1,7},{2,0},{3,1},{4,2},{5,3},{6,4},{7,5},{8,14},{9,15},{10,... | collective-permute-start | bytes 688136 | tf_op jit(solution)/shard_map/ppermute | solution.py:377
  12.9 1.6 collective-permute-start.2
  14.6 0.7 copy-done.23
  15.2 0.7 copy.13.species_ref
  16.6 5.6 %collective-permute-done.3.refs_1_ = bf16[224,512]{1,0:T(8,128)(2,1)S(1)} collective-permute-done((bf16[224,512]{1,0:T(8,128)(2,1)S(1)}, bf16[224,512]{1,0:T(8,128)(2,1)S(1)}, u32[]{:S(2)}, u32[]{:S(2)}) %collective-permute-start.3) | collective-permute-done | bytes 229408 | tf_op jit(solution)/shard_map/ppermute | solution.py:377
  22.9 0.7 copy-done.20
  23.5 49.0 %shard_map.109 = (bf16[768,512]{1,0:T(8,128)(2,1)}, f32[12,8,512]{2,1,0:T(8,128)}, bf16[768,512]{1,0:T(8,128)(2,1)}, bf16[3,64,128]{2,1,0:T(8,128)(2,1)}) custom-call(s32[2]{0:T(128)} %pad_add_fusion.group_ref, s32[24,3]{1,0:T(8,128)} %copy.13.species_ref, f32[24]{0:T(128)} %rate_ref.3, f32[12]{0:T(128)} %speed_ref.3, bf16[224,512]{1,0:T(8,128)(2,1)} %copy-done.20, ...), custom_call_target="tpu_custom_call" | custom-call | tf_op jit(solution)/shard_map/pallas_call | solution.py:391
  72.5 4.7 %collective-permute-start.7 = (bf16[768,512]{1,0:T(8,128)(2,1)}, bf16[768,512]{1,0:T(8,128)(2,1)S(1)}, u32[]{:S(2)}, u32[]{:S(2)}) collective-permute-start(bf16[768,512]{1,0:T(8,128)(2,1)} %get-tuple-element.17.refs_0_), channel_id=1, source_target_pairs={{0,64},{1,65},{2,66},{3,67},{4,68},{5,69},{6,70},{7,71},{8,72},{9,... | collective-permute-start | bytes 2359304 | tf_op jit(solution)/shard_map/ppermute | solution.py:377
  77.2 3.2 %collective-permute-start.5 = (bf16[768,512]{1,0:T(8,128)(2,1)}, bf16[768,512]{1,0:T(8,128)(2,1)S(1)}, u32[]{:S(2)}, u32[]{:S(2)}) collective-permute-start(bf16[768,512]{1,0:T(8,128)(2,1)} %get-tuple-element.17.refs_0_), channel_id=1, source_target_pairs={{0,16},{1,17},{2,18},{3,19},{4,20},{5,21},{6,22},{7,23},{8,24},{9,... | collective-permute-start | bytes 2359304 | tf_op jit(solution)/shard_map/ppermute | solution.py:377
  80.5 10.9 %collective-permute-done.7.refs_8_ = bf16[768,512]{1,0:T(8,128)(2,1)S(1)} collective-permute-done((bf16[768,512]{1,0:T(8,128)(2,1)}, bf16[768,512]{1,0:T(8,128)(2,1)S(1)}, u32[]{:S(2)}, u32[]{:S(2)}) %collective-permute-start.7) | collective-permute-done | bytes 786464 | tf_op jit(solution)/shard_map/ppermute | solution.py:377
  91.4 2.8 %collective-permute-start.9 = (bf16[768,512]{1,0:T(8,128)(2,1)S(1)}, bf16[768,512]{1,0:T(8,128)(2,1)S(1)}, u32[]{:S(2)}, u32[]{:S(2)}) collective-permute-start(bf16[768,512]{1,0:T(8,128)(2,1)S(1)} %collective-permute-done.7.refs_8_), channel_id=1, source_target_pairs={{0,48},{1,49},{2,50},{3,51},{4,52},{5,53},{6,54},{7,55},{8,56},{9,... | collective-permute-start | bytes 2359304 | tf_op jit(solution)/shard_map/ppermute | solution.py:377
  94.2 2.2 %collective-permute-done.5.refs_6_ = bf16[768,512]{1,0:T(8,128)(2,1)S(1)} collective-permute-done((bf16[768,512]{1,0:T(8,128)(2,1)}, bf16[768,512]{1,0:T(8,128)(2,1)S(1)}, u32[]{:S(2)}, u32[]{:S(2)}) %collective-permute-start.5) | collective-permute-done | bytes 786464 | tf_op jit(solution)/shard_map/ppermute | solution.py:377
  96.7 2.3 %collective-permute-start.8 = (bf16[768,512]{1,0:T(8,128)(2,1)S(1)}, bf16[768,512]{1,0:T(8,128)(2,1)S(1)}, u32[]{:S(2)}, u32[]{:S(2)}) collective-permute-start(bf16[768,512]{1,0:T(8,128)(2,1)S(1)} %collective-permute-done.5.refs_6_), channel_id=1, source_target_pairs={{0,16},{1,17},{2,18},{3,19},{4,20},{5,21},{6,22},{7,23},{8,24},{9,... | collective-permute-start | bytes 2359304 | tf_op jit(solution)/shard_map/ppermute | solution.py:377
  99.0 16.7 %collective-permute-done.9.refs_10_ = bf16[768,512]{1,0:T(8,128)(2,1)S(1)} collective-permute-done((bf16[768,512]{1,0:T(8,128)(2,1)S(1)}, bf16[768,512]{1,0:T(8,128)(2,1)S(1)}, u32[]{:S(2)}, u32[]{:S(2)}) %collective-permute-start.9) | collective-permute-done | bytes 786464 | tf_op jit(solution)/shard_map/ppermute | solution.py:377
  115.7 2.1 %collective-permute-start.11 = (bf16[768,512]{1,0:T(8,128)(2,1)}, bf16[768,512]{1,0:T(8,128)(2,1)S(1)}, u32[]{:S(2)}, u32[]{:S(2)}) collective-permute-start(bf16[768,512]{1,0:T(8,128)(2,1)} %get-tuple-element.17.refs_0_), channel_id=1, source_target_pairs={{0,8},{1,9},{2,10},{3,11},{4,12},{5,13},{6,14},{7,15},{8,0},{9,1},... | collective-permute-start | bytes 2359304 | tf_op jit(solution)/shard_map/ppermute | solution.py:377
  117.9 1.2 collective-permute-start.19
  119.1 1.7 collective-permute-start.18
  120.7 1.2 collective-permute-start.20
  121.9 4.6 %collective-permute-done.19.refs_15_ = bf16[256,512]{1,0:T(8,128)(2,1)S(1)} collective-permute-done((bf16[256,512]{1,0:T(8,128)(2,1)S(1)}, bf16[256,512]{1,0:T(8,128)(2,1)S(1)}, u32[]{:S(2)}, u32[]{:S(2)}) %collective-permute-start.19) | collective-permute-done | bytes 262176 | tf_op jit(solution)/shard_map/ppermute | solution.py:377
  126.5 1.4 collective-permute-start.22
  128.0 1.6 collective-permute-start.23
  131.8 1.1 collective-permute-done.14.refs_7_
  133.0 1.1 collective-permute-done.15.refs_9_
  134.1 1.1 collective-permute-done.16.refs_11_
  135.2 1.1 collective-permute-done.17.refs_13_
  136.3 0.9 copy-done.12
  137.3 57.0 %shard_map.110 = f32[4,12,8,512]{3,2,1,0:T(8,128)} custom-call(s32[2]{0:T(128)} %pad_add_fusion.group_ref, s32[24,3]{1,0:T(8,128)} %copy.13.species_ref, f32[24]{0:T(128)} %rate_ref.3, f32[12]{0:T(128)} %speed_ref.3, bf16[768,512]{1,0:T(8,128)(2,1)} %get-tuple-element.17.refs_0_, bf16[768,512]{1,0:T(8,128)(2,1)} %copy-done.6, bf16[768,512]{1,0:T(8,128)(2,1)} %copy-done.5, ...), custom_call_target="tpu_custom_call" | custom-call | tf_op jit(solution)/shard_map/pallas_call | solution.py:437
  (76 shorter events, 4.2 us)
Async XLA Ops:
  1.7 6.1 %collective-permute-start = (bf16[112,512]{1,0:T(8,128)(2,1)S(1)}, bf16[112,512]{1,0:T(8,128)(2,1)S(1)}, u32[]{:S(2)}, u32[]{:S(2)}) collective-permute-start(bf16[112,512]{1,0:T(8,128)(2,1)S(1)} %fusion.2), channel_id=1, source_target_pairs={{0,8},{1,9},{2,10},{3,11},{4,12},{5,13},{6,14},{7,15},{8,16},{9,17... | collective-permute-start | bytes 344072 | tf_op jit(solution)/shard_map/ppermute | solution.py:377
  4.4 5.7 %collective-permute-start.1 = (bf16[112,512]{1,0:T(8,128)(2,1)S(1)}, bf16[112,512]{1,0:T(8,128)(2,1)S(1)}, u32[]{:S(2)}, u32[]{:S(2)}) collective-permute-start(bf16[112,512]{1,0:T(8,128)(2,1)S(1)} %fusion.2), channel_id=1, source_target_pairs={{0,9},{1,8},{2,11},{3,10},{4,13},{5,12},{6,15},{7,14},{8,17},{9,16... | collective-permute-start | bytes 344072 | tf_op jit(solution)/shard_map/ppermute | solution.py:377
  10.1 12.1 %copy-start.13 = (bf16[224,512]{1,0:T(8,128)(2,1)}, bf16[224,512]{1,0:T(8,128)(2,1)S(1)}, u32[]{:S(2)}) copy-start(bf16[224,512]{1,0:T(8,128)(2,1)S(1)} %constant_dynamic-update-slice_fusion.refs_2_) | copy-start | bytes 688132
  10.1 6.5 %collective-permute-start.4 = (bf16[224,512]{1,0:T(8,128)(2,1)S(1)}, bf16[224,512]{1,0:T(8,128)(2,1)S(1)}, u32[]{:S(2)}, u32[]{:S(2)}) collective-permute-start(bf16[224,512]{1,0:T(8,128)(2,1)S(1)} %constant_dynamic-update-slice_fusion.refs_2_), channel_id=1, source_target_pairs={{0,6},{1,7},{2,0},{3,1},{4,2},{5,3},{6,4},{7,5},{8,14},{9,15},{10,... | collective-permute-start | bytes 688136 | tf_op jit(solution)/shard_map/ppermute | solution.py:377
  12.9 9.3 %collective-permute-start.3 = (bf16[224,512]{1,0:T(8,128)(2,1)S(1)}, bf16[224,512]{1,0:T(8,128)(2,1)S(1)}, u32[]{:S(2)}, u32[]{:S(2)}) collective-permute-start(bf16[224,512]{1,0:T(8,128)(2,1)S(1)} %constant_dynamic-update-slice_fusion.refs_2_), channel_id=1, source_target_pairs={{0,2},{1,3},{2,4},{3,5},{4,6},{5,7},{6,0},{7,1},{8,10},{9,11},{10,... | collective-permute-start | bytes 688136 | tf_op jit(solution)/shard_map/ppermute | solution.py:377
  12.9 9.3 %collective-permute-start.2 = (bf16[224,512]{1,0:T(8,128)(2,1)S(1)}, bf16[224,512]{1,0:T(8,128)(2,1)S(1)}, u32[]{:S(2)}, u32[]{:S(2)}) collective-permute-start(bf16[224,512]{1,0:T(8,128)(2,1)S(1)} %constant_dynamic-update-slice_fusion.refs_2_), channel_id=1, source_target_pairs={{0,4},{1,5},{2,6},{3,7},{4,0},{5,1},{6,2},{7,3},{8,12},{9,13},{10,... | collective-permute-start | bytes 688136 | tf_op jit(solution)/shard_map/ppermute | solution.py:377
  72.5 18.9 %collective-permute-start.7 = (bf16[768,512]{1,0:T(8,128)(2,1)}, bf16[768,512]{1,0:T(8,128)(2,1)S(1)}, u32[]{:S(2)}, u32[]{:S(2)}) collective-permute-start(bf16[768,512]{1,0:T(8,128)(2,1)} %get-tuple-element.17.refs_0_), channel_id=1, source_target_pairs={{0,64},{1,65},{2,66},{3,67},{4,68},{5,69},{6,70},{7,71},{8,72},{9,... | collective-permute-start | bytes 2359304 | tf_op jit(solution)/shard_map/ppermute | solution.py:377
  77.2 19.1 %collective-permute-start.5 = (bf16[768,512]{1,0:T(8,128)(2,1)}, bf16[768,512]{1,0:T(8,128)(2,1)S(1)}, u32[]{:S(2)}, u32[]{:S(2)}) collective-permute-start(bf16[768,512]{1,0:T(8,128)(2,1)} %get-tuple-element.17.refs_0_), channel_id=1, source_target_pairs={{0,16},{1,17},{2,18},{3,19},{4,20},{5,21},{6,22},{7,23},{8,24},{9,... | collective-permute-start | bytes 2359304 | tf_op jit(solution)/shard_map/ppermute | solution.py:377
  80.5 18.5 %collective-permute-start.6 = (bf16[768,512]{1,0:T(8,128)(2,1)}, bf16[768,512]{1,0:T(8,128)(2,1)S(1)}, u32[]{:S(2)}, u32[]{:S(2)}) collective-permute-start(bf16[768,512]{1,0:T(8,128)(2,1)} %get-tuple-element.17.refs_0_), channel_id=1, source_target_pairs={{0,48},{1,49},{2,50},{3,51},{4,52},{5,53},{6,54},{7,55},{8,56},{9,... | collective-permute-start | bytes 2359304 | tf_op jit(solution)/shard_map/ppermute | solution.py:377
  91.4 45.8 %copy-start.3 = (bf16[768,512]{1,0:T(8,128)(2,1)}, bf16[768,512]{1,0:T(8,128)(2,1)S(1)}, u32[]{:S(2)}) copy-start(bf16[768,512]{1,0:T(8,128)(2,1)S(1)} %collective-permute-done.7.refs_8_) | copy-start | bytes 2359300
  91.4 24.3 %collective-permute-start.9 = (bf16[768,512]{1,0:T(8,128)(2,1)S(1)}, bf16[768,512]{1,0:T(8,128)(2,1)S(1)}, u32[]{:S(2)}, u32[]{:S(2)}) collective-permute-start(bf16[768,512]{1,0:T(8,128)(2,1)S(1)} %collective-permute-done.7.refs_8_), channel_id=1, source_target_pairs={{0,48},{1,49},{2,50},{3,51},{4,52},{5,53},{6,54},{7,55},{8,56},{9,... | collective-permute-start | bytes 2359304 | tf_op jit(solution)/shard_map/ppermute | solution.py:377
  96.3 40.9 %copy-start.4 = (bf16[768,512]{1,0:T(8,128)(2,1)}, bf16[768,512]{1,0:T(8,128)(2,1)S(1)}, u32[]{:S(2)}) copy-start(bf16[768,512]{1,0:T(8,128)(2,1)S(1)} %collective-permute-done.5.refs_6_) | copy-start | bytes 2359300
  96.3 19.4 %collective-permute-start.10 = (bf16[768,512]{1,0:T(8,128)(2,1)S(1)}, bf16[768,512]{1,0:T(8,128)(2,1)S(1)}, u32[]{:S(2)}, u32[]{:S(2)}) collective-permute-start(bf16[768,512]{1,0:T(8,128)(2,1)S(1)} %collective-permute-done.5.refs_6_), channel_id=1, source_target_pairs={{0,64},{1,65},{2,66},{3,67},{4,68},{5,69},{6,70},{7,71},{8,72},{9,... | collective-permute-start | bytes 2359304 | tf_op jit(solution)/shard_map/ppermute | solution.py:377
  96.7 19.0 %collective-permute-start.8 = (bf16[768,512]{1,0:T(8,128)(2,1)S(1)}, bf16[768,512]{1,0:T(8,128)(2,1)S(1)}, u32[]{:S(2)}, u32[]{:S(2)}) collective-permute-start(bf16[768,512]{1,0:T(8,128)(2,1)S(1)} %collective-permute-done.5.refs_6_), channel_id=1, source_target_pairs={{0,16},{1,17},{2,18},{3,19},{4,20},{5,21},{6,22},{7,23},{8,24},{9,... | collective-permute-start | bytes 2359304 | tf_op jit(solution)/shard_map/ppermute | solution.py:377
  99.0 38.3 %copy-start.5 = (bf16[768,512]{1,0:T(8,128)(2,1)}, bf16[768,512]{1,0:T(8,128)(2,1)S(1)}, u32[]{:S(2)}) copy-start(bf16[768,512]{1,0:T(8,128)(2,1)S(1)} %collective-permute-done.6.refs_2_) | copy-start | bytes 2359300
  115.7 15.5 %copy-start = (bf16[768,512]{1,0:T(8,128)(2,1)}, bf16[768,512]{1,0:T(8,128)(2,1)S(1)}, u32[]{:S(2)}) copy-start(bf16[768,512]{1,0:T(8,128)(2,1)S(1)} %collective-permute-done.9.refs_10_) | copy-start | bytes 2359300
  115.7 21.5 %copy-start.1 = (bf16[768,512]{1,0:T(8,128)(2,1)}, bf16[768,512]{1,0:T(8,128)(2,1)S(1)}, u32[]{:S(2)}) copy-start(bf16[768,512]{1,0:T(8,128)(2,1)S(1)} %collective-permute-done.10.refs_12_) | copy-start | bytes 2359300
  115.7 21.5 %copy-start.2 = (bf16[768,512]{1,0:T(8,128)(2,1)}, bf16[768,512]{1,0:T(8,128)(2,1)S(1)}, u32[]{:S(2)}) copy-start(bf16[768,512]{1,0:T(8,128)(2,1)S(1)} %collective-permute-done.8.refs_4_) | copy-start | bytes 2359300
  115.7 15.5 %collective-permute-start.11 = (bf16[768,512]{1,0:T(8,128)(2,1)}, bf16[768,512]{1,0:T(8,128)(2,1)S(1)}, u32[]{:S(2)}, u32[]{:S(2)}) collective-permute-start(bf16[768,512]{1,0:T(8,128)(2,1)} %get-tuple-element.17.refs_0_), channel_id=1, source_target_pairs={{0,8},{1,9},{2,10},{3,11},{4,12},{5,13},{6,14},{7,15},{8,0},{9,1},... | collective-permute-start | bytes 2359304 | tf_op jit(solution)/shard_map/ppermute | solution.py:377
  117.9 13.6 %collective-permute-start.12 = (bf16[768,512]{1,0:T(8,128)(2,1)S(1)}, bf16[768,512]{1,0:T(8,128)(2,1)S(1)}, u32[]{:S(2)}, u32[]{:S(2)}) collective-permute-start(bf16[768,512]{1,0:T(8,128)(2,1)S(1)} %collective-permute-done.6.refs_2_), channel_id=1, source_target_pairs={{0,8},{1,9},{2,10},{3,11},{4,12},{5,13},{6,14},{7,15},{8,0},{9,1},... | collective-permute-start | bytes 2359304 | tf_op jit(solution)/shard_map/ppermute | solution.py:377
  117.9 8.6 %collective-permute-start.19 = (bf16[256,512]{1,0:T(8,128)(2,1)S(1)}, bf16[256,512]{1,0:T(8,128)(2,1)S(1)}, u32[]{:S(2)}, u32[]{:S(2)}) collective-permute-start(bf16[256,512]{1,0:T(8,128)(2,1)S(1)} %slice.10), channel_id=1, source_target_pairs={{0,16},{1,17},{2,18},{3,19},{4,20},{5,21},{6,22},{7,23},{8,24},{9,... | collective-permute-start | bytes 786440 | tf_op jit(solution)/shard_map/ppermute | solution.py:377
  119.1 8.8 %collective-permute-start.18 = (bf16[256,512]{1,0:T(8,128)(2,1)S(1)}, bf16[256,512]{1,0:T(8,128)(2,1)S(1)}, u32[]{:S(2)}, u32[]{:S(2)}) collective-permute-start(bf16[256,512]{1,0:T(8,128)(2,1)S(1)} %slice.9), channel_id=1, source_target_pairs={{0,48},{1,49},{2,50},{3,51},{4,52},{5,53},{6,54},{7,55},{8,56},{9,... | collective-permute-start | bytes 786440 | tf_op jit(solution)/shard_map/ppermute | solution.py:377
  120.7 7.2 %collective-permute-start.20 = (bf16[256,512]{1,0:T(8,128)(2,1)S(1)}, bf16[256,512]{1,0:T(8,128)(2,1)S(1)}, u32[]{:S(2)}, u32[]{:S(2)}) collective-permute-start(bf16[256,512]{1,0:T(8,128)(2,1)S(1)} %slice.11), channel_id=1, source_target_pairs={{0,64},{1,65},{2,66},{3,67},{4,68},{5,69},{6,70},{7,71},{8,72},{9,... | collective-permute-start | bytes 786440 | tf_op jit(solution)/shard_map/ppermute | solution.py:377
  126.5 10.7 %copy-start.14 = (bf16[256,512]{1,0:T(8,128)(2,1)}, bf16[256,512]{1,0:T(8,128)(2,1)S(1)}, u32[]{:S(2)}) copy-start(bf16[256,512]{1,0:T(8,128)(2,1)S(1)} %collective-permute-done.19.refs_15_) | copy-start | bytes 786436
  126.5 3.0 %collective-permute-start.22 = (bf16[256,512]{1,0:T(8,128)(2,1)S(1)}, bf16[256,512]{1,0:T(8,128)(2,1)S(1)}, u32[]{:S(2)}, u32[]{:S(2)}) collective-permute-start(bf16[256,512]{1,0:T(8,128)(2,1)S(1)} %collective-permute-done.19.refs_15_), channel_id=1, source_target_pairs={{0,8},{1,9},{2,10},{3,11},{4,12},{5,13},{6,14},{7,15},{8,0},{9,1},... | collective-permute-start | bytes 786440 | tf_op jit(solution)/shard_map/ppermute | solution.py:377
  127.9 2.4 %collective-permute-start.21 = (bf16[256,512]{1,0:T(8,128)(2,1)S(1)}, bf16[256,512]{1,0:T(8,128)(2,1)}, u32[]{:S(2)}, u32[]{:S(2)}) collective-permute-start(bf16[256,512]{1,0:T(8,128)(2,1)S(1)} %collective-permute-done.18.refs_14_), channel_id=1, source_target_pairs={{0,8},{1,9},{2,10},{3,11},{4,12},{5,13},{6,14},{7,15},{8,0},{9,1},... | collective-permute-start | bytes 786440 | tf_op jit(solution)/shard_map/ppermute | solution.py:377
  128.0 2.8 %collective-permute-start.23 = (bf16[256,512]{1,0:T(8,128)(2,1)S(1)}, bf16[256,512]{1,0:T(8,128)(2,1)}, u32[]{:S(2)}, u32[]{:S(2)}) collective-permute-start(bf16[256,512]{1,0:T(8,128)(2,1)S(1)} %collective-permute-done.20.refs_16_), channel_id=1, source_target_pairs={{0,8},{1,9},{2,10},{3,11},{4,12},{5,13},{6,14},{7,15},{8,0},{9,1},... | collective-permute-start | bytes 786440 | tf_op jit(solution)/shard_map/ppermute | solution.py:377
  129.5 4.5 %collective-permute-start.13 = (bf16[768,512]{1,0:T(8,128)(2,1)S(1)}, bf16[768,512]{1,0:T(8,128)(2,1)S(1)}, u32[]{:S(2)}, u32[]{:S(2)}) collective-permute-start(bf16[768,512]{1,0:T(8,128)(2,1)S(1)} %collective-permute-done.8.refs_4_), channel_id=1, source_target_pairs={{0,8},{1,9},{2,10},{3,11},{4,12},{5,13},{6,14},{7,15},{8,0},{9,1},... | collective-permute-start | bytes 2359304 | tf_op jit(solution)/shard_map/ppermute | solution.py:377
  130.3 2.7 %collective-permute-start.14 = (bf16[768,512]{1,0:T(8,128)(2,1)S(1)}, bf16[768,512]{1,0:T(8,128)(2,1)S(1)}, u32[]{:S(2)}, u32[]{:S(2)}) collective-permute-start(bf16[768,512]{1,0:T(8,128)(2,1)S(1)} %collective-permute-done.5.refs_6_), channel_id=1, source_target_pairs={{0,8},{1,9},{2,10},{3,11},{4,12},{5,13},{6,14},{7,15},{8,0},{9,1},... | collective-permute-start | bytes 2359304 | tf_op jit(solution)/shard_map/ppermute | solution.py:377
  130.8 3.2 %collective-permute-start.15 = (bf16[768,512]{1,0:T(8,128)(2,1)S(1)}, bf16[768,512]{1,0:T(8,128)(2,1)S(1)}, u32[]{:S(2)}, u32[]{:S(2)}) collective-permute-start(bf16[768,512]{1,0:T(8,128)(2,1)S(1)} %collective-permute-done.7.refs_8_), channel_id=1, source_target_pairs={{0,8},{1,9},{2,10},{3,11},{4,12},{5,13},{6,14},{7,15},{8,0},{9,1},... | collective-permute-start | bytes 2359304 | tf_op jit(solution)/shard_map/ppermute | solution.py:377
  131.2 4.0 %collective-permute-start.16 = (bf16[768,512]{1,0:T(8,128)(2,1)S(1)}, bf16[768,512]{1,0:T(8,128)(2,1)S(1)}, u32[]{:S(2)}, u32[]{:S(2)}) collective-permute-start(bf16[768,512]{1,0:T(8,128)(2,1)S(1)} %collective-permute-done.9.refs_10_), channel_id=1, source_target_pairs={{0,8},{1,9},{2,10},{3,11},{4,12},{5,13},{6,14},{7,15},{8,0},{9,1},... | collective-permute-start | bytes 2359304 | tf_op jit(solution)/shard_map/ppermute | solution.py:377
  131.4 4.9 %collective-permute-start.17 = (bf16[768,512]{1,0:T(8,128)(2,1)S(1)}, bf16[768,512]{1,0:T(8,128)(2,1)S(1)}, u32[]{:S(2)}, u32[]{:S(2)}) collective-permute-start(bf16[768,512]{1,0:T(8,128)(2,1)S(1)} %collective-permute-done.10.refs_12_), channel_id=1, source_target_pairs={{0,8},{1,9},{2,10},{3,11},{4,12},{5,13},{6,14},{7,15},{8,0},{9,1},... | collective-permute-start | bytes 2359304 | tf_op jit(solution)/shard_map/ppermute | solution.py:377
  (16 other events, 37.6 us)

commit v6 on v4

--- a/solution.py
+++ b/solution.py
@@ -414,14 +414,18 @@
 
     low, middle, high = (slice(k * THIRD, (k + 1) * THIRD) for k in range(3))
     below, above, across = over(send, 0, 1, 0), over(send, 0, -1, 0), over(send, 1, 0, 0)
-    send_pair = over(send, 0, 0, 1)
     far_x, across_above, across_below = over(below, 0, 1, 0), over(across, 0, -1, 0), over(below, 1, 0, 0)
-    below_pair, above_pair, across_pair = (over(item, 0, 0, 1) for item in (below, above, across))
+    held = lax.optimization_barrier((send, below, above, across))
+    send_pair, above_pair = over(held[0], 0, 0, 1), over(held[2], 0, 0, 1)
+    below, across, far_x, across_above, across_below = lax.optimization_barrier(
+        (below, across, far_x, across_above, across_below)
+    )
     last = [
         over(across_above[low], 0, -1, 0),
         over(across_below[middle], 0, 1, 0),
         over(far_x[high], 1, 0, 0),
     ]
+    below_pair, across_pair = (over(item, 0, 0, 1) for item in (below, across))
     far_pair, across_above_pair, across_below_pair = (
         over(item, 0, 0, 1) for item in (far_x, across_above, across_below)
     )

time: 209 us -> 194 us (0.928)
  waiting for transfers between devices: 54.2 us -> 44.1 us
  starting transfers between devices: 41.2 us -> 36.2 us
    ppermute x24, waiting for transfers between devices: 54.2 us -> 44.1 us  [sent(): return lax.ppermute(array, ('tm', 'space'), pairs)]
    ppermute x24, starting transfers between devices: 41.2 us -> 36.2 us  [sent(): return lax.ppermute(array, ('tm', 'space'), pairs)]
    unnamed x54 -> x48, local copies, waits for them, and re-layouts: 5.32 us -> 4.37 us
  transfers between devices with their start and end apart: 24 -> 24, of which waited for: 10 -> 11; matrix products, arithmetic and copies ran while one was open for 1% -> 1% of each run, Pallas kernels for 0% -> 0%
where the time goes in v6:
time: 194 us; the launch traced here: 193 us
  Pallas kernels  106 us (55%)
  waiting for transfers between devices  44.1 us (23%)
  starting transfers between devices  36.2 us (19%)
  local copies, waits for them, and re-layouts  4.44 us (2%)
    pallas_call x1, Pallas kernels, body(): pl.pallas_call(chain_kernel, out_shape=jax.ShapeDtypeStruct((STRIDE, VARS...  56.9 us
    pallas_call x1, Pallas kernels, body(): pl.pallas_call(relax_kernel, out_shape=(jax.ShapeDtypeStruct((ROWS, NODES...  49 us
    ppermute x24, waiting for transfers between devices, sent(): return lax.ppermute(array, ('tm', 'space'), pairs)  44.1 us
    ppermute x24, starting transfers between devices, sent(): return lax.ppermute(array, ('tm', 'space'), pairs)  36.2 us
    unnamed x48, local copies, waits for them, and re-layouts  4.37 us
  transfers between devices with their start and end apart: 24, of which 11 were waited for; matrix products, arithmetic and copies ran while one was open for 1% of the time, Pallas kernels for 0%

profile of v6, /device:TPU:1, one launch (start us, length us, event | category | flops | bytes accessed | tf_op | source)
XLA Modules:
  0.0 192.6 jit_solution(9784052248728211175)
XLA Ops:
  0.0 0.7 copy-done.21
  0.7 1.0 fusion.3
  1.7 2.7 %collective-permute-start = (bf16[112,512]{1,0:T(8,128)(2,1)S(1)}, bf16[112,512]{1,0:T(8,128)(2,1)S(1)}, u32[]{:S(2)}, u32[]{:S(2)}) collective-permute-start(bf16[112,512]{1,0:T(8,128)(2,1)S(1)} %fusion.2), channel_id=1, source_target_pairs={{0,8},{1,9},{2,10},{3,11},{4,12},{5,13},{6,14},{7,15},{8,16},{9,17... | collective-permute-start | bytes 344072 | tf_op jit(solution)/shard_map/ppermute | solution.py:377
  4.4 3.4 %collective-permute-start.1 = (bf16[112,512]{1,0:T(8,128)(2,1)S(1)}, bf16[112,512]{1,0:T(8,128)(2,1)S(1)}, u32[]{:S(2)}, u32[]{:S(2)}) collective-permute-start(bf16[112,512]{1,0:T(8,128)(2,1)S(1)} %fusion.2), channel_id=1, source_target_pairs={{0,9},{1,8},{2,11},{3,10},{4,13},{5,12},{6,15},{7,14},{8,17},{9,16... | collective-permute-start | bytes 344072 | tf_op jit(solution)/shard_map/ppermute | solution.py:377
  7.8 2.3 %collective-permute-done.1 = bf16[112,512]{1,0:T(8,128)(2,1)S(1)} collective-permute-done((bf16[112,512]{1,0:T(8,128)(2,1)S(1)}, bf16[112,512]{1,0:T(8,128)(2,1)S(1)}, u32[]{:S(2)}, u32[]{:S(2)}) %collective-permute-start.1) | collective-permute-done | bytes 114720 | tf_op jit(solution)/shard_map/ppermute | solution.py:377
  10.1 2.8 %collective-permute-start.4 = (bf16[224,512]{1,0:T(8,128)(2,1)S(1)}, bf16[224,512]{1,0:T(8,128)(2,1)S(1)}, u32[]{:S(2)}, u32[]{:S(2)}) collective-permute-start(bf16[224,512]{1,0:T(8,128)(2,1)S(1)} %constant_dynamic-update-slice_fusion.refs_2_), channel_id=1, source_target_pairs={{0,6},{1,7},{2,0},{3,1},{4,2},{5,3},{6,4},{7,5},{8,14},{9,15},{10,... | collective-permute-start | bytes 688136 | tf_op jit(solution)/shard_map/ppermute | solution.py:377
  12.9 1.6 collective-permute-start.2
  14.6 0.7 copy-done.22
  15.2 0.7 copy.13.species_ref
  15.9 0.6 pad_add_fusion.group_ref
  16.6 5.6 %collective-permute-done.3.refs_1_ = bf16[224,512]{1,0:T(8,128)(2,1)S(1)} collective-permute-done((bf16[224,512]{1,0:T(8,128)(2,1)S(1)}, bf16[224,512]{1,0:T(8,128)(2,1)S(1)}, u32[]{:S(2)}, u32[]{:S(2)}) %collective-permute-start.3) | collective-permute-done | bytes 229408 | tf_op jit(solution)/shard_map/ppermute | solution.py:377
  22.2 0.7 copy-done.18
  22.9 0.7 copy-done.19
  23.5 49.0 %shard_map.109 = (bf16[768,512]{1,0:T(8,128)(2,1)}, f32[12,8,512]{2,1,0:T(8,128)}, bf16[768,512]{1,0:T(8,128)(2,1)}, bf16[3,64,128]{2,1,0:T(8,128)(2,1)}) custom-call(s32[2]{0:T(128)} %pad_add_fusion.group_ref, s32[24,3]{1,0:T(8,128)} %copy.13.species_ref, f32[24]{0:T(128)} %rate_ref.3, f32[12]{0:T(128)} %speed_ref.3, bf16[224,512]{1,0:T(8,128)(2,1)} %copy-done.19, ...), custom_call_target="tpu_custom_call" | custom-call | tf_op jit(solution)/shard_map/pallas_call | solution.py:391
  72.5 4.7 %collective-permute-start.7 = (bf16[768,512]{1,0:T(8,128)(2,1)}, bf16[768,512]{1,0:T(8,128)(2,1)S(1)}, u32[]{:S(2)}, u32[]{:S(2)}) collective-permute-start(bf16[768,512]{1,0:T(8,128)(2,1)} %get-tuple-element.17.refs_0_), channel_id=1, source_target_pairs={{0,64},{1,65},{2,66},{3,67},{4,68},{5,69},{6,70},{7,71},{8,72},{9,... | collective-permute-start | bytes 2359304 | tf_op jit(solution)/shard_map/ppermute | solution.py:377
  77.2 3.2 %collective-permute-start.5 = (bf16[768,512]{1,0:T(8,128)(2,1)}, bf16[768,512]{1,0:T(8,128)(2,1)S(1)}, u32[]{:S(2)}, u32[]{:S(2)}) collective-permute-start(bf16[768,512]{1,0:T(8,128)(2,1)} %get-tuple-element.17.refs_0_), channel_id=1, source_target_pairs={{0,16},{1,17},{2,18},{3,19},{4,20},{5,21},{6,22},{7,23},{8,24},{9,... | collective-permute-start | bytes 2359304 | tf_op jit(solution)/shard_map/ppermute | solution.py:377
  80.4 11.0 %collective-permute-done.7.refs_8_ = bf16[768,512]{1,0:T(8,128)(2,1)S(1)} collective-permute-done((bf16[768,512]{1,0:T(8,128)(2,1)}, bf16[768,512]{1,0:T(8,128)(2,1)S(1)}, u32[]{:S(2)}, u32[]{:S(2)}) %collective-permute-start.7) | collective-permute-done | bytes 786464 | tf_op jit(solution)/shard_map/ppermute | solution.py:377
  91.4 2.8 %collective-permute-start.11 = (bf16[768,512]{1,0:T(8,128)(2,1)S(1)}, bf16[768,512]{1,0:T(8,128)(2,1)S(1)}, u32[]{:S(2)}, u32[]{:S(2)}) collective-permute-start(bf16[768,512]{1,0:T(8,128)(2,1)S(1)} %collective-permute-done.7.refs_8_), channel_id=1, source_target_pairs={{0,48},{1,49},{2,50},{3,51},{4,52},{5,53},{6,54},{7,55},{8,56},{9,... | collective-permute-start | bytes 2359304 | tf_op jit(solution)/shard_map/ppermute | solution.py:377
  94.2 2.1 %collective-permute-done.5.refs_6_ = bf16[768,512]{1,0:T(8,128)(2,1)S(1)} collective-permute-done((bf16[768,512]{1,0:T(8,128)(2,1)}, bf16[768,512]{1,0:T(8,128)(2,1)S(1)}, u32[]{:S(2)}, u32[]{:S(2)}) %collective-permute-start.5) | collective-permute-done | bytes 786464 | tf_op jit(solution)/shard_map/ppermute | solution.py:377
  96.7 2.3 %collective-permute-start.10 = (bf16[768,512]{1,0:T(8,128)(2,1)S(1)}, bf16[768,512]{1,0:T(8,128)(2,1)S(1)}, u32[]{:S(2)}, u32[]{:S(2)}) collective-permute-start(bf16[768,512]{1,0:T(8,128)(2,1)S(1)} %collective-permute-done.5.refs_6_), channel_id=1, source_target_pairs={{0,16},{1,17},{2,18},{3,19},{4,20},{5,21},{6,22},{7,23},{8,24},{9,... | collective-permute-start | bytes 2359304 | tf_op jit(solution)/shard_map/ppermute | solution.py:377
  99.0 3.0 %collective-permute-start.8 = (bf16[768,512]{1,0:T(8,128)(2,1)}, bf16[768,512]{1,0:T(8,128)(2,1)S(1)}, u32[]{:S(2)}, u32[]{:S(2)}) collective-permute-start(bf16[768,512]{1,0:T(8,128)(2,1)} %get-tuple-element.17.refs_0_), channel_id=1, source_target_pairs={{0,8},{1,9},{2,10},{3,11},{4,12},{5,13},{6,14},{7,15},{8,0},{9,1},... | collective-permute-start | bytes 2359304 | tf_op jit(solution)/shard_map/ppermute | solution.py:377
  102.0 13.7 %collective-permute-done.11.refs_10_ = bf16[768,512]{1,0:T(8,128)(2,1)S(1)} collective-permute-done((bf16[768,512]{1,0:T(8,128)(2,1)S(1)}, bf16[768,512]{1,0:T(8,128)(2,1)S(1)}, u32[]{:S(2)}, u32[]{:S(2)}) %collective-permute-start.11) | collective-permute-done | bytes 786464 | tf_op jit(solution)/shard_map/ppermute | solution.py:377
  115.9 2.7 %collective-permute-start.18 = (bf16[256,512]{1,0:T(8,128)(2,1)S(1)}, bf16[256,512]{1,0:T(8,128)(2,1)S(1)}, u32[]{:S(2)}, u32[]{:S(2)}) collective-permute-start(bf16[256,512]{1,0:T(8,128)(2,1)S(1)} %slice.9), channel_id=1, source_target_pairs={{0,48},{1,49},{2,50},{3,51},{4,52},{5,53},{6,54},{7,55},{8,56},{9,... | collective-permute-start | bytes 786440 | tf_op jit(solution)/shard_map/ppermute | solution.py:377
  118.7 4.0 %collective-permute-done.19.refs_15_ = bf16[256,512]{1,0:T(8,128)(2,1)S(1)} collective-permute-done((bf16[256,512]{1,0:T(8,128)(2,1)S(1)}, bf16[256,512]{1,0:T(8,128)(2,1)S(1)}, u32[]{:S(2)}, u32[]{:S(2)}) %collective-permute-start.19) | collective-permute-done | bytes 262176 | tf_op jit(solution)/shard_map/ppermute | solution.py:377
  122.7 3.0 %collective-permute-start.22 = (bf16[256,512]{1,0:T(8,128)(2,1)S(1)}, bf16[256,512]{1,0:T(8,128)(2,1)}, u32[]{:S(2)}, u32[]{:S(2)}) collective-permute-start(bf16[256,512]{1,0:T(8,128)(2,1)S(1)} %collective-permute-done.19.refs_15_), channel_id=1, source_target_pairs={{0,8},{1,9},{2,10},{3,11},{4,12},{5,13},{6,14},{7,15},{8,0},{9,1},... | collective-permute-start | bytes 786440 | tf_op jit(solution)/shard_map/ppermute | solution.py:377
  125.9 1.9 collective-permute-start.23
  129.4 1.7 collective-permute-done.14.refs_7_
  131.2 1.1 collective-permute-done.15.refs_9_
  132.3 1.1 collective-permute-done.16.refs_11_
  133.4 1.1 collective-permute-done.17.refs_13_
  134.5 0.9 copy-done.12
  135.5 56.9 %shard_map.110 = f32[4,12,8,512]{3,2,1,0:T(8,128)} custom-call(s32[2]{0:T(128)} %pad_add_fusion.group_ref, s32[24,3]{1,0:T(8,128)} %copy.13.species_ref, f32[24]{0:T(128)} %rate_ref.3, f32[12]{0:T(128)} %speed_ref.3, bf16[768,512]{1,0:T(8,128)(2,1)} %get-tuple-element.17.refs_0_, bf16[768,512]{1,0:T(8,128)(2,1)} %copy-done.6, bf16[768,512]{1,0:T(8,128)(2,1)} %copy-done.5, ...), custom_call_target="tpu_custom_call" | custom-call | tf_op jit(solution)/shard_map/pallas_call | solution.py:438
  (74 shorter events, 2.5 us)
Async XLA Ops:
  1.7 6.1 %collective-permute-start = (bf16[112,512]{1,0:T(8,128)(2,1)S(1)}, bf16[112,512]{1,0:T(8,128)(2,1)S(1)}, u32[]{:S(2)}, u32[]{:S(2)}) collective-permute-start(bf16[112,512]{1,0:T(8,128)(2,1)S(1)} %fusion.2), channel_id=1, source_target_pairs={{0,8},{1,9},{2,10},{3,11},{4,12},{5,13},{6,14},{7,15},{8,16},{9,17... | collective-permute-start | bytes 344072 | tf_op jit(solution)/shard_map/ppermute | solution.py:377
  4.4 5.7 %collective-permute-start.1 = (bf16[112,512]{1,0:T(8,128)(2,1)S(1)}, bf16[112,512]{1,0:T(8,128)(2,1)S(1)}, u32[]{:S(2)}, u32[]{:S(2)}) collective-permute-start(bf16[112,512]{1,0:T(8,128)(2,1)S(1)} %fusion.2), channel_id=1, source_target_pairs={{0,9},{1,8},{2,11},{3,10},{4,13},{5,12},{6,15},{7,14},{8,17},{9,16... | collective-permute-start | bytes 344072 | tf_op jit(solution)/shard_map/ppermute | solution.py:377
  10.1 12.1 %copy-start.13 = (bf16[224,512]{1,0:T(8,128)(2,1)}, bf16[224,512]{1,0:T(8,128)(2,1)S(1)}, u32[]{:S(2)}) copy-start(bf16[224,512]{1,0:T(8,128)(2,1)S(1)} %constant_dynamic-update-slice_fusion.refs_2_) | copy-start | bytes 688132
  10.1 6.5 %collective-permute-start.4 = (bf16[224,512]{1,0:T(8,128)(2,1)S(1)}, bf16[224,512]{1,0:T(8,128)(2,1)S(1)}, u32[]{:S(2)}, u32[]{:S(2)}) collective-permute-start(bf16[224,512]{1,0:T(8,128)(2,1)S(1)} %constant_dynamic-update-slice_fusion.refs_2_), channel_id=1, source_target_pairs={{0,6},{1,7},{2,0},{3,1},{4,2},{5,3},{6,4},{7,5},{8,14},{9,15},{10,... | collective-permute-start | bytes 688136 | tf_op jit(solution)/shard_map/ppermute | solution.py:377
  12.9 9.3 %collective-permute-start.3 = (bf16[224,512]{1,0:T(8,128)(2,1)S(1)}, bf16[224,512]{1,0:T(8,128)(2,1)S(1)}, u32[]{:S(2)}, u32[]{:S(2)}) collective-permute-start(bf16[224,512]{1,0:T(8,128)(2,1)S(1)} %constant_dynamic-update-slice_fusion.refs_2_), channel_id=1, source_target_pairs={{0,2},{1,3},{2,4},{3,5},{4,6},{5,7},{6,0},{7,1},{8,10},{9,11},{10,... | collective-permute-start | bytes 688136 | tf_op jit(solution)/shard_map/ppermute | solution.py:377
  12.9 9.3 %collective-permute-start.2 = (bf16[224,512]{1,0:T(8,128)(2,1)S(1)}, bf16[224,512]{1,0:T(8,128)(2,1)S(1)}, u32[]{:S(2)}, u32[]{:S(2)}) collective-permute-start(bf16[224,512]{1,0:T(8,128)(2,1)S(1)} %constant_dynamic-update-slice_fusion.refs_2_), channel_id=1, source_target_pairs={{0,4},{1,5},{2,6},{3,7},{4,0},{5,1},{6,2},{7,3},{8,12},{9,13},{10,... | collective-permute-start | bytes 688136 | tf_op jit(solution)/shard_map/ppermute | solution.py:377
  72.5 18.9 %collective-permute-start.7 = (bf16[768,512]{1,0:T(8,128)(2,1)}, bf16[768,512]{1,0:T(8,128)(2,1)S(1)}, u32[]{:S(2)}, u32[]{:S(2)}) collective-permute-start(bf16[768,512]{1,0:T(8,128)(2,1)} %get-tuple-element.17.refs_0_), channel_id=1, source_target_pairs={{0,64},{1,65},{2,66},{3,67},{4,68},{5,69},{6,70},{7,71},{8,72},{9,... | collective-permute-start | bytes 2359304 | tf_op jit(solution)/shard_map/ppermute | solution.py:377
  77.2 19.1 %collective-permute-start.5 = (bf16[768,512]{1,0:T(8,128)(2,1)}, bf16[768,512]{1,0:T(8,128)(2,1)S(1)}, u32[]{:S(2)}, u32[]{:S(2)}) collective-permute-start(bf16[768,512]{1,0:T(8,128)(2,1)} %get-tuple-element.17.refs_0_), channel_id=1, source_target_pairs={{0,16},{1,17},{2,18},{3,19},{4,20},{5,21},{6,22},{7,23},{8,24},{9,... | collective-permute-start | bytes 2359304 | tf_op jit(solution)/shard_map/ppermute | solution.py:377
  80.4 18.5 %collective-permute-start.6 = (bf16[768,512]{1,0:T(8,128)(2,1)}, bf16[768,512]{1,0:T(8,128)(2,1)S(1)}, u32[]{:S(2)}, u32[]{:S(2)}) collective-permute-start(bf16[768,512]{1,0:T(8,128)(2,1)} %get-tuple-element.17.refs_0_), channel_id=1, source_target_pairs={{0,48},{1,49},{2,50},{3,51},{4,52},{5,53},{6,54},{7,55},{8,56},{9,... | collective-permute-start | bytes 2359304 | tf_op jit(solution)/shard_map/ppermute | solution.py:377
  91.4 44.0 %copy-start.3 = (bf16[768,512]{1,0:T(8,128)(2,1)}, bf16[768,512]{1,0:T(8,128)(2,1)S(1)}, u32[]{:S(2)}) copy-start(bf16[768,512]{1,0:T(8,128)(2,1)S(1)} %collective-permute-done.7.refs_8_) | copy-start | bytes 2359300
  91.4 24.3 %collective-permute-start.11 = (bf16[768,512]{1,0:T(8,128)(2,1)S(1)}, bf16[768,512]{1,0:T(8,128)(2,1)S(1)}, u32[]{:S(2)}, u32[]{:S(2)}) collective-permute-start(bf16[768,512]{1,0:T(8,128)(2,1)S(1)} %collective-permute-done.7.refs_8_), channel_id=1, source_target_pairs={{0,48},{1,49},{2,50},{3,51},{4,52},{5,53},{6,54},{7,55},{8,56},{9,... | collective-permute-start | bytes 2359304 | tf_op jit(solution)/shard_map/ppermute | solution.py:377
  96.3 39.1 %copy-start.4 = (bf16[768,512]{1,0:T(8,128)(2,1)}, bf16[768,512]{1,0:T(8,128)(2,1)S(1)}, u32[]{:S(2)}) copy-start(bf16[768,512]{1,0:T(8,128)(2,1)S(1)} %collective-permute-done.5.refs_6_) | copy-start | bytes 2359300
  96.3 19.4 %collective-permute-start.12 = (bf16[768,512]{1,0:T(8,128)(2,1)S(1)}, bf16[768,512]{1,0:T(8,128)(2,1)S(1)}, u32[]{:S(2)}, u32[]{:S(2)}) collective-permute-start(bf16[768,512]{1,0:T(8,128)(2,1)S(1)} %collective-permute-done.5.refs_6_), channel_id=1, source_target_pairs={{0,64},{1,65},{2,66},{3,67},{4,68},{5,69},{6,70},{7,71},{8,72},{9,... | collective-permute-start | bytes 2359304 | tf_op jit(solution)/shard_map/ppermute | solution.py:377
  96.7 19.0 %collective-permute-start.10 = (bf16[768,512]{1,0:T(8,128)(2,1)S(1)}, bf16[768,512]{1,0:T(8,128)(2,1)S(1)}, u32[]{:S(2)}, u32[]{:S(2)}) collective-permute-start(bf16[768,512]{1,0:T(8,128)(2,1)S(1)} %collective-permute-done.5.refs_6_), channel_id=1, source_target_pairs={{0,16},{1,17},{2,18},{3,19},{4,20},{5,21},{6,22},{7,23},{8,24},{9,... | collective-permute-start | bytes 2359304 | tf_op jit(solution)/shard_map/ppermute | solution.py:377
  99.0 36.5 %copy-start.5 = (bf16[768,512]{1,0:T(8,128)(2,1)}, bf16[768,512]{1,0:T(8,128)(2,1)S(1)}, u32[]{:S(2)}) copy-start(bf16[768,512]{1,0:T(8,128)(2,1)S(1)} %collective-permute-done.6.refs_2_) | copy-start | bytes 2359300
  99.0 28.8 %collective-permute-start.8 = (bf16[768,512]{1,0:T(8,128)(2,1)}, bf16[768,512]{1,0:T(8,128)(2,1)S(1)}, u32[]{:S(2)}, u32[]{:S(2)}) collective-permute-start(bf16[768,512]{1,0:T(8,128)(2,1)} %get-tuple-element.17.refs_0_), channel_id=1, source_target_pairs={{0,8},{1,9},{2,10},{3,11},{4,12},{5,13},{6,14},{7,15},{8,0},{9,1},... | collective-permute-start | bytes 2359304 | tf_op jit(solution)/shard_map/ppermute | solution.py:377
  102.0 25.9 %collective-permute-start.9 = (bf16[768,512]{1,0:T(8,128)(2,1)S(1)}, bf16[768,512]{1,0:T(8,128)(2,1)S(1)}, u32[]{:S(2)}, u32[]{:S(2)}) collective-permute-start(bf16[768,512]{1,0:T(8,128)(2,1)S(1)} %collective-permute-done.6.refs_2_), channel_id=1, source_target_pairs={{0,8},{1,9},{2,10},{3,11},{4,12},{5,13},{6,14},{7,15},{8,0},{9,1},... | collective-permute-start | bytes 2359304 | tf_op jit(solution)/shard_map/ppermute | solution.py:377
  115.7 12.7 %copy-start = (bf16[768,512]{1,0:T(8,128)(2,1)}, bf16[768,512]{1,0:T(8,128)(2,1)S(1)}, u32[]{:S(2)}) copy-start(bf16[768,512]{1,0:T(8,128)(2,1)S(1)} %collective-permute-done.11.refs_10_) | copy-start | bytes 2359300
  115.7 19.7 %copy-start.1 = (bf16[768,512]{1,0:T(8,128)(2,1)}, bf16[768,512]{1,0:T(8,128)(2,1)S(1)}, u32[]{:S(2)}) copy-start(bf16[768,512]{1,0:T(8,128)(2,1)S(1)} %collective-permute-done.12.refs_12_) | copy-start | bytes 2359300
  115.7 19.7 %copy-start.2 = (bf16[768,512]{1,0:T(8,128)(2,1)}, bf16[768,512]{1,0:T(8,128)(2,1)S(1)}, u32[]{:S(2)}) copy-start(bf16[768,512]{1,0:T(8,128)(2,1)S(1)} %collective-permute-done.10.refs_4_) | copy-start | bytes 2359300
  115.8 7.0 %collective-permute-start.19 = (bf16[256,512]{1,0:T(8,128)(2,1)S(1)}, bf16[256,512]{1,0:T(8,128)(2,1)S(1)}, u32[]{:S(2)}, u32[]{:S(2)}) collective-permute-start(bf16[256,512]{1,0:T(8,128)(2,1)S(1)} %slice.10), channel_id=1, source_target_pairs={{0,16},{1,17},{2,18},{3,19},{4,20},{5,21},{6,22},{7,23},{8,24},{9,... | collective-permute-start | bytes 786440 | tf_op jit(solution)/shard_map/ppermute | solution.py:377
  115.9 9.8 %collective-permute-start.18 = (bf16[256,512]{1,0:T(8,128)(2,1)S(1)}, bf16[256,512]{1,0:T(8,128)(2,1)S(1)}, u32[]{:S(2)}, u32[]{:S(2)}) collective-permute-start(bf16[256,512]{1,0:T(8,128)(2,1)S(1)} %slice.9), channel_id=1, source_target_pairs={{0,48},{1,49},{2,50},{3,51},{4,52},{5,53},{6,54},{7,55},{8,56},{9,... | collective-permute-start | bytes 786440 | tf_op jit(solution)/shard_map/ppermute | solution.py:377
  118.6 7.2 %collective-permute-start.20 = (bf16[256,512]{1,0:T(8,128)(2,1)S(1)}, bf16[256,512]{1,0:T(8,128)(2,1)S(1)}, u32[]{:S(2)}, u32[]{:S(2)}) collective-permute-start(bf16[256,512]{1,0:T(8,128)(2,1)S(1)} %slice.11), channel_id=1, source_target_pairs={{0,64},{1,65},{2,66},{3,67},{4,68},{5,69},{6,70},{7,71},{8,72},{9,... | collective-permute-start | bytes 786440 | tf_op jit(solution)/shard_map/ppermute | solution.py:377
  122.7 12.7 %copy-start.14 = (bf16[256,512]{1,0:T(8,128)(2,1)}, bf16[256,512]{1,0:T(8,128)(2,1)S(1)}, u32[]{:S(2)}) copy-start(bf16[256,512]{1,0:T(8,128)(2,1)S(1)} %collective-permute-done.19.refs_15_) | copy-start | bytes 786436
  122.7 5.5 %collective-permute-start.22 = (bf16[256,512]{1,0:T(8,128)(2,1)S(1)}, bf16[256,512]{1,0:T(8,128)(2,1)}, u32[]{:S(2)}, u32[]{:S(2)}) collective-permute-start(bf16[256,512]{1,0:T(8,128)(2,1)S(1)} %collective-permute-done.19.refs_15_), channel_id=1, source_target_pairs={{0,8},{1,9},{2,10},{3,11},{4,12},{5,13},{6,14},{7,15},{8,0},{9,1},... | collective-permute-start | bytes 786440 | tf_op jit(solution)/shard_map/ppermute | solution.py:377
  125.8 2.6 %collective-permute-start.21 = (bf16[256,512]{1,0:T(8,128)(2,1)S(1)}, bf16[256,512]{1,0:T(8,128)(2,1)}, u32[]{:S(2)}, u32[]{:S(2)}) collective-permute-start(bf16[256,512]{1,0:T(8,128)(2,1)S(1)} %collective-permute-done.18.refs_14_), channel_id=1, source_target_pairs={{0,8},{1,9},{2,10},{3,11},{4,12},{5,13},{6,14},{7,15},{8,0},{9,1},... | collective-permute-start | bytes 786440 | tf_op jit(solution)/shard_map/ppermute | solution.py:377
  125.9 3.2 %collective-permute-start.23 = (bf16[256,512]{1,0:T(8,128)(2,1)S(1)}, bf16[256,512]{1,0:T(8,128)(2,1)}, u32[]{:S(2)}, u32[]{:S(2)}) collective-permute-start(bf16[256,512]{1,0:T(8,128)(2,1)S(1)} %collective-permute-done.20.refs_16_), channel_id=1, source_target_pairs={{0,8},{1,9},{2,10},{3,11},{4,12},{5,13},{6,14},{7,15},{8,0},{9,1},... | collective-permute-start | bytes 786440 | tf_op jit(solution)/shard_map/ppermute | solution.py:377
  127.7 4.5 %collective-permute-start.13 = (bf16[768,512]{1,0:T(8,128)(2,1)S(1)}, bf16[768,512]{1,0:T(8,128)(2,1)S(1)}, u32[]{:S(2)}, u32[]{:S(2)}) collective-permute-start(bf16[768,512]{1,0:T(8,128)(2,1)S(1)} %collective-permute-done.10.refs_4_), channel_id=1, source_target_pairs={{0,8},{1,9},{2,10},{3,11},{4,12},{5,13},{6,14},{7,15},{8,0},{9,1},... | collective-permute-start | bytes 2359304 | tf_op jit(solution)/shard_map/ppermute | solution.py:377
  127.8 3.3 %collective-permute-start.14 = (bf16[768,512]{1,0:T(8,128)(2,1)S(1)}, bf16[768,512]{1,0:T(8,128)(2,1)S(1)}, u32[]{:S(2)}, u32[]{:S(2)}) collective-permute-start(bf16[768,512]{1,0:T(8,128)(2,1)S(1)} %collective-permute-done.5.refs_6_), channel_id=1, source_target_pairs={{0,8},{1,9},{2,10},{3,11},{4,12},{5,13},{6,14},{7,15},{8,0},{9,1},... | collective-permute-start | bytes 2359304 | tf_op jit(solution)/shard_map/ppermute | solution.py:377
  128.3 4.0 %collective-permute-start.15 = (bf16[768,512]{1,0:T(8,128)(2,1)S(1)}, bf16[768,512]{1,0:T(8,128)(2,1)S(1)}, u32[]{:S(2)}, u32[]{:S(2)}) collective-permute-start(bf16[768,512]{1,0:T(8,128)(2,1)S(1)} %collective-permute-done.7.refs_8_), channel_id=1, source_target_pairs={{0,8},{1,9},{2,10},{3,11},{4,12},{5,13},{6,14},{7,15},{8,0},{9,1},... | collective-permute-start | bytes 2359304 | tf_op jit(solution)/shard_map/ppermute | solution.py:377
  128.4 5.0 %collective-permute-start.16 = (bf16[768,512]{1,0:T(8,128)(2,1)S(1)}, bf16[768,512]{1,0:T(8,128)(2,1)S(1)}, u32[]{:S(2)}, u32[]{:S(2)}) collective-permute-start(bf16[768,512]{1,0:T(8,128)(2,1)S(1)} %collective-permute-done.11.refs_10_), channel_id=1, source_target_pairs={{0,8},{1,9},{2,10},{3,11},{4,12},{5,13},{6,14},{7,15},{8,0},{9,1},... | collective-permute-start | bytes 2359304 | tf_op jit(solution)/shard_map/ppermute | solution.py:377
  129.0 5.5 %collective-permute-start.17 = (bf16[768,512]{1,0:T(8,128)(2,1)S(1)}, bf16[768,512]{1,0:T(8,128)(2,1)S(1)}, u32[]{:S(2)}, u32[]{:S(2)}) collective-permute-start(bf16[768,512]{1,0:T(8,128)(2,1)S(1)} %collective-permute-done.12.refs_12_), channel_id=1, source_target_pairs={{0,8},{1,9},{2,10},{3,11},{4,12},{5,13},{6,14},{7,15},{8,0},{9,1},... | collective-permute-start | bytes 2359304 | tf_op jit(solution)/shard_map/ppermute | solution.py:377
  (15 other events, 47.9 us)

commit v7 on v6

--- a/solution.py
+++ b/solution.py
@@ -417,15 +417,19 @@
     far_x, across_above, across_below = over(below, 0, 1, 0), over(across, 0, -1, 0), over(below, 1, 0, 0)
     held = lax.optimization_barrier((send, below, above, across))
     send_pair, above_pair = over(held[0], 0, 0, 1), over(held[2], 0, 0, 1)
-    below, across, far_x, across_above, across_below = lax.optimization_barrier(
-        (below, across, far_x, across_above, across_below)
+    after = lax.optimization_barrier((send_pair, above_pair, below, across))
+    below_pair, across_pair = over(after[2], 0, 0, 1), over(after[3], 0, 0, 1)
+    below_pair, across_pair, far_x, across_above, across_below = lax.optimization_barrier(
+        (below_pair, across_pair, far_x, across_above, across_below)
     )
     last = [
         over(across_above[low], 0, -1, 0),
         over(across_below[middle], 0, 1, 0),
         over(far_x[high], 1, 0, 0),
     ]
-    below_pair, across_pair = (over(item, 0, 0, 1) for item in (below, across))
+    *last, far_x, across_above, across_below = lax.optimization_barrier(
+        (*last, far_x, across_above, across_below)
+    )
     far_pair, across_above_pair, across_below_pair = (
         over(item, 0, 0, 1) for item in (far_x, across_above, across_below)
     )

time: 194 us -> 199 us (1.026)
  waiting for transfers between devices: 44.1 us -> 49 us
    ppermute x24, waiting for transfers between devices: 44.1 us -> 49 us  [sent(): return lax.ppermute(array, ('tm', 'space'), pairs)]
    unnamed x48 -> x54, local copies, waits for them, and re-layouts: 4.37 us -> 5.3 us
  transfers between devices with their start and end apart: 24 -> 24, of which waited for: 11 -> 12; matrix products, arithmetic and copies ran while one was open for 1% -> 1% of each run, Pallas kernels for 0% -> 0%
where the time goes in v7:
time: 199 us; the launch traced here: 197 us
  Pallas kernels  106 us (53%)
  waiting for transfers between devices  49 us (25%)
  starting transfers between devices  35 us (18%)
  local copies, waits for them, and re-layouts  5.37 us (3%)
    pallas_call x1, Pallas kernels, body(): pl.pallas_call(chain_kernel, out_shape=jax.ShapeDtypeStruct((STRIDE, VARS...  56.9 us
    ppermute x24, waiting for transfers between devices, sent(): return lax.ppermute(array, ('tm', 'space'), pairs)  49 us
    pallas_call x1, Pallas kernels, body(): pl.pallas_call(relax_kernel, out_shape=(jax.ShapeDtypeStruct((ROWS, NODES...  48.9 us
    ppermute x24, starting transfers between devices, sent(): return lax.ppermute(array, ('tm', 'space'), pairs)  35 us
    unnamed x54, local copies, waits for them, and re-layouts  5.3 us
  transfers between devices with their start and end apart: 24, of which 12 were waited for; matrix products, arithmetic and copies ran while one was open for 1% of the time, Pallas kernels for 0%

profile of v7, /device:TPU:1, one launch (start us, length us, event | category | flops | bytes accessed | tf_op | source)
XLA Modules:
  0.0 197.2 jit_solution(11522352846747219400)
XLA Ops:
  0.0 0.7 copy-done.24
  0.7 1.0 fusion.3
  1.7 2.7 %collective-permute-start = (bf16[112,512]{1,0:T(8,128)(2,1)S(1)}, bf16[112,512]{1,0:T(8,128)(2,1)S(1)}, u32[]{:S(2)}, u32[]{:S(2)}) collective-permute-start(bf16[112,512]{1,0:T(8,128)(2,1)S(1)} %fusion.2), channel_id=1, source_target_pairs={{0,8},{1,9},{2,10},{3,11},{4,12},{5,13},{6,14},{7,15},{8,16},{9,17... | collective-permute-start | bytes 344072 | tf_op jit(solution)/shard_map/ppermute | solution.py:377
  4.4 3.4 %collective-permute-start.1 = (bf16[112,512]{1,0:T(8,128)(2,1)S(1)}, bf16[112,512]{1,0:T(8,128)(2,1)S(1)}, u32[]{:S(2)}, u32[]{:S(2)}) collective-permute-start(bf16[112,512]{1,0:T(8,128)(2,1)S(1)} %fusion.2), channel_id=1, source_target_pairs={{0,9},{1,8},{2,11},{3,10},{4,13},{5,12},{6,15},{7,14},{8,17},{9,16... | collective-permute-start | bytes 344072 | tf_op jit(solution)/shard_map/ppermute | solution.py:377
  7.8 2.3 %collective-permute-done.1 = bf16[112,512]{1,0:T(8,128)(2,1)S(1)} collective-permute-done((bf16[112,512]{1,0:T(8,128)(2,1)S(1)}, bf16[112,512]{1,0:T(8,128)(2,1)S(1)}, u32[]{:S(2)}, u32[]{:S(2)}) %collective-permute-start.1) | collective-permute-done | bytes 114720 | tf_op jit(solution)/shard_map/ppermute | solution.py:377
  10.1 2.8 %collective-permute-start.4 = (bf16[224,512]{1,0:T(8,128)(2,1)S(1)}, bf16[224,512]{1,0:T(8,128)(2,1)S(1)}, u32[]{:S(2)}, u32[]{:S(2)}) collective-permute-start(bf16[224,512]{1,0:T(8,128)(2,1)S(1)} %constant_dynamic-update-slice_fusion.refs_2_), channel_id=1, source_target_pairs={{0,6},{1,7},{2,0},{3,1},{4,2},{5,3},{6,4},{7,5},{8,14},{9,15},{10,... | collective-permute-start | bytes 688136 | tf_op jit(solution)/shard_map/ppermute | solution.py:377
  12.9 1.6 collective-permute-start.2
  14.6 0.7 copy-done.25
  16.6 5.6 %collective-permute-done.3.refs_1_ = bf16[224,512]{1,0:T(8,128)(2,1)S(1)} collective-permute-done((bf16[224,512]{1,0:T(8,128)(2,1)S(1)}, bf16[224,512]{1,0:T(8,128)(2,1)S(1)}, u32[]{:S(2)}, u32[]{:S(2)}) %collective-permute-start.3) | collective-permute-done | bytes 229408 | tf_op jit(solution)/shard_map/ppermute | solution.py:377
  22.9 0.7 copy-done.22
  23.6 48.9 %shard_map.109 = (bf16[768,512]{1,0:T(8,128)(2,1)}, f32[12,8,512]{2,1,0:T(8,128)}, bf16[768,512]{1,0:T(8,128)(2,1)}, bf16[3,64,128]{2,1,0:T(8,128)(2,1)}) custom-call(s32[2]{0:T(128)} %pad_add_fusion.group_ref, s32[24,3]{1,0:T(8,128)} %copy.13.species_ref, f32[24]{0:T(128)} %rate_ref.3, f32[12]{0:T(128)} %speed_ref.3, bf16[224,512]{1,0:T(8,128)(2,1)} %copy-done.22, ...), custom_call_target="tpu_custom_call" | custom-call | tf_op jit(solution)/shard_map/pallas_call | solution.py:391
  72.5 4.7 %collective-permute-start.7 = (bf16[768,512]{1,0:T(8,128)(2,1)}, bf16[768,512]{1,0:T(8,128)(2,1)S(1)}, u32[]{:S(2)}, u32[]{:S(2)}) collective-permute-start(bf16[768,512]{1,0:T(8,128)(2,1)} %get-tuple-element.25.refs_0_), channel_id=1, source_target_pairs={{0,64},{1,65},{2,66},{3,67},{4,68},{5,69},{6,70},{7,71},{8,72},{9,... | collective-permute-start | bytes 2359304 | tf_op jit(solution)/shard_map/ppermute | solution.py:377
  77.2 1.0 collective-permute-start.6
  78.3 2.2 %collective-permute-start.5 = (bf16[768,512]{1,0:T(8,128)(2,1)}, bf16[768,512]{1,0:T(8,128)(2,1)S(1)}, u32[]{:S(2)}, u32[]{:S(2)}) collective-permute-start(bf16[768,512]{1,0:T(8,128)(2,1)} %get-tuple-element.25.refs_0_), channel_id=1, source_target_pairs={{0,16},{1,17},{2,18},{3,19},{4,20},{5,21},{6,22},{7,23},{8,24},{9,... | collective-permute-start | bytes 2359304 | tf_op jit(solution)/shard_map/ppermute | solution.py:377
  80.5 10.9 %collective-permute-done.7.refs_8_ = bf16[768,512]{1,0:T(8,128)(2,1)S(1)} collective-permute-done((bf16[768,512]{1,0:T(8,128)(2,1)}, bf16[768,512]{1,0:T(8,128)(2,1)S(1)}, u32[]{:S(2)}, u32[]{:S(2)}) %collective-permute-start.7) | collective-permute-done | bytes 786464 | tf_op jit(solution)/shard_map/ppermute | solution.py:377
  91.4 4.5 %collective-permute-done.6.refs_2_ = bf16[768,512]{1,0:T(8,128)(2,1)S(1)} collective-permute-done((bf16[768,512]{1,0:T(8,128)(2,1)}, bf16[768,512]{1,0:T(8,128)(2,1)S(1)}, u32[]{:S(2)}, u32[]{:S(2)}) %collective-permute-start.6) | collective-permute-done | bytes 786464 | tf_op jit(solution)/shard_map/ppermute | solution.py:377
  95.9 3.7 %collective-permute-start.8 = (bf16[768,512]{1,0:T(8,128)(2,1)}, bf16[768,512]{1,0:T(8,128)(2,1)S(1)}, u32[]{:S(2)}, u32[]{:S(2)}) collective-permute-start(bf16[768,512]{1,0:T(8,128)(2,1)} %get-tuple-element.25.refs_0_), channel_id=1, source_target_pairs={{0,8},{1,9},{2,10},{3,11},{4,12},{5,13},{6,14},{7,15},{8,0},{9,1},... | collective-permute-start | bytes 2359304 | tf_op jit(solution)/shard_map/ppermute | solution.py:377
  99.6 1.6 collective-permute-start.13
  101.4 1.1 collective-permute-start.12
  102.8 1.1 collective-permute-start.10
  104.0 14.2 %collective-permute-done.13.refs_10_ = bf16[768,512]{1,0:T(8,128)(2,1)S(1)} collective-permute-done((bf16[768,512]{1,0:T(8,128)(2,1)S(1)}, bf16[768,512]{1,0:T(8,128)(2,1)S(1)}, u32[]{:S(2)}, u32[]{:S(2)}) %collective-permute-start.13) | collective-permute-done | bytes 786464 | tf_op jit(solution)/shard_map/ppermute | solution.py:377
  118.2 1.3 collective-permute-done.14.refs_12_
  119.6 1.0 collective-permute-done.12.refs_4_
  120.7 1.4 collective-permute-start.17
  122.1 2.7 %collective-permute-start.15 = (bf16[256,512]{1,0:T(8,128)(2,1)S(1)}, bf16[256,512]{1,0:T(8,128)(2,1)S(1)}, u32[]{:S(2)}, u32[]{:S(2)}) collective-permute-start(bf16[256,512]{1,0:T(8,128)(2,1)S(1)} %slice.9), channel_id=1, source_target_pairs={{0,48},{1,49},{2,50},{3,51},{4,52},{5,53},{6,54},{7,55},{8,56},{9,... | collective-permute-start | bytes 786440 | tf_op jit(solution)/shard_map/ppermute | solution.py:377
  124.8 1.8 collective-permute-done.17.refs_16_
  126.6 2.2 %collective-permute-done.16.refs_15_ = bf16[256,512]{1,0:T(8,128)(2,1)S(1)} collective-permute-done((bf16[256,512]{1,0:T(8,128)(2,1)S(1)}, bf16[256,512]{1,0:T(8,128)(2,1)S(1)}, u32[]{:S(2)}, u32[]{:S(2)}) %collective-permute-start.16) | collective-permute-done | bytes 262176 | tf_op jit(solution)/shard_map/ppermute | solution.py:377
  128.8 3.3 %collective-permute-start.18 = (bf16[768,512]{1,0:T(8,128)(2,1)S(1)}, bf16[768,512]{1,0:T(8,128)(2,1)S(1)}, u32[]{:S(2)}, u32[]{:S(2)}) collective-permute-start(bf16[768,512]{1,0:T(8,128)(2,1)S(1)} %collective-permute-done.12.refs_4_), channel_id=1, source_target_pairs={{0,8},{1,9},{2,10},{3,11},{4,12},{5,13},{6,14},{7,15},{8,0},{9,1},... | collective-permute-start | bytes 2359304 | tf_op jit(solution)/shard_map/ppermute | solution.py:377
  133.1 3.5 %collective-permute-done.21.refs_17_ = bf16[256,512]{1,0:T(8,128)(2,1)S(1)} collective-permute-done((bf16[256,512]{1,0:T(8,128)(2,1)S(1)}, bf16[256,512]{1,0:T(8,128)(2,1)S(1)}, u32[]{:S(2)}, u32[]{:S(2)}) %collective-permute-start.21) | collective-permute-done | bytes 262176 | tf_op jit(solution)/shard_map/ppermute | solution.py:377
  137.0 1.2 collective-permute-done.23.refs_19_
  138.2 0.9 copy-done.10
  140.1 56.9 %shard_map.110 = f32[4,12,8,512]{3,2,1,0:T(8,128)} custom-call(s32[2]{0:T(128)} %pad_add_fusion.group_ref, s32[24,3]{1,0:T(8,128)} %copy.13.species_ref, f32[24]{0:T(128)} %rate_ref.3, f32[12]{0:T(128)} %speed_ref.3, bf16[768,512]{1,0:T(8,128)(2,1)} %get-tuple-element.25.refs_0_, bf16[768,512]{1,0:T(8,128)(2,1)} %copy-done.6, bf16[768,512]{1,0:T(8,128)(2,1)} %copy-done.4, ...), custom_call_target="tpu_custom_call" | custom-call | tf_op jit(solution)/shard_map/pallas_call | solution.py:442
  (80 shorter events, 5.0 us)
Async XLA Ops:
  1.7 6.1 %collective-permute-start = (bf16[112,512]{1,0:T(8,128)(2,1)S(1)}, bf16[112,512]{1,0:T(8,128)(2,1)S(1)}, u32[]{:S(2)}, u32[]{:S(2)}) collective-permute-start(bf16[112,512]{1,0:T(8,128)(2,1)S(1)} %fusion.2), channel_id=1, source_target_pairs={{0,8},{1,9},{2,10},{3,11},{4,12},{5,13},{6,14},{7,15},{8,16},{9,17... | collective-permute-start | bytes 344072 | tf_op jit(solution)/shard_map/ppermute | solution.py:377
  4.4 5.7 %collective-permute-start.1 = (bf16[112,512]{1,0:T(8,128)(2,1)S(1)}, bf16[112,512]{1,0:T(8,128)(2,1)S(1)}, u32[]{:S(2)}, u32[]{:S(2)}) collective-permute-start(bf16[112,512]{1,0:T(8,128)(2,1)S(1)} %fusion.2), channel_id=1, source_target_pairs={{0,9},{1,8},{2,11},{3,10},{4,13},{5,12},{6,15},{7,14},{8,17},{9,16... | collective-permute-start | bytes 344072 | tf_op jit(solution)/shard_map/ppermute | solution.py:377
  10.1 6.5 %collective-permute-start.4 = (bf16[224,512]{1,0:T(8,128)(2,1)S(1)}, bf16[224,512]{1,0:T(8,128)(2,1)S(1)}, u32[]{:S(2)}, u32[]{:S(2)}) collective-permute-start(bf16[224,512]{1,0:T(8,128)(2,1)S(1)} %constant_dynamic-update-slice_fusion.refs_2_), channel_id=1, source_target_pairs={{0,6},{1,7},{2,0},{3,1},{4,2},{5,3},{6,4},{7,5},{8,14},{9,15},{10,... | collective-permute-start | bytes 688136 | tf_op jit(solution)/shard_map/ppermute | solution.py:377
  12.9 9.3 %collective-permute-start.3 = (bf16[224,512]{1,0:T(8,128)(2,1)S(1)}, bf16[224,512]{1,0:T(8,128)(2,1)S(1)}, u32[]{:S(2)}, u32[]{:S(2)}) collective-permute-start(bf16[224,512]{1,0:T(8,128)(2,1)S(1)} %constant_dynamic-update-slice_fusion.refs_2_), channel_id=1, source_target_pairs={{0,2},{1,3},{2,4},{3,5},{4,6},{5,7},{6,0},{7,1},{8,10},{9,11},{10,... | collective-permute-start | bytes 688136 | tf_op jit(solution)/shard_map/ppermute | solution.py:377
  12.9 9.3 %collective-permute-start.2 = (bf16[224,512]{1,0:T(8,128)(2,1)S(1)}, bf16[224,512]{1,0:T(8,128)(2,1)S(1)}, u32[]{:S(2)}, u32[]{:S(2)}) collective-permute-start(bf16[224,512]{1,0:T(8,128)(2,1)S(1)} %constant_dynamic-update-slice_fusion.refs_2_), channel_id=1, source_target_pairs={{0,4},{1,5},{2,6},{3,7},{4,0},{5,1},{6,2},{7,3},{8,12},{9,13},{10,... | collective-permute-start | bytes 688136 | tf_op jit(solution)/shard_map/ppermute | solution.py:377
  72.5 18.9 %collective-permute-start.7 = (bf16[768,512]{1,0:T(8,128)(2,1)}, bf16[768,512]{1,0:T(8,128)(2,1)S(1)}, u32[]{:S(2)}, u32[]{:S(2)}) collective-permute-start(bf16[768,512]{1,0:T(8,128)(2,1)} %get-tuple-element.25.refs_0_), channel_id=1, source_target_pairs={{0,64},{1,65},{2,66},{3,67},{4,68},{5,69},{6,70},{7,71},{8,72},{9,... | collective-permute-start | bytes 2359304 | tf_op jit(solution)/shard_map/ppermute | solution.py:377
  77.2 18.7 %collective-permute-start.6 = (bf16[768,512]{1,0:T(8,128)(2,1)}, bf16[768,512]{1,0:T(8,128)(2,1)S(1)}, u32[]{:S(2)}, u32[]{:S(2)}) collective-permute-start(bf16[768,512]{1,0:T(8,128)(2,1)} %get-tuple-element.25.refs_0_), channel_id=1, source_target_pairs={{0,48},{1,49},{2,50},{3,51},{4,52},{5,53},{6,54},{7,55},{8,56},{9,... | collective-permute-start | bytes 2359304 | tf_op jit(solution)/shard_map/ppermute | solution.py:377
  78.3 17.7 %collective-permute-start.5 = (bf16[768,512]{1,0:T(8,128)(2,1)}, bf16[768,512]{1,0:T(8,128)(2,1)S(1)}, u32[]{:S(2)}, u32[]{:S(2)}) collective-permute-start(bf16[768,512]{1,0:T(8,128)(2,1)} %get-tuple-element.25.refs_0_), channel_id=1, source_target_pairs={{0,16},{1,17},{2,18},{3,19},{4,20},{5,21},{6,22},{7,23},{8,24},{9,... | collective-permute-start | bytes 2359304 | tf_op jit(solution)/shard_map/ppermute | solution.py:377
  91.4 48.6 %copy-start.3 = (bf16[768,512]{1,0:T(8,128)(2,1)}, bf16[768,512]{1,0:T(8,128)(2,1)S(1)}, u32[]{:S(2)}) copy-start(bf16[768,512]{1,0:T(8,128)(2,1)S(1)} %collective-permute-done.7.refs_8_) | copy-start | bytes 2359300
  95.9 44.1 %copy-start.4 = (bf16[768,512]{1,0:T(8,128)(2,1)}, bf16[768,512]{1,0:T(8,128)(2,1)S(1)}, u32[]{:S(2)}) copy-start(bf16[768,512]{1,0:T(8,128)(2,1)S(1)} %collective-permute-done.6.refs_2_) | copy-start | bytes 2359300
  95.9 44.1 %copy-start.5 = (bf16[768,512]{1,0:T(8,128)(2,1)}, bf16[768,512]{1,0:T(8,128)(2,1)S(1)}, u32[]{:S(2)}) copy-start(bf16[768,512]{1,0:T(8,128)(2,1)S(1)} %collective-permute-done.5.refs_6_) | copy-start | bytes 2359300
  95.9 6.9 %collective-permute-start.8 = (bf16[768,512]{1,0:T(8,128)(2,1)}, bf16[768,512]{1,0:T(8,128)(2,1)S(1)}, u32[]{:S(2)}, u32[]{:S(2)}) collective-permute-start(bf16[768,512]{1,0:T(8,128)(2,1)} %get-tuple-element.25.refs_0_), channel_id=1, source_target_pairs={{0,8},{1,9},{2,10},{3,11},{4,12},{5,13},{6,14},{7,15},{8,0},{9,1},... | collective-permute-start | bytes 2359304 | tf_op jit(solution)/shard_map/ppermute | solution.py:377
  99.6 3.2 %collective-permute-start.9 = (bf16[768,512]{1,0:T(8,128)(2,1)S(1)}, bf16[768,512]{1,0:T(8,128)(2,1)S(1)}, u32[]{:S(2)}, u32[]{:S(2)}) collective-permute-start(bf16[768,512]{1,0:T(8,128)(2,1)S(1)} %collective-permute-done.6.refs_2_), channel_id=1, source_target_pairs={{0,8},{1,9},{2,10},{3,11},{4,12},{5,13},{6,14},{7,15},{8,0},{9,1},... | collective-permute-start | bytes 2359304 | tf_op jit(solution)/shard_map/ppermute | solution.py:377
  99.6 18.6 %collective-permute-start.13 = (bf16[768,512]{1,0:T(8,128)(2,1)S(1)}, bf16[768,512]{1,0:T(8,128)(2,1)S(1)}, u32[]{:S(2)}, u32[]{:S(2)}) collective-permute-start(bf16[768,512]{1,0:T(8,128)(2,1)S(1)} %collective-permute-done.7.refs_8_), channel_id=1, source_target_pairs={{0,48},{1,49},{2,50},{3,51},{4,52},{5,53},{6,54},{7,55},{8,56},{9,... | collective-permute-start | bytes 2359304 | tf_op jit(solution)/shard_map/ppermute | solution.py:377
  101.3 18.3 %collective-permute-start.14 = (bf16[768,512]{1,0:T(8,128)(2,1)S(1)}, bf16[768,512]{1,0:T(8,128)(2,1)S(1)}, u32[]{:S(2)}, u32[]{:S(2)}) collective-permute-start(bf16[768,512]{1,0:T(8,128)(2,1)S(1)} %collective-permute-done.5.refs_6_), channel_id=1, source_target_pairs={{0,64},{1,65},{2,66},{3,67},{4,68},{5,69},{6,70},{7,71},{8,72},{9,... | collective-permute-start | bytes 2359304 | tf_op jit(solution)/shard_map/ppermute | solution.py:377
  101.4 19.2 %collective-permute-start.12 = (bf16[768,512]{1,0:T(8,128)(2,1)S(1)}, bf16[768,512]{1,0:T(8,128)(2,1)S(1)}, u32[]{:S(2)}, u32[]{:S(2)}) collective-permute-start(bf16[768,512]{1,0:T(8,128)(2,1)S(1)} %collective-permute-done.5.refs_6_), channel_id=1, source_target_pairs={{0,16},{1,17},{2,18},{3,19},{4,20},{5,21},{6,22},{7,23},{8,24},{9,... | collective-permute-start | bytes 2359304 | tf_op jit(solution)/shard_map/ppermute | solution.py:377
  102.8 37.2 %copy-start.6 = (bf16[768,512]{1,0:T(8,128)(2,1)}, bf16[768,512]{1,0:T(8,128)(2,1)S(1)}, u32[]{:S(2)}) copy-start(bf16[768,512]{1,0:T(8,128)(2,1)S(1)} %collective-permute-done.8.refs_1_) | copy-start | bytes 2359300
  102.8 37.2 %copy-start.7 = (bf16[768,512]{1,0:T(8,128)(2,1)}, bf16[768,512]{1,0:T(8,128)(2,1)S(1)}, u32[]{:S(2)}) copy-start(bf16[768,512]{1,0:T(8,128)(2,1)S(1)} %collective-permute-done.9.refs_3_) | copy-start | bytes 2359300
  102.8 17.7 %collective-permute-start.10 = (bf16[768,512]{1,0:T(8,128)(2,1)S(1)}, bf16[768,512]{1,0:T(8,128)(2,1)S(1)}, u32[]{:S(2)}, u32[]{:S(2)}) collective-permute-start(bf16[768,512]{1,0:T(8,128)(2,1)S(1)} %collective-permute-done.5.refs_6_), channel_id=1, source_target_pairs={{0,8},{1,9},{2,10},{3,11},{4,12},{5,13},{6,14},{7,15},{8,0},{9,1},... | collective-permute-start | bytes 2359304 | tf_op jit(solution)/shard_map/ppermute | solution.py:377
  103.9 16.6 %collective-permute-start.11 = (bf16[768,512]{1,0:T(8,128)(2,1)S(1)}, bf16[768,512]{1,0:T(8,128)(2,1)S(1)}, u32[]{:S(2)}, u32[]{:S(2)}) collective-permute-start(bf16[768,512]{1,0:T(8,128)(2,1)S(1)} %collective-permute-done.7.refs_8_), channel_id=1, source_target_pairs={{0,8},{1,9},{2,10},{3,11},{4,12},{5,13},{6,14},{7,15},{8,0},{9,1},... | collective-permute-start | bytes 2359304 | tf_op jit(solution)/shard_map/ppermute | solution.py:377
  119.5 20.5 %copy-start.1 = (bf16[768,512]{1,0:T(8,128)(2,1)}, bf16[768,512]{1,0:T(8,128)(2,1)S(1)}, u32[]{:S(2)}) copy-start(bf16[768,512]{1,0:T(8,128)(2,1)S(1)} %collective-permute-done.14.refs_12_) | copy-start | bytes 2359300
  120.6 19.5 %copy-start.8 = (bf16[768,512]{1,0:T(8,128)(2,1)}, bf16[768,512]{1,0:T(8,128)(2,1)S(1)}, u32[]{:S(2)}) copy-start(bf16[768,512]{1,0:T(8,128)(2,1)S(1)} %collective-permute-done.10.refs_7_) | copy-start | bytes 2359300
  120.6 19.5 %copy-start.9 = (bf16[768,512]{1,0:T(8,128)(2,1)}, bf16[768,512]{1,0:T(8,128)(2,1)S(1)}, u32[]{:S(2)}) copy-start(bf16[768,512]{1,0:T(8,128)(2,1)S(1)} %collective-permute-done.11.refs_9_) | copy-start | bytes 2359300
  120.7 5.9 %collective-permute-start.17 = (bf16[256,512]{1,0:T(8,128)(2,1)S(1)}, bf16[256,512]{1,0:T(8,128)(2,1)S(1)}, u32[]{:S(2)}, u32[]{:S(2)}) collective-permute-start(bf16[256,512]{1,0:T(8,128)(2,1)S(1)} %slice.11), channel_id=1, source_target_pairs={{0,64},{1,65},{2,66},{3,67},{4,68},{5,69},{6,70},{7,71},{8,72},{9,... | collective-permute-start | bytes 786440 | tf_op jit(solution)/shard_map/ppermute | solution.py:377
  122.1 6.7 %collective-permute-start.16 = (bf16[256,512]{1,0:T(8,128)(2,1)S(1)}, bf16[256,512]{1,0:T(8,128)(2,1)S(1)}, u32[]{:S(2)}, u32[]{:S(2)}) collective-permute-start(bf16[256,512]{1,0:T(8,128)(2,1)S(1)} %slice.10), channel_id=1, source_target_pairs={{0,16},{1,17},{2,18},{3,19},{4,20},{5,21},{6,22},{7,23},{8,24},{9,... | collective-permute-start | bytes 786440 | tf_op jit(solution)/shard_map/ppermute | solution.py:377
  122.1 6.7 %collective-permute-start.15 = (bf16[256,512]{1,0:T(8,128)(2,1)S(1)}, bf16[256,512]{1,0:T(8,128)(2,1)S(1)}, u32[]{:S(2)}, u32[]{:S(2)}) collective-permute-start(bf16[256,512]{1,0:T(8,128)(2,1)S(1)} %slice.9), channel_id=1, source_target_pairs={{0,48},{1,49},{2,50},{3,51},{4,52},{5,53},{6,54},{7,55},{8,56},{9,... | collective-permute-start | bytes 786440 | tf_op jit(solution)/shard_map/ppermute | solution.py:377
  128.8 9.3 %collective-permute-start.18 = (bf16[768,512]{1,0:T(8,128)(2,1)S(1)}, bf16[768,512]{1,0:T(8,128)(2,1)S(1)}, u32[]{:S(2)}, u32[]{:S(2)}) collective-permute-start(bf16[768,512]{1,0:T(8,128)(2,1)S(1)} %collective-permute-done.12.refs_4_), channel_id=1, source_target_pairs={{0,8},{1,9},{2,10},{3,11},{4,12},{5,13},{6,14},{7,15},{8,0},{9,1},... | collective-permute-start | bytes 2359304 | tf_op jit(solution)/shard_map/ppermute | solution.py:377
  132.1 6.1 %collective-permute-start.19 = (bf16[768,512]{1,0:T(8,128)(2,1)S(1)}, bf16[768,512]{1,0:T(8,128)(2,1)S(1)}, u32[]{:S(2)}, u32[]{:S(2)}) collective-permute-start(bf16[768,512]{1,0:T(8,128)(2,1)S(1)} %collective-permute-done.13.refs_10_), channel_id=1, source_target_pairs={{0,8},{1,9},{2,10},{3,11},{4,12},{5,13},{6,14},{7,15},{8,0},{9,1},... | collective-permute-start | bytes 2359304 | tf_op jit(solution)/shard_map/ppermute | solution.py:377
  132.2 6.0 %collective-permute-start.20 = (bf16[768,512]{1,0:T(8,128)(2,1)S(1)}, bf16[768,512]{1,0:T(8,128)(2,1)S(1)}, u32[]{:S(2)}, u32[]{:S(2)}) collective-permute-start(bf16[768,512]{1,0:T(8,128)(2,1)S(1)} %collective-permute-done.14.refs_12_), channel_id=1, source_target_pairs={{0,8},{1,9},{2,10},{3,11},{4,12},{5,13},{6,14},{7,15},{8,0},{9,1},... | collective-permute-start | bytes 2359304 | tf_op jit(solution)/shard_map/ppermute | solution.py:377
  132.6 4.0 %collective-permute-start.21 = (bf16[256,512]{1,0:T(8,128)(2,1)S(1)}, bf16[256,512]{1,0:T(8,128)(2,1)S(1)}, u32[]{:S(2)}, u32[]{:S(2)}) collective-permute-start(bf16[256,512]{1,0:T(8,128)(2,1)S(1)} %collective-permute-done.15.refs_14_), channel_id=1, source_target_pairs={{0,8},{1,9},{2,10},{3,11},{4,12},{5,13},{6,14},{7,15},{8,0},{9,1},... | collective-permute-start | bytes 786440 | tf_op jit(solution)/shard_map/ppermute | solution.py:377
  132.7 4.3 %collective-permute-start.22 = (bf16[256,512]{1,0:T(8,128)(2,1)S(1)}, bf16[256,512]{1,0:T(8,128)(2,1)S(1)}, u32[]{:S(2)}, u32[]{:S(2)}) collective-permute-start(bf16[256,512]{1,0:T(8,128)(2,1)S(1)} %collective-permute-done.16.refs_15_), channel_id=1, source_target_pairs={{0,8},{1,9},{2,10},{3,11},{4,12},{5,13},{6,14},{7,15},{8,0},{9,1},... | collective-permute-start | bytes 786440 | tf_op jit(solution)/shard_map/ppermute | solution.py:377
  136.7 1.5 collective-permute-start.23
  (18 other events, 98.7 us)
